TPU v7x, 32 devices: a whole 2x2x4 slice. The times are simulated.
32 devices in a mesh: groups: 2 (over y), dp: 8 (over z, x), tensor: 2 (over core).
Axes of the slice: x: 2, y: 2, z: 4, core: 2. Of those that a mesh axis runs over, the one named last changes fastest.
Arguments:
- xbc: bfloat16 [2048, 9216], P(('groups', 'dp', 'tensor')), parts along dimension 0, may hold values from -6 to 6
- gate_z: bfloat16 [2048, 8192], P(('groups', 'dp', 'tensor')), parts along dimension 0, may hold values from -6 to 6
- dt_raw: bfloat16 [2048, 128], P(('groups', 'dp', 'tensor')), parts along dimension 0, may hold values from -6 to 6
- conv_weight: float32 [4, 9216], replicated, may hold values from -3 to 3
- conv_bias: float32 [9216], replicated, may hold values from -3 to 3
- dt_bias: float32 [128], P('tensor'), may hold values from -4 to -1
- decay_rate: float32 [128], P('tensor'), may hold values from 0.02 to 2
- d_skip: float32 [128], P('tensor'), may hold values from 0.5 to 2
- norm_gain: float32 [8192], P('tensor'), may hold values from 0.5 to 1.5
- ssm_store: bfloat16 [16, 128, 64, 128], P(('groups', 'dp'), 'tensor'), parts along dimension 0, may hold values from -1.1953125 to 1.1953125
- conv_store: bfloat16 [16, 3, 9216], P(('groups', 'dp'), None, 'tensor'), parts along dimension 0, may hold values from -6 to 6
- source_of: int32 [16], P('groups'), parts along dimension 0, may hold values from 0 to 7, each once
- prefix_len: int32 [16], P(('groups', 'dp')), parts along dimension 0, may hold values from 0 to 8192, as said below
- span_len: int32 [16], P(('groups', 'dp')), parts along dimension 0, may hold values from 32 to 128
Outputs:
- mixed: bfloat16 [2048, 8192], P(('groups', 'dp'), 'tensor'), parts along dimension 0
There are 2 independent parts, one for each index of `groups`. A program takes and returns all parts, laid end to end along the dimension named above; an argument that names none is the same for every part. Nothing has to cross between parts.
Inputs may be any that keep to these rules, and one draw needn't show every extreme that they name: `source_of`: each of 0 to 7 appears once. `prefix_len`: 0 marks a request without kept states.
All inputs are finite; a program needn't handle non-finite values.
Results may differ from a plain program's by a relative error of at most 0.0045.
Values may be sent and summed in bfloat16 or wider, within the bound.
No kernel may reach another device: no remote copies, remote signals or barrier semaphores. Data moves between devices by JAX's collectives and lax.ppermute only.
A program may use at most 64 MiB of HBM per device.

v0:
```python
import functools

import jax
import jax.numpy as jnp
from jax import lax
from jax.experimental import pallas as pl
from jax.experimental.pallas import tpu as pltpu
from jax.sharding import PartitionSpec as P


HEAD_DIM = 64
STATE = 128
NORM_WIDTH = 2048
EPSILON = 1e-05
LANES = 128
DIRECT_MAX = 8


def swap(value, axis, offset):
    count = lax.axis_size(axis)
    return lax.ppermute(value, axis, [(i, i ^ offset) for i in range(count)])


def offsets(count):
    return sorted(range(1, count), key=lambda k: (-(k.bit_length()), k))


def main_kernel(
    core_ref,
    live_ref,
    skip_ref,
    own_x,
    peer_x,
    own_bc,
    peer_bc,
    weight_x,
    weight_bc,
    bias_x,
    bias_bc,
    rims_x,
    rims_bc,
    own_gate,
    peer_gate,
    own_dt,
    peer_dt,
    head_rows,
    intra_out,
    carry_out,
    c_out,
    extended,
    scores,
    columns,
    cum_rows,
    step_rows,
):
    block = pl.program_id(0)
    count = 2 * own_x.shape[0]
    half = own_x.shape[0]
    width = own_x.shape[1]
    per_block = width // HEAD_DIM
    groups = c_out.shape[1] // STATE
    blocks = pl.num_programs(0)
    first = core_ref[0] == 0
    live = live_ref[0] > 0
    taps = weight_x.shape[0]
    pad = 8 - (taps - 1)

    def whole(own, peer):
        mine = own[...].astype(jnp.float32)
        other = peer[...].astype(jnp.float32)
        return jnp.where(first, mine, other), jnp.where(first, other, mine)

    def convolve(own, peer, rims, weight, bias):
        low, high = whole(own, peer)
        edge = rims[...].astype(jnp.float32)
        extended[pad:8, :] = jnp.where(live, edge, jnp.zeros_like(edge))
        extended[8 : 8 + half, :] = low
        extended[8 + half : 8 + count, :] = high
        total = jnp.broadcast_to(bias[...], (count, width))
        for k in range(taps):
            total = total + weight[k : k + 1, :] * extended[pad + k : pad + k + count, :]
        return jax.nn.silu(total).astype(jnp.bfloat16)

    row = lax.broadcasted_iota(jnp.int32, (count, LANES), 0)
    lane = lax.broadcasted_iota(jnp.int32, (count, LANES), 1)

    @pl.when(block == 0)
    def _():
        active = convolve(own_bc, peer_bc, rims_bc, weight_bc, bias_bc)
        c_out[...] = active[:, groups * STATE :]
        for g in range(groups):
            b = active[:, g * STATE : (g + 1) * STATE]
            c = active[:, (groups + g) * STATE : (groups + g + 1) * STATE]
            product = lax.dot_general(
                c, b, (((1,), (1,)), ((), ())), preferred_element_type=jnp.float32
            )
            scores[g] = jnp.where(row >= lane, product, 0.0)
        low, high = whole(own_dt, peer_dt)
        raw = jnp.concatenate([low, high], axis=0)
        raw = jnp.where(first, raw, pltpu.roll(raw, LANES // 2, 1))
        step = jax.nn.softplus(raw + head_rows[0:1, :])
        total = -head_rows[1:2, :] * step
        shift = 1
        while shift < count:
            total = total + jnp.where(row >= shift, pltpu.roll(total, shift, 0), 0.0)
            shift *= 2
        cum_rows[...] = total.T
        step_rows[...] = step.T
        for i in range(columns.shape[0]):
            columns[i] = total[:, i * per_block : (i + 1) * per_block]

    active = convolve(own_x, peer_x, rims_x, weight_x, bias_x)
    low, high = whole(own_gate, peer_gate)
    gate = jax.nn.silu(jnp.concatenate([low, high], axis=0))
    score = scores[block // (blocks // groups)]
    column = columns[block]
    at = pl.multiple_of(block * per_block, per_block)
    cum_row = cum_rows[pl.ds(at, per_block), :]
    step_row = step_rows[pl.ds(at, per_block), :]
    left = lane < HEAD_DIM
    scale = jnp.where(live, 1.0, 0.0)
    for pair in range(per_block // 2):
        spread, weights = [], []
        for j in (2 * pair, 2 * pair + 1):
            cum = jnp.broadcast_to(column[:, j : j + 1], (count, LANES))
            decay = jnp.exp(jnp.minimum(cum - cum_row[j : j + 1, :], 0.0))
            weights.append((decay * score * step_row[j : j + 1, :]).astype(jnp.bfloat16))
            spread.append(cum)
        lanes = slice(pair * LANES, (pair + 1) * LANES)
        x = active[:, lanes]
        zero = jnp.zeros_like(x)
        stacked = jnp.concatenate([jnp.where(left, x, zero), jnp.where(left, zero, x)], axis=0)
        intra = lax.dot_general(
            jnp.concatenate(weights, axis=1),
            stacked,
            (((1,), (0,)), ((), ())),
            preferred_element_type=jnp.float32,
        )
        skip = jnp.where(left, skip_ref[at + 2 * pair], skip_ref[at + 2 * pair + 1])
        gates = gate[:, lanes]
        intra_out[:, lanes] = (intra + skip * x.astype(jnp.float32)) * gates
        decayed = jnp.exp(jnp.where(left, spread[0], spread[1]))
        carry_out[:, lanes] = gates * decayed * scale


def main_stage(core, live, d_skip, xbc, peer_xbc, weight, bias, rims, gate, peer_gate, dt, peer_dt, heads):
    rows, channels = xbc.shape
    half = channels // 2
    count = 2 * rows
    inner = gate.shape[1] // 2
    width = half - inner
    groups = width // (2 * STATE)
    blocks = inner // width
    per_half = half // width
    per_inner = inner // width
    at_x = lambda i, core, *_: (0, core[0] * per_half + i)
    at_bc = lambda i, core, *_: (0, core[0] * per_half + blocks)
    at_gate = lambda i, core, *_: (0, core[0] * per_inner + i)
    fixed = lambda i, *_: (0, 0)
    step = lambda i, *_: (0, i)
    last = lambda i, *_: (0, blocks)
    taps = weight.shape[0]
    token = lambda index: pl.BlockSpec((rows, width), index)
    grid_spec = pltpu.PrefetchScalarGridSpec(
        num_scalar_prefetch=3,
        grid=(blocks,),
        in_specs=[
            token(at_x),
            token(at_x),
            token(at_bc),
            token(at_bc),
            pl.BlockSpec((taps, width), at_x),
            pl.BlockSpec((taps, width), at_bc),
            pl.BlockSpec((1, width), at_x),
            pl.BlockSpec((1, width), at_bc),
            pl.BlockSpec((taps - 1, width), step),
            pl.BlockSpec((taps - 1, width), last),
            token(at_gate),
            token(at_gate),
            pl.BlockSpec((rows, LANES), fixed),
            pl.BlockSpec((rows, LANES), fixed),
            pl.BlockSpec((8, LANES), fixed),
        ],
        out_specs=[
            pl.BlockSpec((count, width), step),
            pl.BlockSpec((count, width), step),
            pl.BlockSpec((count, groups * STATE), fixed),
        ],
        scratch_shapes=[
            pltpu.VMEM((count + 8, width), jnp.float32),
            pltpu.VMEM((groups, count, LANES), jnp.float32),
            pltpu.VMEM((blocks, count, width // HEAD_DIM), jnp.float32),
            pltpu.VMEM((LANES, count), jnp.float32),
            pltpu.VMEM((LANES, count), jnp.float32),
        ],
    )
    return pl.pallas_call(
        main_kernel,
        grid_spec=grid_spec,
        out_shape=[
            jax.ShapeDtypeStruct((count, inner), jnp.float32),
            jax.ShapeDtypeStruct((count, inner), jnp.float32),
            jax.ShapeDtypeStruct((count, groups * STATE), jnp.bfloat16),
        ],
        compiler_params=pltpu.CompilerParams(vmem_limit_bytes=16 << 20),
        cost_estimate=pl.CostEstimate(flops=400_000_000, bytes_accessed=8_000_000, transcendentals=2_000_000),
        name="main_stage",
    )(core, live, d_skip, xbc, peer_xbc, xbc, peer_xbc, weight, weight, bias, bias, rims, rims, gate, peer_gate, dt, peer_dt, heads)


def tail_kernel(count_pieces, turn_ref, span_ref, *refs):
    pieces = refs[:count_pieces]
    intra, carry, c_proj, gain, out, state, sems = refs[count_pieces:]
    copies = []
    for k, piece in enumerate(pieces):
        slot = turn_ref[0] ^ k
        copy = pltpu.make_async_copy(piece, state.at[slot], sems.at[k])
        copy.start()
        copies.append(copy)
    for copy in copies:
        copy.wait()
    tokens, inner = intra.shape
    groups = c_proj.shape[1] // STATE
    rows = state.shape[1]
    width = inner // groups
    norms = width // NORM_WIDTH
    keep = lax.broadcasted_iota(jnp.int32, (tokens, 1), 0) < span_ref[0]
    chunk = min(rows, 512)
    for n in range(inner // NORM_WIDTH):
        g = n // norms
        c = c_proj[:, g * STATE : (g + 1) * STATE]
        gated = []
        total = jnp.zeros((tokens, 1), jnp.float32)
        for at in range(n * NORM_WIDTH, (n + 1) * NORM_WIDTH, chunk):
            part = state[at // rows, at % rows : at % rows + chunk, :]
            carried = lax.dot_general(
                c, part, (((1,), (1,)), ((), ())), preferred_element_type=jnp.float32
            )
            lanes = slice(at, at + chunk)
            value = intra[:, lanes] + carry[:, lanes] * carried
            total = total + jnp.sum(value * value, axis=1, keepdims=True)
            gated.append((lanes, value))
        scale = lax.rsqrt(total * (1.0 / NORM_WIDTH) + EPSILON)
        for lanes, value in gated:
            normed = value * scale * gain[:, lanes]
            out[:, lanes] = jnp.where(keep, normed, 0.0).astype(jnp.bfloat16)


def tail_stage(turn, span_len, pieces, intra, carry, c_proj, gain):
    rows = pieces[0].shape[0]
    vmem = pl.BlockSpec(memory_space=pltpu.VMEM)
    grid_spec = pltpu.PrefetchScalarGridSpec(
        num_scalar_prefetch=2,
        grid=(),
        in_specs=[pl.BlockSpec(memory_space=pl.ANY)] * len(pieces) + [vmem] * 4,
        out_specs=vmem,
        scratch_shapes=[
            pltpu.VMEM((len(pieces), rows, STATE), jnp.bfloat16),
            pltpu.SemaphoreType.DMA((len(pieces),)),
        ],
    )
    return pl.pallas_call(
        functools.partial(tail_kernel, len(pieces)),
        grid_spec=grid_spec,
        out_shape=jax.ShapeDtypeStruct(intra.shape, jnp.bfloat16),
        compiler_params=pltpu.CompilerParams(vmem_limit_bytes=24 << 20),
        cost_estimate=pl.CostEstimate(flops=140_000_000, bytes_accessed=6_000_000, transcendentals=0),
        name="tail_stage",
    )(turn, span_len, *pieces, intra, carry, c_proj, gain)


def cut_kernel(chosen, state, *refs):
    pieces, sems = refs[: len(chosen)], refs[-1]
    copies = []
    for i, (k, piece) in enumerate(zip(chosen, pieces)):
        copy = pltpu.make_async_copy(state.at[k], piece, sems.at[i])
        copy.start()
        copies.append(copy)
    for copy in copies:
        copy.wait()


def cut_stage(state, chosen):
    return pl.pallas_call(
        functools.partial(cut_kernel, chosen),
        in_specs=[pl.BlockSpec(memory_space=pl.ANY)],
        out_specs=[pl.BlockSpec(memory_space=pltpu.VMEM)] * len(chosen),
        out_shape=[jax.ShapeDtypeStruct(state.shape[1:], state.dtype)] * len(chosen),
        scratch_shapes=[pltpu.SemaphoreType.DMA((len(chosen),))],
        compiler_params=pltpu.CompilerParams(vmem_limit_bytes=8 << 20),
        name="cut_stage",
    )(state)


def pick_kernel(order, me_ref, source_ref, *refs):
    count = len(order)
    held, slots = refs[:count], refs[count:]
    for slot, k in zip(slots, order):
        wanted = me_ref[0] ^ source_ref[me_ref[0] ^ k]
        for r in range(count):

            @pl.when(wanted == r)
            def _(slot=slot, r=r):
                slot[...] = held[r][...]


def pick_stage(me, source_of, held, order):
    vmem = pl.BlockSpec(memory_space=pltpu.VMEM)
    grid_spec = pltpu.PrefetchScalarGridSpec(
        num_scalar_prefetch=2,
        grid=(),
        in_specs=[vmem] * len(held),
        out_specs=[vmem] * len(order),
    )
    shape = jax.ShapeDtypeStruct(held[0].shape, held[0].dtype)
    return pl.pallas_call(
        functools.partial(pick_kernel, tuple(order)),
        grid_spec=grid_spec,
        out_shape=[shape] * len(order),
        compiler_params=pltpu.CompilerParams(vmem_limit_bytes=8 << 20),
        name="pick_stage",
    )(me, source_of, *held)


def gather_rims(conv_store, source_of, me):
    count = lax.axis_size("dp")
    held = conv_store
    index = jnp.zeros((), jnp.int32)
    away = source_of[me] ^ me
    bit = count // 2
    place = 1
    while bit > 0:
        other = swap(held, "dp", bit)
        held = jnp.concatenate([held, other], axis=0)
        index = index + place * ((away // bit) & 1)
        bit //= 2
        place *= 2
    return lax.dynamic_index_in_dim(held, index, 0, keepdims=False)


def local(
    xbc,
    gate_z,
    dt_raw,
    conv_weight,
    conv_bias,
    dt_bias,
    decay_rate,
    d_skip,
    norm_gain,
    ssm_store,
    conv_store,
    source_of,
    prefix_len,
    span_len,
):
    me = lax.axis_index("dp")
    owners = lax.axis_size("dp")
    core = lax.axis_index("tensor").astype(jnp.int32).reshape(1)
    direct = owners <= DIRECT_MAX
    order = offsets(owners)
    state = ssm_store.reshape(owners, -1, STATE)
    rims = gather_rims(conv_store, source_of, me)
    if direct:
        held = [None] * owners
        far = [k for k in order if 2 * k >= owners]
        near = [k for k in order if 2 * k < owners]
        for some in (far, near + [0]):
            for k, piece in zip(some, cut_stage(state, some)):
                held[k] = swap(piece, "dp", k) if k else piece
    else:
        held = lax.all_to_all(state, "dp", split_axis=0, concat_axis=0, tiled=True)

    peer_xbc = swap(xbc, "tensor", 1)
    peer_gate = swap(gate_z, "tensor", 1)
    peer_dt = swap(dt_raw, "tensor", 1)
    heads = jnp.pad(jnp.stack([dt_bias, decay_rate]), ((0, 6), (0, LANES - dt_bias.shape[0])))
    intra, carry, c_proj = main_stage(
        core,
        prefix_len,
        d_skip,
        xbc,
        peer_xbc,
        conv_weight,
        conv_bias.reshape(1, -1),
        rims,
        gate_z,
        peer_gate,
        dt_raw,
        peer_dt,
        heads,
    )

    if direct:
        got = [None] * owners
        slots = order + [0]
        picked = pick_stage(me.astype(jnp.int32).reshape(1), source_of, held, slots)
        for k, piece in zip(slots, picked):
            got[k] = swap(piece, "dp", k) if k else piece
        turn = source_of[me] ^ me
    else:
        picked = jnp.take(held, source_of, axis=0)
        arrived = lax.all_to_all(picked, "dp", split_axis=0, concat_axis=0, tiled=True)
        got = [arrived.reshape(-1, STATE)]
        turn = jnp.zeros((), jnp.int32)
    return tail_stage(
        turn.astype(jnp.int32).reshape(1),
        span_len,
        got,
        intra,
        carry,
        c_proj,
        norm_gain.reshape(1, -1),
    )


def solution(mesh):
    in_specs = (
        P(("groups", "dp", "tensor"), None),
        P(("groups", "dp", "tensor"), None),
        P(("groups", "dp", "tensor"), None),
        P(),
        P(),
        P("tensor"),
        P("tensor"),
        P("tensor"),
        P("tensor"),
        P(("groups", "dp"), "tensor", None, None),
        P(("groups", "dp"), None, "tensor"),
        P("groups"),
        P(("groups", "dp")),
        P(("groups", "dp")),
    )
    out_specs = P(("groups", "dp"), "tensor")

    return jax.shard_map(local, mesh=mesh, in_specs=in_specs, out_specs=out_specs, check_vma=False)
```

profile of v0, /device:TPU:0, one launch (start us, length us, event | category | flops | bytes accessed | tf_op | source)
XLA Modules:
  0.0 87.3 jit_solution(3138223634058890284)
XLA Ops:
  0.0 1.3 %copy-done.1 = bf16[1,64,64,128]{3,2,1,0:T(8,128)(2,1)S(1)} copy-done((bf16[1,64,64,128]{3,2,1,0:T(8,128)(2,1)S(1)}, bf16[1,64,64,128]{3,2,1,0:T(8,128)(2,1)}, u32[]{:S(2)}) %copy-start.1) | copy-done | bytes 1048600
  1.3 0.7 cut_stage.2
  2.0 0.0 copy-start.5
  2.0 3.0 %collective-permute-start = (bf16[512,128]{1,0:T(8,128)(2,1)S(1)}, bf16[512,128]{1,0:T(8,128)(2,1)S(1)}, u32[]{:S(2)}, u32[]{:S(2)}) collective-permute-start(bf16[512,128]{1,0:T(8,128)(2,1)S(1)} %get-tuple-element.25), channel_id=1, source_target_pairs={{0,2},{2,0},{4,6},{6,4},{8,10},{10,8},{12,14},{14,12},{1,3},{3,1},... | collective-permute-start | bytes 393224 | tf_op jit(solution)/shard_map/ppermute | solution.py:21
  5.1 1.6 %collective-permute-start.1 = (bf16[512,128]{1,0:T(8,128)(2,1)S(1)}, bf16[512,128]{1,0:T(8,128)(2,1)S(1)}, u32[]{:S(2)}, u32[]{:S(2)}) collective-permute-start(bf16[512,128]{1,0:T(8,128)(2,1)S(1)} %get-tuple-element.26), channel_id=1, source_target_pairs={{0,4},{2,6},{4,0},{6,2},{8,12},{10,14},{12,8},{14,10},{1,5},{3,7},... | collective-permute-start | bytes 393224 | tf_op jit(solution)/shard_map/ppermute | solution.py:21
  6.7 1.4 %cut_stage.3 = (bf16[512,128]{1,0:T(8,128)(2,1)S(1)}, bf16[512,128]{1,0:T(8,128)(2,1)S(1)}, bf16[512,128]{1,0:T(8,128)(2,1)}, bf16[512,128]{1,0:T(8,128)(2,1)}) custom-call(bf16[8,512,128]{2,1,0:T(8,128)(2,1)S(1)} %bitcast.12), custom_call_target="tpu_custom_call" | custom-call | tf_op jit(solution)/shard_map/cut_stage/pallas_call | solution.py:284
  8.1 3.1 %collective-permute-start.3 = (bf16[512,128]{1,0:T(8,128)(2,1)S(1)}, bf16[512,128]{1,0:T(8,128)(2,1)S(1)}, u32[]{:S(2)}, u32[]{:S(2)}) collective-permute-start(bf16[512,128]{1,0:T(8,128)(2,1)S(1)} %get-tuple-element.28), channel_id=1, source_target_pairs={{0,8},{2,10},{4,12},{6,14},{8,0},{10,2},{12,4},{14,6},{1,9},{3,11}... | collective-permute-start | bytes 393224 | tf_op jit(solution)/shard_map/ppermute | solution.py:21
  11.1 0.1 collective-permute-start.15
  11.2 7.4 %collective-permute-done.15 = bf16[1,3,4608]{2,1,0:T(4,128)(2,1)S(1)} collective-permute-done((bf16[1,3,4608]{2,1,0:T(4,128)(2,1)}, bf16[1,3,4608]{2,1,0:T(4,128)(2,1)S(1)}, u32[]{:S(2)}, u32[]{:S(2)}) %collective-permute-start.15) | collective-permute-done | bytes 27680 | tf_op jit(solution)/shard_map/ppermute | solution.py:21
  18.7 0.6 copy-done.7
  19.3 0.5 collective-permute-start.18
  19.8 0.6 copy-done.9
  20.4 0.7 collective-permute-start.4
  21.1 0.6 copy-done.11
  21.8 3.1 %collective-permute-start.5 = (bf16[512,128]{1,0:T(8,128)(2,1)}, bf16[512,128]{1,0:T(8,128)(2,1)}, u32[]{:S(2)}, u32[]{:S(2)}) collective-permute-start(bf16[512,128]{1,0:T(8,128)(2,1)} %get-tuple-element.30), channel_id=1, source_target_pairs={{0,12},{2,14},{4,8},{6,10},{8,4},{10,6},{12,0},{14,2},{1,13},{3,15... | collective-permute-start | bytes 393224 | tf_op jit(solution)/shard_map/ppermute | solution.py:21
  24.8 0.6 copy-done.13
  25.5 1.4 %collective-permute-start.6 = (bf16[512,128]{1,0:T(8,128)(2,1)}, bf16[512,128]{1,0:T(8,128)(2,1)}, u32[]{:S(2)}, u32[]{:S(2)}) collective-permute-start(bf16[512,128]{1,0:T(8,128)(2,1)} %get-tuple-element.31), channel_id=1, source_target_pairs={{0,14},{2,12},{4,10},{6,8},{8,6},{10,4},{12,2},{14,0},{1,15},{3,13... | collective-permute-start | bytes 393224 | tf_op jit(solution)/shard_map/ppermute | solution.py:21
  26.9 1.4 %pad_maximum_fusion.1 = bf16[2,3,4608]{2,1,0:T(4,128)(2,1)} fusion(bf16[1,3,4608]{2,1,0:T(4,128)(2,1)S(1)} %collective-permute-done.15, bf16[1,3,4608]{2,1,0:T(4,128)(2,1)} %param.24), kind=kLoop, calls=%fused_computation.5 | loop fusion | flops 27648 | bytes 110592 | tf_op jit(solution)/shard_map/concatenate | solution.py:334
  28.3 8.4 %collective-permute-done.4.refs_5_ = bf16[512,128]{1,0:T(8,128)(2,1)S(1)} collective-permute-done((bf16[512,128]{1,0:T(8,128)(2,1)S(1)}, bf16[512,128]{1,0:T(8,128)(2,1)S(1)}, u32[]{:S(2)}, u32[]{:S(2)}) %collective-permute-start.4) | collective-permute-done | bytes 131104 | tf_op jit(solution)/shard_map/ppermute | solution.py:21
  36.7 0.6 copy-done.15
  37.4 1.2 %dynamic_slice.8 = s32[1]{0:T(128)} dynamic-slice(s32[8]{0:T(128)} %source_ref.1, s32[]{:T(128)S(6)} %select_n.17), dynamic_slice_sizes={1} | dynamic-slice | bytes 12 | tf_op jit(solution)/shard_map/dynamic_slice | solution.py:400
  40.5 0.1 collective-permute-start.19
  40.6 0.9 %copy-done.6 = bf16[512,128]{1,0:T(8,128)(2,1)S(1)} copy-done((bf16[512,128]{1,0:T(8,128)(2,1)S(1)}, bf16[512,128]{1,0:T(8,128)(2,1)}, u32[]{:S(2)}) %copy-start.6) | copy-done | bytes 131096
  41.5 0.9 %copy-done.8 = bf16[512,128]{1,0:T(8,128)(2,1)S(1)} copy-done((bf16[512,128]{1,0:T(8,128)(2,1)S(1)}, bf16[512,128]{1,0:T(8,128)(2,1)}, u32[]{:S(2)}) %copy-start.8) | copy-done | bytes 131096
  42.4 0.9 %copy-done.10 = bf16[512,128]{1,0:T(8,128)(2,1)S(1)} copy-done((bf16[512,128]{1,0:T(8,128)(2,1)S(1)}, bf16[512,128]{1,0:T(8,128)(2,1)}, u32[]{:S(2)}) %copy-start.10) | copy-done | bytes 131096
  43.3 0.9 %copy-done.12 = bf16[512,128]{1,0:T(8,128)(2,1)S(1)} copy-done((bf16[512,128]{1,0:T(8,128)(2,1)S(1)}, bf16[512,128]{1,0:T(8,128)(2,1)}, u32[]{:S(2)}) %copy-start.12) | copy-done | bytes 131096
  44.2 0.9 %copy-done.14 = bf16[512,128]{1,0:T(8,128)(2,1)S(1)} copy-done((bf16[512,128]{1,0:T(8,128)(2,1)S(1)}, bf16[512,128]{1,0:T(8,128)(2,1)}, u32[]{:S(2)}) %copy-start.14) | copy-done | bytes 131096
  45.1 0.9 %copy-done.16 = bf16[512,128]{1,0:T(8,128)(2,1)S(1)} copy-done((bf16[512,128]{1,0:T(8,128)(2,1)S(1)}, bf16[512,128]{1,0:T(8,128)(2,1)}, u32[]{:S(2)}) %copy-start.16) | copy-done | bytes 131096
  46.0 0.7 copy-done.19
  46.6 1.9 %pick_stage.1 = (bf16[512,128]{1,0:T(8,128)(2,1)S(1)}, bf16[512,128]{1,0:T(8,128)(2,1)S(1)}, bf16[512,128]{1,0:T(8,128)(2,1)S(1)}, bf16[512,128]{1,0:T(8,128)(2,...) custom-call(s32[1]{0:T(128)} %bitcast.2.me_ref, ...), custom_call_target="tpu_custom_call" | custom-call | tf_op jit(solution)/shard_map/pick_stage/pallas_call | solution.py:316
  48.5 1.7 %collective-permute-start.10 = (bf16[512,128]{1,0:T(8,128)(2,1)S(1)}, bf16[512,128]{1,0:T(8,128)(2,1)S(1)}, u32[]{:S(2)}, u32[]{:S(2)}) collective-permute-start(bf16[512,128]{1,0:T(8,128)(2,1)S(1)} %get-tuple-element.36), channel_id=1, source_target_pairs={{0,8},{2,10},{4,12},{6,14},{8,0},{10,2},{12,4},{14,6},{1,9},{3,11}... | collective-permute-start | bytes 393224 | tf_op jit(solution)/shard_map/ppermute | solution.py:21
  50.2 1.6 %collective-permute-start.11 = (bf16[512,128]{1,0:T(8,128)(2,1)S(1)}, bf16[512,128]{1,0:T(8,128)(2,1)S(1)}, u32[]{:S(2)}, u32[]{:S(2)}) collective-permute-start(bf16[512,128]{1,0:T(8,128)(2,1)S(1)} %get-tuple-element.37), channel_id=1, source_target_pairs={{0,10},{2,8},{4,14},{6,12},{8,2},{10,0},{12,6},{14,4},{1,11},{3,9}... | collective-permute-start | bytes 393224 | tf_op jit(solution)/shard_map/ppermute | solution.py:21
  51.8 1.0 %pad_maximum_fusion = bf16[4,3,4608]{2,1,0:T(4,128)(2,1)S(1)} fusion(bf16[2,3,4608]{2,1,0:T(4,128)(2,1)} %collective-permute-done.16, bf16[1,3,4608]{2,1,0:T(4,128)(2,1)} %copy-done.21, bf16[1,3,4608]{2,1,0:T(4,128)(2,1)} %param.24), kind=kLoop, calls=%fused_computation.4 | loop fusion | flops 110592 | bytes 221184 | tf_op jit(solution)/shard_map/concatenate | solution.py:334
  52.8 1.3 %collective-permute-start.17 = (bf16[4,3,4608]{2,1,0:T(4,128)(2,1)S(1)}, bf16[4,3,4608]{2,1,0:T(4,128)(2,1)S(1)}, u32[]{:S(2)}, u32[]{:S(2)}) collective-permute-start(bf16[4,3,4608]{2,1,0:T(4,128)(2,1)S(1)} %pad_maximum_fusion), channel_id=1, source_target_pairs={{0,2},{2,0},{4,6},{6,4},{8,10},{10,8},{12,14},{14,12},{1,3},{3,1},... | collective-permute-start | bytes 331784 | tf_op jit(solution)/shard_map/ppermute | solution.py:21
  54.1 0.7 select_maximum_fusion.head_rows
  54.8 3.8 %collective-permute-done.17 = bf16[4,3,4608]{2,1,0:T(4,128)(2,1)S(1)} collective-permute-done((bf16[4,3,4608]{2,1,0:T(4,128)(2,1)S(1)}, bf16[4,3,4608]{2,1,0:T(4,128)(2,1)S(1)}, u32[]{:S(2)}, u32[]{:S(2)}) %collective-permute-start.17) | collective-permute-done | bytes 110624 | tf_op jit(solution)/shard_map/ppermute | solution.py:21
  58.6 1.8 %collective-permute-start.12 = (bf16[512,128]{1,0:T(8,128)(2,1)S(1)}, bf16[512,128]{1,0:T(8,128)(2,1)S(1)}, u32[]{:S(2)}, u32[]{:S(2)}) collective-permute-start(bf16[512,128]{1,0:T(8,128)(2,1)S(1)} %get-tuple-element.38), channel_id=1, source_target_pairs={{0,12},{2,14},{4,8},{6,10},{8,4},{10,6},{12,0},{14,2},{1,13},{3,15... | collective-permute-start | bytes 393224 | tf_op jit(solution)/shard_map/ppermute | solution.py:21
  60.4 1.1 %collective-permute-done.10.refs_4_ = bf16[512,128]{1,0:T(8,128)(2,1)S(1)} collective-permute-done((bf16[512,128]{1,0:T(8,128)(2,1)S(1)}, bf16[512,128]{1,0:T(8,128)(2,1)S(1)}, u32[]{:S(2)}, u32[]{:S(2)}) %collective-permute-start.10) | collective-permute-done | bytes 131104 | tf_op jit(solution)/shard_map/ppermute | solution.py:21
  61.5 2.0 %collective-permute-start.13 = (bf16[512,128]{1,0:T(8,128)(2,1)S(1)}, bf16[512,128]{1,0:T(8,128)(2,1)S(1)}, u32[]{:S(2)}, u32[]{:S(2)}) collective-permute-start(bf16[512,128]{1,0:T(8,128)(2,1)S(1)} %get-tuple-element.39), channel_id=1, source_target_pairs={{0,14},{2,12},{4,10},{6,8},{8,6},{10,4},{12,2},{14,0},{1,15},{3,13... | collective-permute-start | bytes 393224 | tf_op jit(solution)/shard_map/ppermute | solution.py:21
  63.5 6.7 %collective-permute-done.11.refs_5_ = bf16[512,128]{1,0:T(8,128)(2,1)S(1)} collective-permute-done((bf16[512,128]{1,0:T(8,128)(2,1)S(1)}, bf16[512,128]{1,0:T(8,128)(2,1)S(1)}, u32[]{:S(2)}, u32[]{:S(2)}) %collective-permute-start.11) | collective-permute-done | bytes 131104 | tf_op jit(solution)/shard_map/ppermute | solution.py:21
  70.2 1.2 %collective-permute-start.7 = (bf16[512,128]{1,0:T(8,128)(2,1)S(1)}, bf16[512,128]{1,0:T(8,128)(2,1)S(1)}, u32[]{:S(2)}, u32[]{:S(2)}) collective-permute-start(bf16[512,128]{1,0:T(8,128)(2,1)S(1)} %get-tuple-element.33), channel_id=1, source_target_pairs={{0,2},{2,0},{4,6},{6,4},{8,10},{10,8},{12,14},{14,12},{1,3},{3,1},... | collective-permute-start | bytes 393224 | tf_op jit(solution)/shard_map/ppermute | solution.py:21
  71.4 2.3 %collective-permute-start.9 = (bf16[512,128]{1,0:T(8,128)(2,1)S(1)}, bf16[512,128]{1,0:T(8,128)(2,1)S(1)}, u32[]{:S(2)}, u32[]{:S(2)}) collective-permute-start(bf16[512,128]{1,0:T(8,128)(2,1)S(1)} %get-tuple-element.35), channel_id=1, source_target_pairs={{0,6},{2,4},{4,2},{6,0},{8,14},{10,12},{12,10},{14,8},{1,7},{3,5},... | collective-permute-start | bytes 393224 | tf_op jit(solution)/shard_map/ppermute | solution.py:21
  73.7 0.1 fusion.3.rims_x.rims_bc
  73.8 0.8 copy-done.4
  74.6 0.7 copy-done.17
  75.3 0.7 copy-done.20
  75.9 8.1 %main_stage.1 = (f32[128,4096]{1,0:T(8,128)S(1)}, f32[128,4096]{1,0:T(8,128)S(1)}, bf16[128,256]{1,0:T(8,128)(2,1)S(1)}) custom-call(s32[1]{0:T(128)} %bitcast.4.core_ref, s32[1]{0:T(128)S(6)} %copy.15.live_ref, f32[64]{0:T(128)S(1)} %copy-done.20, bf16[64,9216]{1,0:T(8,128)(2,1)S(1)} %copy-done, ...), custom_call_target="tpu_custom_call" | custom-call | flops 400000000 | bytes 8000000 | tf_op jit(solution)/shard_map/main_stage/pallas_call | solution.py:197
  84.1 3.2 %tail_stage.1 = bf16[128,4096]{1,0:T(8,128)(2,1)} custom-call(s32[1]{0:T(128)} %bitcast.1.turn_ref, s32[1]{0:T(128)S(6)} %copy.16.span_ref, bf16[512,128]{1,0:T(8,128)(2,1)S(1)} %get-tuple-element.32.refs_0_, bf16[512,128]{1,0:T(8,128)(2,1)S(1)} %collective-permute-done.7.refs_1_, bf16[512,128]{1,0:T(8,128)(2,1)S(1)} %collective-permute-done.8.refs_2_, ...), custom_call_target="tpu_custom_call" | custom-call | flops 140000000 | bytes 6000000 | tf_op jit(solution)/shard_map/tail_stage/pallas_call | solution.py:262
  (46 shorter events, 0.1 us)
Async XLA Ops:
  0.0 18.6 %copy-start = (bf16[64,9216]{1,0:T(8,128)(2,1)S(1)}, bf16[64,9216]{1,0:T(8,128)(2,1)}, u32[]{:S(2)}) copy-start(bf16[64,9216]{1,0:T(8,128)(2,1)} %own_bc.1) | copy-start | bytes 3538948
  0.0 1.3 %copy-start.1 = (bf16[1,64,64,128]{3,2,1,0:T(8,128)(2,1)S(1)}, bf16[1,64,64,128]{3,2,1,0:T(8,128)(2,1)}, u32[]{:S(2)}) copy-start(bf16[1,64,64,128]{3,2,1,0:T(8,128)(2,1)} %param.23) | copy-start | bytes 3145732
  1.3 72.4 %copy-start.2 = (bf16[64,8192]{1,0:T(8,128)(2,1)S(1)}, bf16[64,8192]{1,0:T(8,128)(2,1)}, u32[]{:S(2)}) copy-start(bf16[64,8192]{1,0:T(8,128)(2,1)} %own_gate.1) | copy-start | bytes 3145732
  1.3 72.4 %copy-start.3 = (f32[4,9216]{1,0:T(4,128)S(1)}, f32[4,9216]{1,0:T(4,128)}, u32[]{:S(2)}) copy-start(f32[4,9216]{1,0:T(4,128)} %weight_bc.1) | copy-start | bytes 442372
  2.0 9.2 %copy-start.5 = (bf16[512,128]{1,0:T(8,128)(2,1)}, bf16[512,128]{1,0:T(8,128)(2,1)S(1)}, u32[]{:S(2)}) copy-start(bf16[512,128]{1,0:T(8,128)(2,1)S(1)} %get-tuple-element.24.refs_0_) | copy-start | bytes 393220
  2.0 16.6 %collective-permute-start = (bf16[512,128]{1,0:T(8,128)(2,1)S(1)}, bf16[512,128]{1,0:T(8,128)(2,1)S(1)}, u32[]{:S(2)}, u32[]{:S(2)}) collective-permute-start(bf16[512,128]{1,0:T(8,128)(2,1)S(1)} %get-tuple-element.25), channel_id=1, source_target_pairs={{0,2},{2,0},{4,6},{6,4},{8,10},{10,8},{12,14},{14,12},{1,3},{3,1},... | collective-permute-start | bytes 393224 | tf_op jit(solution)/shard_map/ppermute | solution.py:21
  5.1 14.7 %collective-permute-start.1 = (bf16[512,128]{1,0:T(8,128)(2,1)S(1)}, bf16[512,128]{1,0:T(8,128)(2,1)S(1)}, u32[]{:S(2)}, u32[]{:S(2)}) collective-permute-start(bf16[512,128]{1,0:T(8,128)(2,1)S(1)} %get-tuple-element.26), channel_id=1, source_target_pairs={{0,4},{2,6},{4,0},{6,2},{8,12},{10,14},{12,8},{14,10},{1,5},{3,7},... | collective-permute-start | bytes 393224 | tf_op jit(solution)/shard_map/ppermute | solution.py:21
  6.7 14.5 %collective-permute-start.2 = (bf16[512,128]{1,0:T(8,128)(2,1)S(1)}, bf16[512,128]{1,0:T(8,128)(2,1)S(1)}, u32[]{:S(2)}, u32[]{:S(2)}) collective-permute-start(bf16[512,128]{1,0:T(8,128)(2,1)S(1)} %get-tuple-element.27), channel_id=1, source_target_pairs={{0,6},{2,4},{4,2},{6,0},{8,14},{10,12},{12,10},{14,8},{1,7},{3,5},... | collective-permute-start | bytes 393224 | tf_op jit(solution)/shard_map/ppermute | solution.py:21
  8.1 16.7 %collective-permute-start.3 = (bf16[512,128]{1,0:T(8,128)(2,1)S(1)}, bf16[512,128]{1,0:T(8,128)(2,1)S(1)}, u32[]{:S(2)}, u32[]{:S(2)}) collective-permute-start(bf16[512,128]{1,0:T(8,128)(2,1)S(1)} %get-tuple-element.28), channel_id=1, source_target_pairs={{0,8},{2,10},{4,12},{6,14},{8,0},{10,2},{12,4},{14,6},{1,9},{3,11}... | collective-permute-start | bytes 393224 | tf_op jit(solution)/shard_map/ppermute | solution.py:21
  11.1 7.5 %collective-permute-start.15 = (bf16[1,3,4608]{2,1,0:T(4,128)(2,1)}, bf16[1,3,4608]{2,1,0:T(4,128)(2,1)S(1)}, u32[]{:S(2)}, u32[]{:S(2)}) collective-permute-start(bf16[1,3,4608]{2,1,0:T(4,128)(2,1)} %param.24), channel_id=1, source_target_pairs={{0,8},{2,10},{4,12},{6,14},{8,0},{10,2},{12,4},{14,6},{1,9},{3,11}... | collective-permute-start | bytes 82952 | tf_op jit(solution)/shard_map/ppermute | solution.py:21
  18.6 18.1 %copy-start.21 = (bf16[1,3,4608]{2,1,0:T(4,128)(2,1)}, bf16[1,3,4608]{2,1,0:T(4,128)(2,1)S(1)}, u32[]{:S(2)}) copy-start(bf16[1,3,4608]{2,1,0:T(4,128)(2,1)S(1)} %collective-permute-done.15) | copy-start | bytes 82948
  18.6 52.8 %collective-permute-start.14 = (bf16[64,9216]{1,0:T(8,128)(2,1)S(1)}, bf16[64,9216]{1,0:T(8,128)(2,1)S(1)}, u32[]{:S(2)}, u32[]{:S(2)}) collective-permute-start(bf16[64,9216]{1,0:T(8,128)(2,1)S(1)} %copy-done), channel_id=1, source_target_pairs={{0,1},{1,0},{2,3},{3,2},{4,5},{5,4},{6,7},{7,6},{8,9},{9,8},{10,11... | collective-permute-start | bytes 3538952 | tf_op jit(solution)/shard_map/ppermute | solution.py:21
  18.6 0.7 copy-start.7
  19.3 52.1 %collective-permute-start.18 = (bf16[64,8192]{1,0:T(8,128)(2,1)}, bf16[64,8192]{1,0:T(8,128)(2,1)}, u32[]{:S(2)}, u32[]{:S(2)}) collective-permute-start(bf16[64,8192]{1,0:T(8,128)(2,1)} %own_gate.1), channel_id=1, source_target_pairs={{0,1},{1,0},{2,3},{3,2},{4,5},{5,4},{6,7},{7,6},{8,9},{9,8},{10,11... | collective-permute-start | bytes 3145736 | tf_op jit(solution)/shard_map/ppermute | solution.py:21
  19.8 0.6 copy-start.9
  20.4 16.3 %collective-permute-start.4 = (bf16[512,128]{1,0:T(8,128)(2,1)S(1)}, bf16[512,128]{1,0:T(8,128)(2,1)S(1)}, u32[]{:S(2)}, u32[]{:S(2)}) collective-permute-start(bf16[512,128]{1,0:T(8,128)(2,1)S(1)} %get-tuple-element.29), channel_id=1, source_target_pairs={{0,10},{2,8},{4,14},{6,12},{8,2},{10,0},{12,6},{14,4},{1,11},{3,9}... | collective-permute-start | bytes 393224 | tf_op jit(solution)/shard_map/ppermute | solution.py:21
  21.1 0.6 copy-start.11
  21.8 18.7 %collective-permute-start.5 = (bf16[512,128]{1,0:T(8,128)(2,1)}, bf16[512,128]{1,0:T(8,128)(2,1)}, u32[]{:S(2)}, u32[]{:S(2)}) collective-permute-start(bf16[512,128]{1,0:T(8,128)(2,1)} %get-tuple-element.30), channel_id=1, source_target_pairs={{0,12},{2,14},{4,8},{6,10},{8,4},{10,6},{12,0},{14,2},{1,13},{3,15... | collective-permute-start | bytes 393224 | tf_op jit(solution)/shard_map/ppermute | solution.py:21
  24.8 0.7 copy-start.13
  25.5 15.1 %collective-permute-start.6 = (bf16[512,128]{1,0:T(8,128)(2,1)}, bf16[512,128]{1,0:T(8,128)(2,1)}, u32[]{:S(2)}, u32[]{:S(2)}) collective-permute-start(bf16[512,128]{1,0:T(8,128)(2,1)} %get-tuple-element.31), channel_id=1, source_target_pairs={{0,14},{2,12},{4,10},{6,8},{8,6},{10,4},{12,2},{14,0},{1,15},{3,13... | collective-permute-start | bytes 393224 | tf_op jit(solution)/shard_map/ppermute | solution.py:21
  36.7 0.6 copy-start.15
  37.4 12.9 %collective-permute-start.16 = (bf16[2,3,4608]{2,1,0:T(4,128)(2,1)}, bf16[2,3,4608]{2,1,0:T(4,128)(2,1)}, u32[]{:S(2)}, u32[]{:S(2)}) collective-permute-start(bf16[2,3,4608]{2,1,0:T(4,128)(2,1)} %pad_maximum_fusion.1), channel_id=1, source_target_pairs={{0,4},{2,6},{4,0},{6,2},{8,12},{10,14},{12,8},{14,10},{1,5},{3,7},... | collective-permute-start | bytes 165896 | tf_op jit(solution)/shard_map/ppermute | solution.py:21
  40.5 12.3 %collective-permute-start.19 = (bf16[64,128]{1,0:T(8,128)(2,1)}, bf16[64,128]{1,0:T(8,128)(2,1)S(1)}, u32[]{:S(2)}, u32[]{:S(2)}) collective-permute-start(bf16[64,128]{1,0:T(8,128)(2,1)} %own_dt.1), channel_id=1, source_target_pairs={{0,1},{1,0},{2,3},{3,2},{4,5},{5,4},{6,7},{7,6},{8,9},{9,8},{10,11... | collective-permute-start | bytes 49160 | tf_op jit(solution)/shard_map/ppermute | solution.py:21
  40.6 0.9 %copy-start.6 = (bf16[512,128]{1,0:T(8,128)(2,1)S(1)}, bf16[512,128]{1,0:T(8,128)(2,1)}, u32[]{:S(2)}) copy-start(bf16[512,128]{1,0:T(8,128)(2,1)} %copy-done.5) | copy-start | bytes 393220
  41.5 0.9 %copy-start.8 = (bf16[512,128]{1,0:T(8,128)(2,1)S(1)}, bf16[512,128]{1,0:T(8,128)(2,1)}, u32[]{:S(2)}) copy-start(bf16[512,128]{1,0:T(8,128)(2,1)} %copy-done.7) | copy-start | bytes 393220
  42.4 0.9 %copy-start.10 = (bf16[512,128]{1,0:T(8,128)(2,1)S(1)}, bf16[512,128]{1,0:T(8,128)(2,1)}, u32[]{:S(2)}) copy-start(bf16[512,128]{1,0:T(8,128)(2,1)} %copy-done.9) | copy-start | bytes 393220
  43.3 0.9 %copy-start.12 = (bf16[512,128]{1,0:T(8,128)(2,1)S(1)}, bf16[512,128]{1,0:T(8,128)(2,1)}, u32[]{:S(2)}) copy-start(bf16[512,128]{1,0:T(8,128)(2,1)} %copy-done.11) | copy-start | bytes 393220
  44.2 0.9 %copy-start.14 = (bf16[512,128]{1,0:T(8,128)(2,1)S(1)}, bf16[512,128]{1,0:T(8,128)(2,1)}, u32[]{:S(2)}) copy-start(bf16[512,128]{1,0:T(8,128)(2,1)} %copy-done.13) | copy-start | bytes 393220
  45.1 0.9 %copy-start.16 = (bf16[512,128]{1,0:T(8,128)(2,1)S(1)}, bf16[512,128]{1,0:T(8,128)(2,1)}, u32[]{:S(2)}) copy-start(bf16[512,128]{1,0:T(8,128)(2,1)} %copy-done.15) | copy-start | bytes 393220
  46.0 0.7 copy-start.19
  48.5 13.0 %collective-permute-start.10 = (bf16[512,128]{1,0:T(8,128)(2,1)S(1)}, bf16[512,128]{1,0:T(8,128)(2,1)S(1)}, u32[]{:S(2)}, u32[]{:S(2)}) collective-permute-start(bf16[512,128]{1,0:T(8,128)(2,1)S(1)} %get-tuple-element.36), channel_id=1, source_target_pairs={{0,8},{2,10},{4,12},{6,14},{8,0},{10,2},{12,4},{14,6},{1,9},{3,11}... | collective-permute-start | bytes 393224 | tf_op jit(solution)/shard_map/ppermute | solution.py:21
  50.2 20.0 %collective-permute-start.11 = (bf16[512,128]{1,0:T(8,128)(2,1)S(1)}, bf16[512,128]{1,0:T(8,128)(2,1)S(1)}, u32[]{:S(2)}, u32[]{:S(2)}) collective-permute-start(bf16[512,128]{1,0:T(8,128)(2,1)S(1)} %get-tuple-element.37), channel_id=1, source_target_pairs={{0,10},{2,8},{4,14},{6,12},{8,2},{10,0},{12,6},{14,4},{1,11},{3,9}... | collective-permute-start | bytes 393224 | tf_op jit(solution)/shard_map/ppermute | solution.py:21
  52.8 5.7 %collective-permute-start.17 = (bf16[4,3,4608]{2,1,0:T(4,128)(2,1)S(1)}, bf16[4,3,4608]{2,1,0:T(4,128)(2,1)S(1)}, u32[]{:S(2)}, u32[]{:S(2)}) collective-permute-start(bf16[4,3,4608]{2,1,0:T(4,128)(2,1)S(1)} %pad_maximum_fusion), channel_id=1, source_target_pairs={{0,2},{2,0},{4,6},{6,4},{8,10},{10,8},{12,14},{14,12},{1,3},{3,1},... | collective-permute-start | bytes 331784 | tf_op jit(solution)/shard_map/ppermute | solution.py:21
  58.6 25.5 %collective-permute-start.12 = (bf16[512,128]{1,0:T(8,128)(2,1)S(1)}, bf16[512,128]{1,0:T(8,128)(2,1)S(1)}, u32[]{:S(2)}, u32[]{:S(2)}) collective-permute-start(bf16[512,128]{1,0:T(8,128)(2,1)S(1)} %get-tuple-element.38), channel_id=1, source_target_pairs={{0,12},{2,14},{4,8},{6,10},{8,4},{10,6},{12,0},{14,2},{1,13},{3,15... | collective-permute-start | bytes 393224 | tf_op jit(solution)/shard_map/ppermute | solution.py:21
  61.5 22.5 %collective-permute-start.13 = (bf16[512,128]{1,0:T(8,128)(2,1)S(1)}, bf16[512,128]{1,0:T(8,128)(2,1)S(1)}, u32[]{:S(2)}, u32[]{:S(2)}) collective-permute-start(bf16[512,128]{1,0:T(8,128)(2,1)S(1)} %get-tuple-element.39), channel_id=1, source_target_pairs={{0,14},{2,12},{4,10},{6,8},{8,6},{10,4},{12,2},{14,0},{1,15},{3,13... | collective-permute-start | bytes 393224 | tf_op jit(solution)/shard_map/ppermute | solution.py:21
  70.2 13.9 %collective-permute-start.7 = (bf16[512,128]{1,0:T(8,128)(2,1)S(1)}, bf16[512,128]{1,0:T(8,128)(2,1)S(1)}, u32[]{:S(2)}, u32[]{:S(2)}) collective-permute-start(bf16[512,128]{1,0:T(8,128)(2,1)S(1)} %get-tuple-element.33), channel_id=1, source_target_pairs={{0,2},{2,0},{4,6},{6,4},{8,10},{10,8},{12,14},{14,12},{1,3},{3,1},... | collective-permute-start | bytes 393224 | tf_op jit(solution)/shard_map/ppermute | solution.py:21
  71.4 12.7 %collective-permute-start.8 = (bf16[512,128]{1,0:T(8,128)(2,1)S(1)}, bf16[512,128]{1,0:T(8,128)(2,1)S(1)}, u32[]{:S(2)}, u32[]{:S(2)}) collective-permute-start(bf16[512,128]{1,0:T(8,128)(2,1)S(1)} %get-tuple-element.34), channel_id=1, source_target_pairs={{0,4},{2,6},{4,0},{6,2},{8,12},{10,14},{12,8},{14,10},{1,5},{3,7},... | collective-permute-start | bytes 393224 | tf_op jit(solution)/shard_map/ppermute | solution.py:21
  71.4 12.7 %collective-permute-start.9 = (bf16[512,128]{1,0:T(8,128)(2,1)S(1)}, bf16[512,128]{1,0:T(8,128)(2,1)S(1)}, u32[]{:S(2)}, u32[]{:S(2)}) collective-permute-start(bf16[512,128]{1,0:T(8,128)(2,1)S(1)} %get-tuple-element.35), channel_id=1, source_target_pairs={{0,6},{2,4},{4,2},{6,0},{8,14},{10,12},{12,10},{14,8},{1,7},{3,5},... | collective-permute-start | bytes 393224 | tf_op jit(solution)/shard_map/ppermute | solution.py:21
  73.8 0.8 copy-start.4
  74.6 0.7 copy-start.17
  75.3 0.7 copy-start.20
  75.9 8.1 %copy-start.18 = (f32[4096]{0:T(1024)S(1)}, f32[4096]{0:T(1024)}, u32[]{:S(2)}) copy-start(f32[4096]{0:T(1024)} %param.22) | copy-start | bytes 49156
where the time goes:
time: 88.2 us; the launch traced here: 87.3 us
  waiting for transfers between devices  27.4 us (31%)
  starting transfers between devices  25.3 us (29%)
  Pallas kernels  15.3 us (17%)
  local copies, waits for them, and re-layouts  14 us (16%)
  other arithmetic  3.23 us (4%)
  between operations  2.1 us (2%)
    ppermute x20, waiting for transfers between devices, swap(): return lax.ppermute(value, axis, [(i, i ^ offset) for i in range(count)])  27.4 us
    ppermute x20, starting transfers between devices, swap(): return lax.ppermute(value, axis, [(i, i ^ offset) for i in range(count)])  25.3 us
    unnamed x44, local copies, waits for them, and re-layouts  12.8 us
    pallas_call x1, Pallas kernels, main_stage(): pl.pallas_call(main_kernel, grid_spec=grid_spec, out_shape=[jax.ShapeDtyp...  8.08 us
    pallas_call x1, Pallas kernels, tail_stage(): pl.pallas_call(functools.partial(tail_kernel, len(pieces)), grid_spec=gri...  3.22 us
    concatenate x2, other arithmetic, gather_rims(): held = jnp.concatenate([held, other], axis=0)  2.45 us
    pallas_call x2, Pallas kernels, cut_stage(): pl.pallas_call(functools.partial(cut_kernel, chosen), in_specs=[pl.BlockS...  2.1 us
    pallas_call x1, Pallas kernels, pick_stage(): pl.pallas_call(functools.partial(pick_kernel, tuple(order)), grid_spec=gr...  1.88 us
  transfers between devices with their start and end apart: 20, of which 5 were waited for; matrix products, arithmetic and copies ran while one was open for 5% of the time, Pallas kernels for 13%

commit v1 on v0

--- a/solution.py
+++ b/solution.py
@@ -19,6 +19,10 @@
 def swap(value, axis, offset):
     count = lax.axis_size(axis)
     return lax.ppermute(value, axis, [(i, i ^ offset) for i in range(count)])
+
+
+def keep_in(space, *values):
+    return [pltpu.with_memory_space_constraint(value, space) for value in values]
 
 
 def offsets(count):
@@ -194,6 +198,7 @@
             pltpu.VMEM((LANES, count), jnp.float32),
         ],
     )
+    xbc, peer_xbc, gate, peer_gate = keep_in(pltpu.HBM, xbc, peer_xbc, gate, peer_gate)
     return pl.pallas_call(
         main_kernel,
         grid_spec=grid_spec,
@@ -208,65 +213,69 @@
     )(core, live, d_skip, xbc, peer_xbc, xbc, peer_xbc, weight, weight, bias, bias, rims, rims, gate, peer_gate, dt, peer_dt, heads)
 
 
-def tail_kernel(count_pieces, turn_ref, span_ref, *refs):
-    pieces = refs[:count_pieces]
-    intra, carry, c_proj, gain, out, state, sems = refs[count_pieces:]
+def tail_kernel(base, has_before, turn_ref, span_ref, *refs):
+    out, wide, narrow, sems = refs[-4:]
+    intra, carry, c_proj, gain = refs[-8 - has_before : -4 - has_before]
+    pieces = refs[: -8 - has_before]
+    tokens = wide.shape[0]
+    count, rows = len(pieces), pieces[0].shape[0]
+    group = base ^ (turn_ref[0] // count)
+    within = turn_ref[0] % count
+    keep = lax.broadcasted_iota(jnp.int32, (tokens, 1), 0) < span_ref[0]
+    c = c_proj[:, pl.ds(pl.multiple_of(group * STATE, STATE), STATE)]
+    part = min(rows, 512)
+    total = jnp.zeros((tokens, 1), jnp.float32)
+    places = []
+    for k, piece in enumerate(pieces):
+        for at in range(0, rows, part):
+            local_at = pl.multiple_of((k ^ within) * rows + at, part)
+            column = pl.multiple_of(group * NORM_WIDTH + local_at, part)
+            carried = lax.dot_general(
+                c, piece[at : at + part, :], (((1,), (1,)), ((), ())), preferred_element_type=jnp.float32
+            )
+            value = intra[:, pl.ds(column, part)] + carry[:, pl.ds(column, part)] * carried
+            total = total + jnp.sum(value * value, axis=1, keepdims=True)
+            index = len(places)
+            wide[:, index * part : (index + 1) * part] = value
+            places.append(column)
+    scale = jnp.where(keep, lax.rsqrt(total * (1.0 / NORM_WIDTH) + EPSILON), 0.0)
     copies = []
-    for k, piece in enumerate(pieces):
-        slot = turn_ref[0] ^ k
-        copy = pltpu.make_async_copy(piece, state.at[slot], sems.at[k])
+    for index, column in enumerate(places):
+        lanes = slice(index * part, (index + 1) * part)
+        normed = wide[:, lanes] * scale * gain[:, pl.ds(column, part)]
+        narrow[:, lanes] = jnp.where(keep, normed, 0.0).astype(jnp.bfloat16)
+        copy = pltpu.make_async_copy(narrow.at[:, lanes], out.at[:, pl.ds(column, part)], sems.at[index])
         copy.start()
         copies.append(copy)
     for copy in copies:
         copy.wait()
-    tokens, inner = intra.shape
-    groups = c_proj.shape[1] // STATE
-    rows = state.shape[1]
-    width = inner // groups
-    norms = width // NORM_WIDTH
-    keep = lax.broadcasted_iota(jnp.int32, (tokens, 1), 0) < span_ref[0]
-    chunk = min(rows, 512)
-    for n in range(inner // NORM_WIDTH):
-        g = n // norms
-        c = c_proj[:, g * STATE : (g + 1) * STATE]
-        gated = []
-        total = jnp.zeros((tokens, 1), jnp.float32)
-        for at in range(n * NORM_WIDTH, (n + 1) * NORM_WIDTH, chunk):
-            part = state[at // rows, at % rows : at % rows + chunk, :]
-            carried = lax.dot_general(
-                c, part, (((1,), (1,)), ((), ())), preferred_element_type=jnp.float32
-            )
-            lanes = slice(at, at + chunk)
-            value = intra[:, lanes] + carry[:, lanes] * carried
-            total = total + jnp.sum(value * value, axis=1, keepdims=True)
-            gated.append((lanes, value))
-        scale = lax.rsqrt(total * (1.0 / NORM_WIDTH) + EPSILON)
-        for lanes, value in gated:
-            normed = value * scale * gain[:, lanes]
-            out[:, lanes] = jnp.where(keep, normed, 0.0).astype(jnp.bfloat16)
-
-
-def tail_stage(turn, span_len, pieces, intra, carry, c_proj, gain):
-    rows = pieces[0].shape[0]
+
+
+def tail_stage(base, turn, span_len, pieces, intra, carry, c_proj, gain, before=None):
+    tokens, _ = intra.shape
     vmem = pl.BlockSpec(memory_space=pltpu.VMEM)
+    whole = pl.BlockSpec(memory_space=pltpu.HBM)
+    earlier = [] if before is None else [before]
+    parts = NORM_WIDTH // min(pieces[0].shape[0], 512)
     grid_spec = pltpu.PrefetchScalarGridSpec(
         num_scalar_prefetch=2,
         grid=(),
-        in_specs=[pl.BlockSpec(memory_space=pl.ANY)] * len(pieces) + [vmem] * 4,
-        out_specs=vmem,
+        in_specs=[vmem] * (len(pieces) + 4) + [whole] * len(earlier),
+        out_specs=whole,
         scratch_shapes=[
-            pltpu.VMEM((len(pieces), rows, STATE), jnp.bfloat16),
-            pltpu.SemaphoreType.DMA((len(pieces),)),
+            pltpu.VMEM((tokens, NORM_WIDTH), jnp.float32),
+            pltpu.VMEM((tokens, NORM_WIDTH), jnp.bfloat16),
+            pltpu.SemaphoreType.DMA((parts,)),
         ],
     )
     return pl.pallas_call(
-        functools.partial(tail_kernel, len(pieces)),
+        functools.partial(tail_kernel, base, len(earlier)),
         grid_spec=grid_spec,
         out_shape=jax.ShapeDtypeStruct(intra.shape, jnp.bfloat16),
-        compiler_params=pltpu.CompilerParams(vmem_limit_bytes=24 << 20),
-        cost_estimate=pl.CostEstimate(flops=140_000_000, bytes_accessed=6_000_000, transcendentals=0),
-        name="tail_stage",
-    )(turn, span_len, *pieces, intra, carry, c_proj, gain)
+        input_output_aliases={2 + len(pieces) + 4: 0} if earlier else {},
+        compiler_params=pltpu.CompilerParams(vmem_limit_bytes=16 << 20),
+        cost_estimate=pl.CostEstimate(flops=70_000_000, bytes_accessed=3_000_000, transcendentals=0),
+    )(turn, span_len, *pieces, intra, carry, c_proj, gain, *earlier)
 
 
 def cut_kernel(chosen, state, *refs):
@@ -283,20 +292,20 @@
 def cut_stage(state, chosen):
     return pl.pallas_call(
         functools.partial(cut_kernel, chosen),
-        in_specs=[pl.BlockSpec(memory_space=pl.ANY)],
+        in_specs=[pl.BlockSpec(memory_space=pltpu.HBM)],
         out_specs=[pl.BlockSpec(memory_space=pltpu.VMEM)] * len(chosen),
-        out_shape=[jax.ShapeDtypeStruct(state.shape[1:], state.dtype)] * len(chosen),
+        out_shape=[pltpu.VMEM(state.shape[1:], state.dtype)] * len(chosen),
         scratch_shapes=[pltpu.SemaphoreType.DMA((len(chosen),))],
         compiler_params=pltpu.CompilerParams(vmem_limit_bytes=8 << 20),
         name="cut_stage",
-    )(state)
-
-
-def pick_kernel(order, me_ref, source_ref, *refs):
+    )(*keep_in(pltpu.HBM, state))
+
+
+def pick_kernel(order, me_ref, turned_ref, *refs):
     count = len(order)
     held, slots = refs[:count], refs[count:]
     for slot, k in zip(slots, order):
-        wanted = me_ref[0] ^ source_ref[me_ref[0] ^ k]
+        wanted = turned_ref[me_ref[0] ^ k]
         for r in range(count):
 
             @pl.when(wanted == r)
@@ -304,7 +313,7 @@
                 slot[...] = held[r][...]
 
 
-def pick_stage(me, source_of, held, order):
+def pick_stage(me, turned, held, order):
     vmem = pl.BlockSpec(memory_space=pltpu.VMEM)
     grid_spec = pltpu.PrefetchScalarGridSpec(
         num_scalar_prefetch=2,
@@ -312,14 +321,14 @@
         in_specs=[vmem] * len(held),
         out_specs=[vmem] * len(order),
     )
-    shape = jax.ShapeDtypeStruct(held[0].shape, held[0].dtype)
+    shape = pltpu.VMEM(held[0].shape, held[0].dtype)
     return pl.pallas_call(
         functools.partial(pick_kernel, tuple(order)),
         grid_spec=grid_spec,
         out_shape=[shape] * len(order),
         compiler_params=pltpu.CompilerParams(vmem_limit_bytes=8 << 20),
         name="pick_stage",
-    )(me, source_of, *held)
+    )(me, turned, *keep_in(pltpu.VMEM, *held))
 
 
 def gather_rims(conv_store, source_of, me):
@@ -363,11 +372,9 @@
     rims = gather_rims(conv_store, source_of, me)
     if direct:
         held = [None] * owners
-        far = [k for k in order if 2 * k >= owners]
-        near = [k for k in order if 2 * k < owners]
-        for some in (far, near + [0]):
-            for k, piece in zip(some, cut_stage(state, some)):
-                held[k] = swap(piece, "dp", k) if k else piece
+        every = order + [0]
+        for k, piece in zip(every, cut_stage(state, every)):
+            held[k] = swap(piece, "dp", k) if k else piece
     else:
         held = lax.all_to_all(state, "dp", split_axis=0, concat_axis=0, tiled=True)
 
@@ -394,24 +401,24 @@
     if direct:
         got = [None] * owners
         slots = order + [0]
-        picked = pick_stage(me.astype(jnp.int32).reshape(1), source_of, held, slots)
+        picked = pick_stage(me.astype(jnp.int32).reshape(1), source_of ^ me, held, slots)
         for k, piece in zip(slots, picked):
             got[k] = swap(piece, "dp", k) if k else piece
         turn = source_of[me] ^ me
     else:
         picked = jnp.take(held, source_of, axis=0)
         arrived = lax.all_to_all(picked, "dp", split_axis=0, concat_axis=0, tiled=True)
-        got = [arrived.reshape(-1, STATE)]
+        got = list(arrived.reshape(-1, NORM_WIDTH, STATE))
         turn = jnp.zeros((), jnp.int32)
-    return tail_stage(
-        turn.astype(jnp.int32).reshape(1),
-        span_len,
-        got,
-        intra,
-        carry,
-        c_proj,
-        norm_gain.reshape(1, -1),
-    )
+    turn = turn.astype(jnp.int32).reshape(1)
+    gain = norm_gain.reshape(1, -1)
+    mixed = None
+    norms = norm_gain.shape[0] // NORM_WIDTH
+    share = len(got) // norms
+    for base in range(norms):
+        mine = got[base * share : (base + 1) * share]
+        mixed = tail_stage(base, turn, span_len, mine, intra, carry, c_proj, gain, mixed)
+    return mixed
 
 
 def solution(mesh):

time: 88.2 us -> 74.4 us (0.84)
  local copies, waits for them, and re-layouts: 14 us -> 1.36 us
  starting transfers between devices: 25.3 us -> 31.6 us
  waiting for transfers between devices: 27.4 us -> 23.5 us
  Pallas kernels: 15.3 us -> 13.5 us
  other arithmetic: 3.23 us -> 1.69 us
    unnamed x44 -> x18, local copies, waits for them, and re-layouts: 12.8 us -> 0.04 us
    ppermute x20, starting transfers between devices: 25.3 us -> 31.6 us  [swap(): return lax.ppermute(value, axis, [(i, i ^ offset) for i in range(count)])]
    ppermute x20, waiting for transfers between devices: 27.4 us -> 23.5 us  [swap(): return lax.ppermute(value, axis, [(i, i ^ offset) for i in range(count)])]
    concatenate x2, other arithmetic: 2.45 us -> 0.93 us  [gather_rims(): held = jnp.concatenate([held, other], axis=0)]
    pallas_call x1, Pallas kernels: 1.88 us -> 0.95 us  [pick_stage(): pl.pallas_call(functools.partial(pick_kernel, tuple(order)), grid_spec=gr...]
    pallas_call x2 -> x1, Pallas kernels: 2.1 us -> 1.44 us  [cut_stage(): pl.pallas_call(functools.partial(cut_kernel, chosen), in_specs=[pl.BlockS...]
    pallas_call x1 -> x2, Pallas kernels: 3.22 us -> 2.64 us  [tail_stage(): pl.pallas_call(functools.partial(tail_kernel, base, len(earlier)), grid_s...]
  transfers between devices with their start and end apart: 20 -> 20, of which waited for: 5 -> 7; matrix products, arithmetic and copies ran while one was open for 5% -> 4% of each run, Pallas kernels for 13% -> 15%
where the time goes in v1:
time: 74.4 us; the launch traced here: 73.8 us
  starting transfers between devices  31.6 us (42%)
  waiting for transfers between devices  23.5 us (32%)
  Pallas kernels  13.5 us (18%)
  between operations  2.22 us (3%)
  other arithmetic  1.69 us (2%)
  local copies, waits for them, and re-layouts  1.36 us (2%)
    ppermute x20, starting transfers between devices, swap(): return lax.ppermute(value, axis, [(i, i ^ offset) for i in range(count)])  31.6 us
    ppermute x20, waiting for transfers between devices, swap(): return lax.ppermute(value, axis, [(i, i ^ offset) for i in range(count)])  23.5 us
    pallas_call x1, Pallas kernels, main_stage(): pl.pallas_call(main_kernel, grid_spec=grid_spec, out_shape=[jax.ShapeDtyp...  8.44 us
    pallas_call x2, Pallas kernels, tail_stage(): pl.pallas_call(functools.partial(tail_kernel, base, len(earlier)), grid_s...  2.64 us
  transfers between devices with their start and end apart: 20, of which 7 were waited for; matrix products, arithmetic and copies ran while one was open for 4% of the time, Pallas kernels for 15%

profile of v1, /device:TPU:0, one launch (start us, length us, event | category | flops | bytes accessed | tf_op | source)
XLA Modules:
  0.0 73.8 jit_solution(10468815940598053435)
XLA Ops:
  0.0 1.4 %cut_stage.1 = (bf16[512,128]{1,0:T(8,128)(2,1)S(1)}, bf16[512,128]{1,0:T(8,128)(2,1)S(1)}, bf16[512,128]{1,0:T(8,128)(2,1)S(1)}, bf16[512,128]{1,0:T(8,128)(2,1...) custom-call(bf16[8,512,128]{2,1,0:T(8,128)(2,1)} %bitcast.15), custom_call_target="tpu_custom_call" | custom-call | tf_op jit(solution)/shard_map/cut_stage/pallas_call | solution.py:293
  1.5 3.0 %collective-permute-start = (bf16[512,128]{1,0:T(8,128)(2,1)S(1)}, bf16[512,128]{1,0:T(8,128)(2,1)S(1)}, u32[]{:S(2)}, u32[]{:S(2)}) collective-permute-start(bf16[512,128]{1,0:T(8,128)(2,1)S(1)} %get-tuple-element.25), channel_id=1, source_target_pairs={{0,2},{2,0},{4,6},{6,4},{8,10},{10,8},{12,14},{14,12},{1,3},{3,1},... | collective-permute-start | bytes 393224 | tf_op jit(solution)/shard_map/ppermute | solution.py:21
  4.5 1.6 %collective-permute-start.1 = (bf16[512,128]{1,0:T(8,128)(2,1)S(1)}, bf16[512,128]{1,0:T(8,128)(2,1)S(1)}, u32[]{:S(2)}, u32[]{:S(2)}) collective-permute-start(bf16[512,128]{1,0:T(8,128)(2,1)S(1)} %get-tuple-element.26), channel_id=1, source_target_pairs={{0,4},{2,6},{4,0},{6,2},{8,12},{10,14},{12,8},{14,10},{1,5},{3,7},... | collective-permute-start | bytes 393224 | tf_op jit(solution)/shard_map/ppermute | solution.py:21
  6.1 2.6 %collective-permute-start.12 = (bf16[1,3,4608]{2,1,0:T(4,128)(2,1)}, bf16[1,3,4608]{2,1,0:T(4,128)(2,1)S(1)}, u32[]{:S(2)}, u32[]{:S(2)}) collective-permute-start(bf16[1,3,4608]{2,1,0:T(4,128)(2,1)} %param.24), channel_id=1, source_target_pairs={{0,8},{2,10},{4,12},{6,14},{8,0},{10,2},{12,4},{14,6},{1,9},{3,11}... | collective-permute-start | bytes 82952 | tf_op jit(solution)/shard_map/ppermute | solution.py:21
  8.7 0.0 collective-permute-start.11
  8.7 0.5 collective-permute-start.15
  9.2 2.0 %collective-permute-done.12 = bf16[1,3,4608]{2,1,0:T(4,128)(2,1)S(1)} collective-permute-done((bf16[1,3,4608]{2,1,0:T(4,128)(2,1)}, bf16[1,3,4608]{2,1,0:T(4,128)(2,1)S(1)}, u32[]{:S(2)}, u32[]{:S(2)}) %collective-permute-start.12) | collective-permute-done | bytes 27680 | tf_op jit(solution)/shard_map/ppermute | solution.py:21
  11.2 1.6 %collective-permute-start.2 = (bf16[512,128]{1,0:T(8,128)(2,1)S(1)}, bf16[512,128]{1,0:T(8,128)(2,1)S(1)}, u32[]{:S(2)}, u32[]{:S(2)}) collective-permute-start(bf16[512,128]{1,0:T(8,128)(2,1)S(1)} %get-tuple-element.27), channel_id=1, source_target_pairs={{0,6},{2,4},{4,2},{6,0},{8,14},{10,12},{12,10},{14,8},{1,7},{3,5},... | collective-permute-start | bytes 393224 | tf_op jit(solution)/shard_map/ppermute | solution.py:21
  12.8 0.0 collective-permute-done.refs_1_
  12.8 1.5 %collective-permute-start.3 = (bf16[512,128]{1,0:T(8,128)(2,1)S(1)}, bf16[512,128]{1,0:T(8,128)(2,1)S(1)}, u32[]{:S(2)}, u32[]{:S(2)}) collective-permute-start(bf16[512,128]{1,0:T(8,128)(2,1)S(1)} %get-tuple-element.28), channel_id=1, source_target_pairs={{0,8},{2,10},{4,12},{6,14},{8,0},{10,2},{12,4},{14,6},{1,9},{3,11}... | collective-permute-start | bytes 393224 | tf_op jit(solution)/shard_map/ppermute | solution.py:21
  14.3 0.0 collective-permute-done.1.refs_2_
  14.3 2.4 %collective-permute-start.4 = (bf16[512,128]{1,0:T(8,128)(2,1)S(1)}, bf16[512,128]{1,0:T(8,128)(2,1)S(1)}, u32[]{:S(2)}, u32[]{:S(2)}) collective-permute-start(bf16[512,128]{1,0:T(8,128)(2,1)S(1)} %get-tuple-element.29), channel_id=1, source_target_pairs={{0,10},{2,8},{4,14},{6,12},{8,2},{10,0},{12,6},{14,4},{1,11},{3,9}... | collective-permute-start | bytes 393224 | tf_op jit(solution)/shard_map/ppermute | solution.py:21
  16.7 0.8 %pad_maximum_fusion.1 = bf16[2,3,4608]{2,1,0:T(4,128)(2,1)S(1)} fusion(bf16[1,3,4608]{2,1,0:T(4,128)(2,1)S(1)} %collective-permute-done.12, bf16[1,3,4608]{2,1,0:T(4,128)(2,1)} %param.24), kind=kLoop, calls=%fused_computation.5 | loop fusion | flops 27648 | bytes 110592 | tf_op jit(solution)/shard_map/concatenate | solution.py:343
  17.5 0.8 %collective-permute-done.2.refs_3_ = bf16[512,128]{1,0:T(8,128)(2,1)S(1)} collective-permute-done((bf16[512,128]{1,0:T(8,128)(2,1)S(1)}, bf16[512,128]{1,0:T(8,128)(2,1)S(1)}, u32[]{:S(2)}, u32[]{:S(2)}) %collective-permute-start.2) | collective-permute-done | bytes 131104 | tf_op jit(solution)/shard_map/ppermute | solution.py:21
  18.3 1.7 %collective-permute-start.5 = (bf16[512,128]{1,0:T(8,128)(2,1)S(1)}, bf16[512,128]{1,0:T(8,128)(2,1)S(1)}, u32[]{:S(2)}, u32[]{:S(2)}) collective-permute-start(bf16[512,128]{1,0:T(8,128)(2,1)S(1)} %get-tuple-element.30), channel_id=1, source_target_pairs={{0,12},{2,14},{4,8},{6,10},{8,4},{10,6},{12,0},{14,2},{1,13},{3,15... | collective-permute-start | bytes 393224 | tf_op jit(solution)/shard_map/ppermute | solution.py:21
  20.0 7.1 %collective-permute-done.3.refs_4_ = bf16[512,128]{1,0:T(8,128)(2,1)S(1)} collective-permute-done((bf16[512,128]{1,0:T(8,128)(2,1)S(1)}, bf16[512,128]{1,0:T(8,128)(2,1)S(1)}, u32[]{:S(2)}, u32[]{:S(2)}) %collective-permute-start.3) | collective-permute-done | bytes 131104 | tf_op jit(solution)/shard_map/ppermute | solution.py:21
  27.1 2.8 %collective-permute-start.6 = (bf16[512,128]{1,0:T(8,128)(2,1)S(1)}, bf16[512,128]{1,0:T(8,128)(2,1)S(1)}, u32[]{:S(2)}, u32[]{:S(2)}) collective-permute-start(bf16[512,128]{1,0:T(8,128)(2,1)S(1)} %get-tuple-element.31), channel_id=1, source_target_pairs={{0,14},{2,12},{4,10},{6,8},{8,6},{10,4},{12,2},{14,0},{1,15},{3,13... | collective-permute-start | bytes 393224 | tf_op jit(solution)/shard_map/ppermute | solution.py:21
  30.0 2.3 %collective-permute-done.4.refs_5_ = bf16[512,128]{1,0:T(8,128)(2,1)S(1)} collective-permute-done((bf16[512,128]{1,0:T(8,128)(2,1)S(1)}, bf16[512,128]{1,0:T(8,128)(2,1)S(1)}, u32[]{:S(2)}, u32[]{:S(2)}) %collective-permute-start.4) | collective-permute-done | bytes 131104 | tf_op jit(solution)/shard_map/ppermute | solution.py:21
  32.3 0.0 collective-permute-start.13
  32.3 0.7 broadcast_xor_fusion.turned_ref
  32.9 1.3 %dynamic_slice.8 = s32[1]{0:T(128)} dynamic-slice(s32[8]{0:T(128)} %param.25, s32[]{:T(128)S(6)} %select_n.17), dynamic_slice_sizes={1} | dynamic-slice | bytes 12 | tf_op jit(solution)/shard_map/dynamic_slice | solution.py:407
  36.3 0.0 collective-permute-done.5.refs_6_
  36.3 0.1 collective-permute-start.16
  36.4 0.0 collective-permute-done.6.refs_7_
  36.4 1.0 %pick_stage.1 = (bf16[512,128]{1,0:T(8,128)(2,1)S(1)}, bf16[512,128]{1,0:T(8,128)(2,1)S(1)}, bf16[512,128]{1,0:T(8,128)(2,1)S(1)}, bf16[512,128]{1,0:T(8,128)(2,...) custom-call(s32[1]{0:T(128)} %bitcast.2.me_ref, ...), custom_call_target="tpu_custom_call" | custom-call | tf_op jit(solution)/shard_map/pick_stage/pallas_call | solution.py:325
  37.4 0.6 collective-permute-start.17
  38.0 0.0 collective-permute-done.13
  38.0 2.0 %collective-permute-start.18 = (bf16[512,128]{1,0:T(8,128)(2,1)S(1)}, bf16[512,128]{1,0:T(8,128)(2,1)S(1)}, u32[]{:S(2)}, u32[]{:S(2)}) collective-permute-start(bf16[512,128]{1,0:T(8,128)(2,1)S(1)} %get-tuple-element.41), channel_id=1, source_target_pairs={{0,4},{2,6},{4,0},{6,2},{8,12},{10,14},{12,8},{14,10},{1,5},{3,7},... | collective-permute-start | bytes 393224 | tf_op jit(solution)/shard_map/ppermute | solution.py:21
  40.0 0.1 pad_maximum_fusion
  40.1 0.0 collective-permute-done.16.peer_dt
  40.1 1.6 %collective-permute-start.14 = (bf16[4,3,4608]{2,1,0:T(4,128)(2,1)S(1)}, bf16[4,3,4608]{2,1,0:T(4,128)(2,1)S(1)}, u32[]{:S(2)}, u32[]{:S(2)}) collective-permute-start(bf16[4,3,4608]{2,1,0:T(4,128)(2,1)S(1)} %pad_maximum_fusion), channel_id=1, source_target_pairs={{0,2},{2,0},{4,6},{6,4},{8,10},{10,8},{12,14},{14,12},{1,3},{3,1},... | collective-permute-start | bytes 331784 | tf_op jit(solution)/shard_map/ppermute | solution.py:21
  41.7 4.8 %collective-permute-done.14 = bf16[4,3,4608]{2,1,0:T(4,128)(2,1)S(1)} collective-permute-done((bf16[4,3,4608]{2,1,0:T(4,128)(2,1)S(1)}, bf16[4,3,4608]{2,1,0:T(4,128)(2,1)S(1)}, u32[]{:S(2)}, u32[]{:S(2)}) %collective-permute-start.14) | collective-permute-done | bytes 110624 | tf_op jit(solution)/shard_map/ppermute | solution.py:21
  46.5 2.0 %collective-permute-start.19 = (bf16[512,128]{1,0:T(8,128)(2,1)S(1)}, bf16[512,128]{1,0:T(8,128)(2,1)S(1)}, u32[]{:S(2)}, u32[]{:S(2)}) collective-permute-start(bf16[512,128]{1,0:T(8,128)(2,1)S(1)} %get-tuple-element.42), channel_id=1, source_target_pairs={{0,6},{2,4},{4,2},{6,0},{8,14},{10,12},{12,10},{14,8},{1,7},{3,5},... | collective-permute-start | bytes 393224 | tf_op jit(solution)/shard_map/ppermute | solution.py:21
  48.5 0.0 collective-permute-done.17.refs_1_
  48.5 2.8 %collective-permute-start.10 = (bf16[512,128]{1,0:T(8,128)(2,1)S(1)}, bf16[512,128]{1,0:T(8,128)(2,1)S(1)}, u32[]{:S(2)}, u32[]{:S(2)}) collective-permute-start(bf16[512,128]{1,0:T(8,128)(2,1)S(1)} %get-tuple-element.35), channel_id=1, source_target_pairs={{0,14},{2,12},{4,10},{6,8},{8,6},{10,4},{12,2},{14,0},{1,15},{3,13... | collective-permute-start | bytes 393224 | tf_op jit(solution)/shard_map/ppermute | solution.py:21
  51.3 0.0 collective-permute-done.18.refs_2_
  51.3 0.0 collective-permute-start.7
  51.3 0.0 collective-permute-done.15.peer_gate
  51.3 2.6 %collective-permute-start.8 = (bf16[512,128]{1,0:T(8,128)(2,1)S(1)}, bf16[512,128]{1,0:T(8,128)(2,1)S(1)}, u32[]{:S(2)}, u32[]{:S(2)}) collective-permute-start(bf16[512,128]{1,0:T(8,128)(2,1)S(1)} %get-tuple-element.33), channel_id=1, source_target_pairs={{0,10},{2,8},{4,14},{6,12},{8,2},{10,0},{12,6},{14,4},{1,11},{3,9}... | collective-permute-start | bytes 393224 | tf_op jit(solution)/shard_map/ppermute | solution.py:21
  53.9 0.0 collective-permute-done.11.peer_x.peer_bc
  53.9 2.2 %collective-permute-start.9 = (bf16[512,128]{1,0:T(8,128)(2,1)S(1)}, bf16[512,128]{1,0:T(8,128)(2,1)S(1)}, u32[]{:S(2)}, u32[]{:S(2)}) collective-permute-start(bf16[512,128]{1,0:T(8,128)(2,1)S(1)} %get-tuple-element.34), channel_id=1, source_target_pairs={{0,12},{2,14},{4,8},{6,10},{8,4},{10,6},{12,0},{14,2},{1,13},{3,15... | collective-permute-start | bytes 393224 | tf_op jit(solution)/shard_map/ppermute | solution.py:21
  56.1 0.1 fusion.3.rims_x.rims_bc
  56.3 0.0 copy-start.2
  56.3 8.4 %main_stage.1 = (f32[128,4096]{1,0:T(8,128)S(1)}, f32[128,4096]{1,0:T(8,128)S(1)}, bf16[128,256]{1,0:T(8,128)(2,1)S(1)}) custom-call(s32[1]{0:T(128)} %bitcast.4.core_ref, s32[1]{0:T(128)S(6)} %copy.17.live_ref, f32[64]{0:T(128)S(1)} %copy-done.4, bf16[64,9216]{1,0:T(8,128)(2,1)} %own_bc.1, bf16[64,9216]{1,0:T(8,128)(2,1)} %copy-done.5, ...), custom_call_target="tpu_custom_call" | custom-call | flops 400000000 | bytes 8000000 | tf_op jit(solution)/shard_map/main_stage/pallas_call | solution.py:202
  64.8 1.3 %shard_map.136.refs_8_ = bf16[128,4096]{1,0:T(8,128)(2,1)} custom-call(s32[1]{0:T(128)} %bitcast.1.turn_ref, s32[1]{0:T(128)S(6)} %copy.18.span_ref, bf16[512,128]{1,0:T(8,128)(2,1)S(1)} %get-tuple-element.39.refs_0_, bf16[512,128]{1,0:T(8,128)(2,1)S(1)} %collective-permute-done.17.refs_1_, bf16[512,128]{1,0:T(8,128)(2,1)S(1)} %collective-permute-done.18.refs_2_, ...), custom_call_target="tpu_custom_call" | custom-call | flops 70000000 | bytes 3000000 | tf_op jit(solution)/shard_map/pallas_call | solution.py:271
  66.1 3.2 %collective-permute-done.7.refs_0_ = bf16[512,128]{1,0:T(8,128)(2,1)S(1)} collective-permute-done((bf16[512,128]{1,0:T(8,128)(2,1)S(1)}, bf16[512,128]{1,0:T(8,128)(2,1)S(1)}, u32[]{:S(2)}, u32[]{:S(2)}) %collective-permute-start.7) | collective-permute-done | bytes 131104 | tf_op jit(solution)/shard_map/ppermute | solution.py:21
  69.3 3.2 %collective-permute-done.8.refs_1_ = bf16[512,128]{1,0:T(8,128)(2,1)S(1)} collective-permute-done((bf16[512,128]{1,0:T(8,128)(2,1)S(1)}, bf16[512,128]{1,0:T(8,128)(2,1)S(1)}, u32[]{:S(2)}, u32[]{:S(2)}) %collective-permute-start.8) | collective-permute-done | bytes 131104 | tf_op jit(solution)/shard_map/ppermute | solution.py:21
  72.5 1.3 %shard_map.137 = bf16[128,4096]{1,0:T(8,128)(2,1)} custom-call(s32[1]{0:T(128)} %bitcast.1.turn_ref, s32[1]{0:T(128)S(6)} %copy.18.span_ref, bf16[512,128]{1,0:T(8,128)(2,1)S(1)} %collective-permute-done.7.refs_0_, bf16[512,128]{1,0:T(8,128)(2,1)S(1)} %collective-permute-done.8.refs_1_, ...), custom_call_target="tpu_custom_call", output_to_operand_aliasing={{}: (10, {})} | custom-call | flops 70000000 | bytes 3000000 | tf_op jit(solution)/shard_map/pallas_call | solution.py:271
  (21 shorter events, 0.1 us)
Async XLA Ops:
  0.0 40.0 %copy-start.6 = (bf16[1,3,4608]{2,1,0:T(4,128)(2,1)S(1)}, bf16[1,3,4608]{2,1,0:T(4,128)(2,1)}, u32[]{:S(2)}) copy-start(bf16[1,3,4608]{2,1,0:T(4,128)(2,1)} %param.24) | copy-start | bytes 82948
  0.0 56.2 %copy-start.3 = (bf16[64,128]{1,0:T(8,128)(2,1)S(1)}, bf16[64,128]{1,0:T(8,128)(2,1)}, u32[]{:S(2)}) copy-start(bf16[64,128]{1,0:T(8,128)(2,1)} %own_dt.1) | copy-start | bytes 49156
  0.0 41.7 %copy-start.8 = (f32[64]{0:T(128)S(1)}, f32[64]{0:T(128)}, u32[]{:S(2)}) copy-start(f32[64]{0:T(128)} %param.19) | copy-start | bytes 772
  0.0 41.7 %copy-start.7 = (f32[64]{0:T(128)S(1)}, f32[64]{0:T(128)}, u32[]{:S(2)}) copy-start(f32[64]{0:T(128)} %param.20) | copy-start | bytes 772
  0.0 56.2 %copy-start.1 = (f32[9216]{0:T(1024)S(1)}, f32[9216]{0:T(1024)}, u32[]{:S(2)}) copy-start(f32[9216]{0:T(1024)} %param.18) | copy-start | bytes 110596
  0.0 56.2 %copy-start = (f32[4,9216]{1,0:T(4,128)S(1)}, f32[4,9216]{1,0:T(4,128)}, u32[]{:S(2)}) copy-start(f32[4,9216]{1,0:T(4,128)} %weight_bc.1) | copy-start | bytes 442372
  0.0 56.2 %copy-start.4 = (f32[64]{0:T(128)S(1)}, f32[64]{0:T(128)}, u32[]{:S(2)}) copy-start(f32[64]{0:T(128)} %skip_ref.1) | copy-start | bytes 772
  1.5 11.4 %collective-permute-start = (bf16[512,128]{1,0:T(8,128)(2,1)S(1)}, bf16[512,128]{1,0:T(8,128)(2,1)S(1)}, u32[]{:S(2)}, u32[]{:S(2)}) collective-permute-start(bf16[512,128]{1,0:T(8,128)(2,1)S(1)} %get-tuple-element.25), channel_id=1, source_target_pairs={{0,2},{2,0},{4,6},{6,4},{8,10},{10,8},{12,14},{14,12},{1,3},{3,1},... | collective-permute-start | bytes 393224 | tf_op jit(solution)/shard_map/ppermute | solution.py:21
  4.5 9.8 %collective-permute-start.1 = (bf16[512,128]{1,0:T(8,128)(2,1)S(1)}, bf16[512,128]{1,0:T(8,128)(2,1)S(1)}, u32[]{:S(2)}, u32[]{:S(2)}) collective-permute-start(bf16[512,128]{1,0:T(8,128)(2,1)S(1)} %get-tuple-element.26), channel_id=1, source_target_pairs={{0,4},{2,6},{4,0},{6,2},{8,12},{10,14},{12,8},{14,10},{1,5},{3,7},... | collective-permute-start | bytes 393224 | tf_op jit(solution)/shard_map/ppermute | solution.py:21
  6.1 5.1 %collective-permute-start.12 = (bf16[1,3,4608]{2,1,0:T(4,128)(2,1)}, bf16[1,3,4608]{2,1,0:T(4,128)(2,1)S(1)}, u32[]{:S(2)}, u32[]{:S(2)}) collective-permute-start(bf16[1,3,4608]{2,1,0:T(4,128)(2,1)} %param.24), channel_id=1, source_target_pairs={{0,8},{2,10},{4,12},{6,14},{8,0},{10,2},{12,4},{14,6},{1,9},{3,11}... | collective-permute-start | bytes 82952 | tf_op jit(solution)/shard_map/ppermute | solution.py:21
  8.7 45.3 %collective-permute-start.11 = (bf16[64,9216]{1,0:T(8,128)(2,1)}, bf16[64,9216]{1,0:T(8,128)(2,1)S(1)}, u32[]{:S(2)}, u32[]{:S(2)}) collective-permute-start(bf16[64,9216]{1,0:T(8,128)(2,1)} %own_bc.1), channel_id=1, source_target_pairs={{0,1},{1,0},{2,3},{3,2},{4,5},{5,4},{6,7},{7,6},{8,9},{9,8},{10,11... | collective-permute-start | bytes 3538952 | tf_op jit(solution)/shard_map/ppermute | solution.py:21
  8.7 42.6 %collective-permute-start.15 = (bf16[64,8192]{1,0:T(8,128)(2,1)}, bf16[64,8192]{1,0:T(8,128)(2,1)}, u32[]{:S(2)}, u32[]{:S(2)}) collective-permute-start(bf16[64,8192]{1,0:T(8,128)(2,1)} %own_gate.1), channel_id=1, source_target_pairs={{0,1},{1,0},{2,3},{3,2},{4,5},{5,4},{6,7},{7,6},{8,9},{9,8},{10,11... | collective-permute-start | bytes 3145736 | tf_op jit(solution)/shard_map/ppermute | solution.py:21
  11.2 7.1 %collective-permute-start.2 = (bf16[512,128]{1,0:T(8,128)(2,1)S(1)}, bf16[512,128]{1,0:T(8,128)(2,1)S(1)}, u32[]{:S(2)}, u32[]{:S(2)}) collective-permute-start(bf16[512,128]{1,0:T(8,128)(2,1)S(1)} %get-tuple-element.27), channel_id=1, source_target_pairs={{0,6},{2,4},{4,2},{6,0},{8,14},{10,12},{12,10},{14,8},{1,7},{3,5},... | collective-permute-start | bytes 393224 | tf_op jit(solution)/shard_map/ppermute | solution.py:21
  12.8 14.3 %collective-permute-start.3 = (bf16[512,128]{1,0:T(8,128)(2,1)S(1)}, bf16[512,128]{1,0:T(8,128)(2,1)S(1)}, u32[]{:S(2)}, u32[]{:S(2)}) collective-permute-start(bf16[512,128]{1,0:T(8,128)(2,1)S(1)} %get-tuple-element.28), channel_id=1, source_target_pairs={{0,8},{2,10},{4,12},{6,14},{8,0},{10,2},{12,4},{14,6},{1,9},{3,11}... | collective-permute-start | bytes 393224 | tf_op jit(solution)/shard_map/ppermute | solution.py:21
  14.3 18.0 %collective-permute-start.4 = (bf16[512,128]{1,0:T(8,128)(2,1)S(1)}, bf16[512,128]{1,0:T(8,128)(2,1)S(1)}, u32[]{:S(2)}, u32[]{:S(2)}) collective-permute-start(bf16[512,128]{1,0:T(8,128)(2,1)S(1)} %get-tuple-element.29), channel_id=1, source_target_pairs={{0,10},{2,8},{4,14},{6,12},{8,2},{10,0},{12,6},{14,4},{1,11},{3,9}... | collective-permute-start | bytes 393224 | tf_op jit(solution)/shard_map/ppermute | solution.py:21
  18.3 18.0 %collective-permute-start.5 = (bf16[512,128]{1,0:T(8,128)(2,1)S(1)}, bf16[512,128]{1,0:T(8,128)(2,1)S(1)}, u32[]{:S(2)}, u32[]{:S(2)}) collective-permute-start(bf16[512,128]{1,0:T(8,128)(2,1)S(1)} %get-tuple-element.30), channel_id=1, source_target_pairs={{0,12},{2,14},{4,8},{6,10},{8,4},{10,6},{12,0},{14,2},{1,13},{3,15... | collective-permute-start | bytes 393224 | tf_op jit(solution)/shard_map/ppermute | solution.py:21
  27.1 9.2 %collective-permute-start.6 = (bf16[512,128]{1,0:T(8,128)(2,1)S(1)}, bf16[512,128]{1,0:T(8,128)(2,1)S(1)}, u32[]{:S(2)}, u32[]{:S(2)}) collective-permute-start(bf16[512,128]{1,0:T(8,128)(2,1)S(1)} %get-tuple-element.31), channel_id=1, source_target_pairs={{0,14},{2,12},{4,10},{6,8},{8,6},{10,4},{12,2},{14,0},{1,15},{3,13... | collective-permute-start | bytes 393224 | tf_op jit(solution)/shard_map/ppermute | solution.py:21
  32.3 5.7 %collective-permute-start.13 = (bf16[2,3,4608]{2,1,0:T(4,128)(2,1)S(1)}, bf16[2,3,4608]{2,1,0:T(4,128)(2,1)S(1)}, u32[]{:S(2)}, u32[]{:S(2)}) collective-permute-start(bf16[2,3,4608]{2,1,0:T(4,128)(2,1)S(1)} %pad_maximum_fusion.1), channel_id=1, source_target_pairs={{0,4},{2,6},{4,0},{6,2},{8,12},{10,14},{12,8},{14,10},{1,5},{3,7},... | collective-permute-start | bytes 165896 | tf_op jit(solution)/shard_map/ppermute | solution.py:21
  36.3 3.8 %collective-permute-start.16 = (bf16[64,128]{1,0:T(8,128)(2,1)}, bf16[64,128]{1,0:T(8,128)(2,1)S(1)}, u32[]{:S(2)}, u32[]{:S(2)}) collective-permute-start(bf16[64,128]{1,0:T(8,128)(2,1)} %own_dt.1), channel_id=1, source_target_pairs={{0,1},{1,0},{2,3},{3,2},{4,5},{5,4},{6,7},{7,6},{8,9},{9,8},{10,11... | collective-permute-start | bytes 49160 | tf_op jit(solution)/shard_map/ppermute | solution.py:21
  37.4 11.1 %collective-permute-start.17 = (bf16[512,128]{1,0:T(8,128)(2,1)S(1)}, bf16[512,128]{1,0:T(8,128)(2,1)S(1)}, u32[]{:S(2)}, u32[]{:S(2)}) collective-permute-start(bf16[512,128]{1,0:T(8,128)(2,1)S(1)} %get-tuple-element.40), channel_id=1, source_target_pairs={{0,2},{2,0},{4,6},{6,4},{8,10},{10,8},{12,14},{14,12},{1,3},{3,1},... | collective-permute-start | bytes 393224 | tf_op jit(solution)/shard_map/ppermute | solution.py:21
  38.0 13.3 %collective-permute-start.18 = (bf16[512,128]{1,0:T(8,128)(2,1)S(1)}, bf16[512,128]{1,0:T(8,128)(2,1)S(1)}, u32[]{:S(2)}, u32[]{:S(2)}) collective-permute-start(bf16[512,128]{1,0:T(8,128)(2,1)S(1)} %get-tuple-element.41), channel_id=1, source_target_pairs={{0,4},{2,6},{4,0},{6,2},{8,12},{10,14},{12,8},{14,10},{1,5},{3,7},... | collective-permute-start | bytes 393224 | tf_op jit(solution)/shard_map/ppermute | solution.py:21
  40.1 6.4 %collective-permute-start.14 = (bf16[4,3,4608]{2,1,0:T(4,128)(2,1)S(1)}, bf16[4,3,4608]{2,1,0:T(4,128)(2,1)S(1)}, u32[]{:S(2)}, u32[]{:S(2)}) collective-permute-start(bf16[4,3,4608]{2,1,0:T(4,128)(2,1)S(1)} %pad_maximum_fusion), channel_id=1, source_target_pairs={{0,2},{2,0},{4,6},{6,4},{8,10},{10,8},{12,14},{14,12},{1,3},{3,1},... | collective-permute-start | bytes 331784 | tf_op jit(solution)/shard_map/ppermute | solution.py:21
  46.5 18.3 %collective-permute-start.19 = (bf16[512,128]{1,0:T(8,128)(2,1)S(1)}, bf16[512,128]{1,0:T(8,128)(2,1)S(1)}, u32[]{:S(2)}, u32[]{:S(2)}) collective-permute-start(bf16[512,128]{1,0:T(8,128)(2,1)S(1)} %get-tuple-element.42), channel_id=1, source_target_pairs={{0,6},{2,4},{4,2},{6,0},{8,14},{10,12},{12,10},{14,8},{1,7},{3,5},... | collective-permute-start | bytes 393224 | tf_op jit(solution)/shard_map/ppermute | solution.py:21
  48.5 17.6 %collective-permute-start.10 = (bf16[512,128]{1,0:T(8,128)(2,1)S(1)}, bf16[512,128]{1,0:T(8,128)(2,1)S(1)}, u32[]{:S(2)}, u32[]{:S(2)}) collective-permute-start(bf16[512,128]{1,0:T(8,128)(2,1)S(1)} %get-tuple-element.35), channel_id=1, source_target_pairs={{0,14},{2,12},{4,10},{6,8},{8,6},{10,4},{12,2},{14,0},{1,15},{3,13... | collective-permute-start | bytes 393224 | tf_op jit(solution)/shard_map/ppermute | solution.py:21
  51.3 18.0 %collective-permute-start.7 = (bf16[512,128]{1,0:T(8,128)(2,1)S(1)}, bf16[512,128]{1,0:T(8,128)(2,1)S(1)}, u32[]{:S(2)}, u32[]{:S(2)}) collective-permute-start(bf16[512,128]{1,0:T(8,128)(2,1)S(1)} %get-tuple-element.32), channel_id=1, source_target_pairs={{0,8},{2,10},{4,12},{6,14},{8,0},{10,2},{12,4},{14,6},{1,9},{3,11}... | collective-permute-start | bytes 393224 | tf_op jit(solution)/shard_map/ppermute | solution.py:21
  51.3 21.2 %collective-permute-start.8 = (bf16[512,128]{1,0:T(8,128)(2,1)S(1)}, bf16[512,128]{1,0:T(8,128)(2,1)S(1)}, u32[]{:S(2)}, u32[]{:S(2)}) collective-permute-start(bf16[512,128]{1,0:T(8,128)(2,1)S(1)} %get-tuple-element.33), channel_id=1, source_target_pairs={{0,10},{2,8},{4,14},{6,12},{8,2},{10,0},{12,6},{14,4},{1,11},{3,9}... | collective-permute-start | bytes 393224 | tf_op jit(solution)/shard_map/ppermute | solution.py:21
  53.9 2.3 %copy-start.5 = (bf16[64,9216]{1,0:T(8,128)(2,1)}, bf16[64,9216]{1,0:T(8,128)(2,1)S(1)}, u32[]{:S(2)}) copy-start(bf16[64,9216]{1,0:T(8,128)(2,1)S(1)} %collective-permute-done.11.peer_x.peer_bc) | copy-start | bytes 3538948
  53.9 18.6 %collective-permute-start.9 = (bf16[512,128]{1,0:T(8,128)(2,1)S(1)}, bf16[512,128]{1,0:T(8,128)(2,1)S(1)}, u32[]{:S(2)}, u32[]{:S(2)}) collective-permute-start(bf16[512,128]{1,0:T(8,128)(2,1)S(1)} %get-tuple-element.34), channel_id=1, source_target_pairs={{0,12},{2,14},{4,8},{6,10},{8,4},{10,6},{12,0},{14,2},{1,13},{3,15... | collective-permute-start | bytes 393224 | tf_op jit(solution)/shard_map/ppermute | solution.py:21
  56.3 8.5 %copy-start.2 = (f32[4096]{0:T(1024)S(1)}, f32[4096]{0:T(1024)}, u32[]{:S(2)}) copy-start(f32[4096]{0:T(1024)} %param.22) | copy-start | bytes 49156

commit v2 on v1

v2 whole, which is shorter than its diff:
```python
import functools

import jax
import jax.numpy as jnp
from jax import lax
from jax.experimental import pallas as pl
from jax.experimental.pallas import tpu as pltpu
from jax.sharding import PartitionSpec as P


HEAD_DIM = 64
STATE = 128
NORM_WIDTH = 2048
EPSILON = 1e-05
LANES = 128
DIRECT_MAX = 8


def swap(value, axis, offset):
    count = lax.axis_size(axis)
    return lax.ppermute(value, axis, [(i, i ^ offset) for i in range(count)])


CORE, ME, PREFIX, SPAN, TURNED = 0, 1, 2, 3, 4


def silu(value):
    half = 0.5 * value
    return half + half * jnp.tanh(half)


def keep_in(space, *values):
    return [pltpu.with_memory_space_constraint(value, space) for value in values]


def offsets(count):
    return sorted(range(1, count), key=lambda k: (-(k.bit_length()), k))


def main_kernel(
    rims_count,
    plan,
    skip_ref,
    own_x,
    peer_x,
    own_bc,
    peer_bc,
    weight_x,
    weight_bc,
    bias_x,
    bias_bc,
    own_gate,
    peer_gate,
    own_dt,
    peer_dt,
    dt_bias,
    decay_rate,
    *refs,
):
    rims = refs[:rims_count]
    intra_out, carry_out, c_out, extended, gates, scores, columns, cum_rows, step_rows = refs[rims_count:]
    block = pl.program_id(0)
    half, width = own_x.shape
    count = 2 * half
    per_block = width // HEAD_DIM
    groups = c_out.shape[1] // STATE
    blocks = pl.num_programs(0)
    live = plan[PREFIX] > 0
    taps = weight_x.shape[0]
    pad = 8 - (taps - 1)
    mine = pl.multiple_of(plan[CORE] * half, half)
    theirs = pl.multiple_of(half - mine, half)

    def edges(at):
        lanes = pl.ds(pl.multiple_of(at * width, width), width)
        edge = rims[0][0, :, lanes]
        if rims_count > 1:
            away = plan[TURNED + plan[ME]]
            choice = jnp.where((away & 1) == 0, away // 2, rims_count - 1)
            for i in range(1, rims_count):
                edge = jnp.where(choice == i, rims[i][0, :, lanes], edge)
        edge = edge.astype(jnp.float32)
        return jnp.where(live, edge, jnp.zeros_like(edge))

    def convolve(own, peer, at, weight, bias):
        extended[pad:8, :] = edges(at)
        extended[pl.ds(8 + mine, half), :] = own[...].astype(jnp.float32)
        extended[pl.ds(8 + theirs, half), :] = peer[...].astype(jnp.float32)
        total = jnp.broadcast_to(bias[...], (count, width))
        for k in range(taps):
            total = total + weight[k : k + 1, :] * extended[pad + k : pad + k + count, :]
        return silu(total).astype(jnp.bfloat16)

    row = lax.broadcasted_iota(jnp.int32, (count, LANES), 0)
    lane = lax.broadcasted_iota(jnp.int32, (count, LANES), 1)

    @pl.when(block == 0)
    def _():
        active = convolve(own_bc, peer_bc, blocks, weight_bc, bias_bc)
        c_out[...] = active[:, groups * STATE :]
        for g in range(groups):
            b = active[:, g * STATE : (g + 1) * STATE]
            c = active[:, (groups + g) * STATE : (groups + g + 1) * STATE]
            product = lax.dot_general(
                c, b, (((1,), (1,)), ((), ())), preferred_element_type=jnp.float32
            )
            scores[g] = jnp.where(row >= lane, product, 0.0)
        extended[pl.ds(8 + mine, half), :LANES] = own_dt[...].astype(jnp.float32)
        extended[pl.ds(8 + theirs, half), :LANES] = peer_dt[...].astype(jnp.float32)
        raw = extended[8 : 8 + count, :LANES]
        raw = jnp.where(plan[CORE] == 0, raw, pltpu.roll(raw, LANES // 2, 1))
        spare = jnp.zeros((1, LANES - dt_bias.shape[1]), jnp.float32)
        step = jax.nn.softplus(raw + jnp.concatenate([dt_bias[...], spare], axis=1))
        total = -jnp.concatenate([decay_rate[...], spare], axis=1) * step
        shift = 1
        while shift < count:
            total = total + jnp.where(row >= shift, pltpu.roll(total, shift, 0), 0.0)
            shift *= 2
        cum_rows[...] = total.T
        step_rows[...] = step.T
        for i in range(columns.shape[0]):
            columns[i] = total[:, i * per_block : (i + 1) * per_block]

    active = convolve(own_x, peer_x, block, weight_x, bias_x)
    gates[pl.ds(mine, half), :] = silu(own_gate[...].astype(jnp.float32))
    gates[pl.ds(theirs, half), :] = silu(peer_gate[...].astype(jnp.float32))
    score = scores[block // (blocks // groups)]
    column = columns[block]
    at = pl.multiple_of(block * per_block, per_block)
    cum_row = cum_rows[pl.ds(at, per_block), :]
    step_row = step_rows[pl.ds(at, per_block), :]
    left = lane < HEAD_DIM
    scale = jnp.where(live, 1.0, 0.0)
    for pair in range(per_block // 2):
        spread, weights = [], []
        for j in (2 * pair, 2 * pair + 1):
            cum = jnp.broadcast_to(column[:, j : j + 1], (count, LANES))
            decay = jnp.exp(jnp.minimum(cum - cum_row[j : j + 1, :], 0.0))
            weights.append((decay * score * step_row[j : j + 1, :]).astype(jnp.bfloat16))
            spread.append(cum)
        lanes = slice(pair * LANES, (pair + 1) * LANES)
        x = active[:, lanes]
        zero = jnp.zeros_like(x)
        stacked = jnp.concatenate([jnp.where(left, x, zero), jnp.where(left, zero, x)], axis=0)
        intra = lax.dot_general(
            jnp.concatenate(weights, axis=1),
            stacked,
            (((1,), (0,)), ((), ())),
            preferred_element_type=jnp.float32,
        )
        skip = jnp.where(left, skip_ref[at + 2 * pair], skip_ref[at + 2 * pair + 1])
        gate = gates[:, lanes]
        intra_out[:, lanes] = (intra + skip * x.astype(jnp.float32)) * gate
        decayed = jnp.exp(jnp.where(left, spread[0], spread[1]))
        carry_out[:, lanes] = gate * decayed * scale


def main_stage(plan, d_skip, xbc, peer_xbc, weight, bias, gate, peer_gate, dt, peer_dt, dt_bias, decay_rate, rims):
    rows, channels = xbc.shape
    half = channels // 2
    count = 2 * rows
    inner = gate.shape[1] // 2
    width = half - inner
    groups = width // (2 * STATE)
    blocks = inner // width
    per_half = half // width
    per_inner = inner // width
    heads = dt_bias.shape[0]
    at_x = lambda i, plan, *_: (0, plan[CORE] * per_half + i)
    at_bc = lambda i, plan, *_: (0, plan[CORE] * per_half + blocks)
    at_gate = lambda i, plan, *_: (0, plan[CORE] * per_inner + i)
    fixed = lambda i, *_: (0, 0)
    step = lambda i, *_: (0, i)
    taps = weight.shape[0]
    token = lambda index: pl.BlockSpec((rows, width), index)
    grid_spec = pltpu.PrefetchScalarGridSpec(
        num_scalar_prefetch=2,
        grid=(blocks,),
        in_specs=[
            token(at_x),
            token(at_x),
            token(at_bc),
            token(at_bc),
            pl.BlockSpec((taps, width), at_x),
            pl.BlockSpec((taps, width), at_bc),
            pl.BlockSpec((1, width), at_x),
            pl.BlockSpec((1, width), at_bc),
            token(at_gate),
            token(at_gate),
            pl.BlockSpec((rows, LANES), fixed),
            pl.BlockSpec((rows, LANES), fixed),
            pl.BlockSpec((1, heads), fixed),
            pl.BlockSpec((1, heads), fixed),
        ]
        + [pl.BlockSpec((1, taps - 1, half), lambda i, *_: (0, 0, 0))] * len(rims),
        out_specs=[
            pl.BlockSpec((count, width), step),
            pl.BlockSpec((count, width), step),
            pl.BlockSpec((count, groups * STATE), fixed),
        ],
        scratch_shapes=[
            pltpu.VMEM((count + 8, width), jnp.float32),
            pltpu.VMEM((count, width), jnp.float32),
            pltpu.VMEM((groups, count, LANES), jnp.float32),
            pltpu.VMEM((blocks, count, width // HEAD_DIM), jnp.float32),
            pltpu.VMEM((LANES, count), jnp.float32),
            pltpu.VMEM((LANES, count), jnp.float32),
        ],
    )
    xbc, gate = keep_in(pltpu.HBM, xbc, gate)
    return pl.pallas_call(
        functools.partial(main_kernel, len(rims)),
        grid_spec=grid_spec,
        out_shape=[
            jax.ShapeDtypeStruct((count, inner), jnp.float32),
            jax.ShapeDtypeStruct((count, inner), jnp.float32),
            jax.ShapeDtypeStruct((count, groups * STATE), jnp.bfloat16),
        ],
        compiler_params=pltpu.CompilerParams(vmem_limit_bytes=16 << 20),
        cost_estimate=pl.CostEstimate(flops=400_000_000, bytes_accessed=8_000_000, transcendentals=2_000_000),
        name="main_stage",
    )(
        plan,
        d_skip,
        xbc,
        peer_xbc,
        xbc,
        peer_xbc,
        weight,
        weight,
        bias,
        bias,
        gate,
        peer_gate,
        dt,
        peer_dt,
        dt_bias.reshape(1, -1),
        decay_rate.reshape(1, -1),
        *rims,
    )


def tail_kernel(base, has_before, plan, *refs):
    out, wide, narrow, sems = refs[-4:]
    intra, carry, c_proj, gain = refs[-8 - has_before : -4 - has_before]
    pieces = refs[: -8 - has_before]
    tokens = wide.shape[0]
    count, rows = len(pieces), pieces[0].shape[0]
    turn = plan[TURNED + plan[ME]] if count > 1 else 0
    group = base ^ (turn // count)
    within = turn % count
    keep = lax.broadcasted_iota(jnp.int32, (tokens, 1), 0) < plan[SPAN]
    c = c_proj[:, pl.ds(pl.multiple_of(group * STATE, STATE), STATE)]
    part = min(rows, 512)
    total = jnp.zeros((tokens, 1), jnp.float32)
    places = []
    for k, piece in enumerate(pieces):
        for at in range(0, rows, part):
            local_at = pl.multiple_of((k ^ within) * rows + at, part)
            column = pl.multiple_of(group * NORM_WIDTH + local_at, part)
            carried = lax.dot_general(
                c, piece[at : at + part, :], (((1,), (1,)), ((), ())), preferred_element_type=jnp.float32
            )
            value = intra[:, pl.ds(column, part)] + carry[:, pl.ds(column, part)] * carried
            total = total + jnp.sum(value * value, axis=1, keepdims=True)
            index = len(places)
            wide[:, index * part : (index + 1) * part] = value
            places.append(column)
    scale = lax.rsqrt(total * (1.0 / NORM_WIDTH) + EPSILON)
    copies = []
    for index, column in enumerate(places):
        lanes = slice(index * part, (index + 1) * part)
        normed = wide[:, lanes] * scale * gain[:, pl.ds(column, part)]
        narrow[:, lanes] = jnp.where(keep, normed, 0.0).astype(jnp.bfloat16)
        copy = pltpu.make_async_copy(narrow.at[:, lanes], out.at[:, pl.ds(column, part)], sems.at[index])
        copy.start()
        copies.append(copy)
    for copy in copies:
        copy.wait()


def tail_stage(base, plan, pieces, intra, carry, c_proj, gain, before=None):
    tokens, _ = intra.shape
    vmem = pl.BlockSpec(memory_space=pltpu.VMEM)
    whole = pl.BlockSpec(memory_space=pltpu.HBM)
    earlier = [] if before is None else [before]
    parts = NORM_WIDTH // min(pieces[0].shape[0], 512)
    grid_spec = pltpu.PrefetchScalarGridSpec(
        num_scalar_prefetch=1,
        grid=(),
        in_specs=[vmem] * (len(pieces) + 4) + [whole] * len(earlier),
        out_specs=whole,
        scratch_shapes=[
            pltpu.VMEM((tokens, NORM_WIDTH), jnp.float32),
            pltpu.VMEM((tokens, NORM_WIDTH), jnp.bfloat16),
            pltpu.SemaphoreType.DMA((parts,)),
        ],
    )
    return pl.pallas_call(
        functools.partial(tail_kernel, base, len(earlier)),
        grid_spec=grid_spec,
        out_shape=jax.ShapeDtypeStruct(intra.shape, jnp.bfloat16),
        input_output_aliases={1 + len(pieces) + 4: 0} if earlier else {},
        compiler_params=pltpu.CompilerParams(vmem_limit_bytes=16 << 20),
        cost_estimate=pl.CostEstimate(flops=70_000_000, bytes_accessed=3_000_000, transcendentals=0),
    )(plan, *pieces, intra, carry, c_proj, gain, *earlier)


def plan_kernel(prefix_len, span_len, source_of, plan):
    me = lax.axis_index("dp")
    plan[CORE] = lax.axis_index("tensor")
    plan[ME] = me
    plan[PREFIX] = prefix_len[0]
    plan[SPAN] = span_len[0]
    for i in range(source_of.shape[0]):
        plan[TURNED + i] = source_of[i] ^ me


def plan_stage(prefix_len, span_len, source_of):
    smem = pl.BlockSpec(memory_space=pltpu.SMEM)
    return pl.pallas_call(
        plan_kernel,
        in_specs=[smem] * 3,
        out_specs=smem,
        out_shape=pltpu.SMEM((TURNED + source_of.shape[0],), jnp.int32),
        compiler_params=pltpu.CompilerParams(vmem_limit_bytes=1 << 20),
        name="plan_stage",
    )(prefix_len, span_len, source_of)


def cut_kernel(chosen, state, rims, *refs):
    pieces, rims_out, sems = refs[: len(chosen)], refs[-2], refs[-1]
    copies = []
    for i, (k, piece) in enumerate(zip(chosen, pieces)):
        copies.append(pltpu.make_async_copy(state.at[k], piece, sems.at[i]))
    copies.append(pltpu.make_async_copy(rims, rims_out, sems.at[len(chosen)]))
    for copy in copies:
        copy.start()
    for copy in copies:
        copy.wait()


def cut_stage(state, rims, chosen):
    return pl.pallas_call(
        functools.partial(cut_kernel, chosen),
        in_specs=[pl.BlockSpec(memory_space=pltpu.HBM)] * 2,
        out_specs=[pl.BlockSpec(memory_space=pltpu.VMEM)] * (len(chosen) + 1),
        out_shape=[pltpu.VMEM(state.shape[1:], state.dtype)] * len(chosen) + [pltpu.VMEM(rims.shape, rims.dtype)],
        scratch_shapes=[pltpu.SemaphoreType.DMA((len(chosen) + 1,))],
        compiler_params=pltpu.CompilerParams(vmem_limit_bytes=8 << 20),
        name="cut_stage",
    )(*keep_in(pltpu.HBM, state, rims))


def pick_kernel(order, column_count, plan, *refs):
    count = len(order)
    held, column = refs[:count], refs[count : count + column_count]
    slots, rim_out = refs[count + column_count : -1], refs[-1]
    for slot, k in zip(slots, order):
        wanted = plan[TURNED + (plan[ME] ^ k)]
        for r in range(count):

            @pl.when(wanted == r)
            def _(slot=slot, r=r):
                slot[...] = held[r][...]

    wanted = plan[TURNED + (plan[ME] ^ 1)] // 2
    for i in range(column_count):

        @pl.when(wanted == i)
        def _(i=i):
            rim_out[...] = column[i][...]


def pick_stage(plan, held, column, order):
    vmem = pl.BlockSpec(memory_space=pltpu.VMEM)
    grid_spec = pltpu.PrefetchScalarGridSpec(
        num_scalar_prefetch=1,
        grid=(),
        in_specs=[vmem] * (len(held) + len(column)),
        out_specs=[vmem] * (len(order) + 1),
    )
    shape = pltpu.VMEM(held[0].shape, held[0].dtype)
    return pl.pallas_call(
        functools.partial(pick_kernel, tuple(order), len(column)),
        grid_spec=grid_spec,
        out_shape=[shape] * len(order) + [pltpu.VMEM(column[0].shape, column[0].dtype)],
        compiler_params=pltpu.CompilerParams(vmem_limit_bytes=8 << 20),
        name="pick_stage",
    )(plan, *keep_in(pltpu.VMEM, *held), *keep_in(pltpu.VMEM, *column))


def column_rims(conv_store):
    count = lax.axis_size("dp")
    held = {0: conv_store}
    bit = count // 2
    while bit > 1:
        for k in sorted(held):
            held[k ^ bit] = swap(held[k], "dp", bit)
        bit //= 2
    return [held[2 * i] for i in range(count // 2)]


def gather_rims(conv_store, source_of, me):
    count = lax.axis_size("dp")
    held = conv_store
    index = jnp.zeros((), jnp.int32)
    away = source_of[me] ^ me
    bit = count // 2
    place = 1
    while bit > 0:
        held = jnp.concatenate([held, swap(held, "dp", bit)], axis=0)
        index = index + place * ((away // bit) & 1)
        bit //= 2
        place *= 2
    return lax.dynamic_index_in_dim(held, index, 0)


def local(
    xbc,
    gate_z,
    dt_raw,
    conv_weight,
    conv_bias,
    dt_bias,
    decay_rate,
    d_skip,
    norm_gain,
    ssm_store,
    conv_store,
    source_of,
    prefix_len,
    span_len,
):
    me = lax.axis_index("dp").astype(jnp.int32)
    owners = lax.axis_size("dp")
    direct = owners <= DIRECT_MAX
    order = offsets(owners)
    plan = plan_stage(prefix_len, span_len, source_of)
    state = ssm_store.reshape(owners, -1, STATE)
    if direct:
        held = [None] * owners
        every = order + [0]
        *pieces, own_rims = cut_stage(state, conv_store, every)
        column = column_rims(own_rims)
        for k, piece in zip(every, pieces):
            held[k] = swap(piece, "dp", k) if k else piece
        got = [None] * owners
        *picked, rim = pick_stage(plan, held, column, every)
        for k, piece in zip(every, picked):
            got[k] = swap(piece, "dp", k) if k else piece
        rims = column + [swap(rim, "dp", 1)]
    else:
        rims = [gather_rims(conv_store, source_of, me)]
        held = lax.all_to_all(state, "dp", split_axis=0, concat_axis=0, tiled=True)
        picked = jnp.take(held, source_of, axis=0)
        arrived = lax.all_to_all(picked, "dp", split_axis=0, concat_axis=0, tiled=True)
        got = list(arrived.reshape(-1, NORM_WIDTH, STATE))

    peer_xbc = swap(xbc, "tensor", 1)
    peer_gate = swap(gate_z, "tensor", 1)
    peer_dt = swap(dt_raw, "tensor", 1)
    intra, carry, c_proj = main_stage(
        plan,
        d_skip,
        xbc,
        peer_xbc,
        conv_weight,
        conv_bias.reshape(1, -1),
        gate_z,
        peer_gate,
        dt_raw,
        peer_dt,
        dt_bias,
        decay_rate,
        rims,
    )
    gain = norm_gain.reshape(1, -1)
    mixed = None
    norms = norm_gain.shape[0] // NORM_WIDTH
    share = len(got) // norms
    for base in range(norms):
        mine = got[base * share : (base + 1) * share]
        mixed = tail_stage(base, plan, mine, intra, carry, c_proj, gain, mixed)
    return mixed


def solution(mesh):
    in_specs = (
        P(("groups", "dp", "tensor"), None),
        P(("groups", "dp", "tensor"), None),
        P(("groups", "dp", "tensor"), None),
        P(),
        P(),
        P("tensor"),
        P("tensor"),
        P("tensor"),
        P("tensor"),
        P(("groups", "dp"), "tensor", None, None),
        P(("groups", "dp"), None, "tensor"),
        P("groups"),
        P(("groups", "dp")),
        P(("groups", "dp")),
    )
    out_specs = P(("groups", "dp"), "tensor")

    return jax.shard_map(local, mesh=mesh, in_specs=in_specs, out_specs=out_specs, check_vma=False)
```

time: 74.4 us -> 73.7 us (level)
  the two profiles are of different devices: /device:TPU:0 before, /device:TPU:8 now
where the time goes in v2:
time: 73.7 us; the launch traced here: 73.2 us
  waiting for transfers between devices  33.3 us (45%)
  starting transfers between devices  24.4 us (33%)
  Pallas kernels  13.4 us (18%)
  between operations  1.46 us (2%)
    ppermute x21, waiting for transfers between devices, swap(): return lax.ppermute(value, axis, [(i, i ^ offset) for i in range(count)])  33.3 us
    ppermute x21, starting transfers between devices, swap(): return lax.ppermute(value, axis, [(i, i ^ offset) for i in range(count)])  24.4 us
    pallas_call x1, Pallas kernels, main_stage(): pl.pallas_call(functools.partial(main_kernel, len(rims)), grid_spec=grid_...  8.47 us
    pallas_call x2, Pallas kernels, tail_stage(): pl.pallas_call(functools.partial(tail_kernel, base, len(earlier)), grid_s...  2.59 us
  transfers between devices with their start and end apart: 21, of which 13 were waited for; matrix products, arithmetic and copies ran while one was open for 0% of the time, Pallas kernels for 17%

profile of v2, /device:TPU:8, one launch (start us, length us, event | category | flops | bytes accessed | tf_op | source)
XLA Modules:
  0.0 73.2 jit_solution(989613743657767394)
XLA Ops:
  0.0 0.1 collective-permute-start.14
  0.1 0.5 collective-permute-start.15
  0.6 1.4 %cut_stage.1 = (bf16[512,128]{1,0:T(8,128)(2,1)S(1)}, bf16[512,128]{1,0:T(8,128)(2,1)S(1)}, bf16[512,128]{1,0:T(8,128)(2,1)S(1)}, bf16[512,128]{1,0:T(8,128)(2,1...) custom-call(bf16[8,512,128]{2,1,0:T(8,128)(2,1)} %bitcast.11, ...), custom_call_target="tpu_custom_call" | custom-call | tf_op jit(solution)/shard_map/cut_stage/pallas_call | solution.py:344
  2.0 1.6 %collective-permute-start = (bf16[512,128]{1,0:T(8,128)(2,1)S(1)}, bf16[512,128]{1,0:T(8,128)(2,1)S(1)}, u32[]{:S(2)}, u32[]{:S(2)}) collective-permute-start(bf16[512,128]{1,0:T(8,128)(2,1)S(1)} %get-tuple-element.27), channel_id=1, source_target_pairs={{0,2},{2,0},{4,6},{6,4},{8,10},{10,8},{12,14},{14,12},{1,3},{3,1},... | collective-permute-start | bytes 393224 | tf_op jit(solution)/shard_map/ppermute | solution.py:21
  3.5 2.6 %collective-permute-start.8 = (bf16[1,3,4608]{2,1,0:T(4,128)(2,1)S(1)}, bf16[1,3,4608]{2,1,0:T(4,128)(2,1)S(1)}, u32[]{:S(2)}, u32[]{:S(2)}) collective-permute-start(bf16[1,3,4608]{2,1,0:T(4,128)(2,1)S(1)} %get-tuple-element.34.refs_8_.refs_0_), channel_id=1, source_target_pairs={{0,8},{2,10},{4,12},{6,14},{8,0},{10,2},{12,4},{14,6},{1,9},{3,11}... | collective-permute-start | bytes 82952 | tf_op jit(solution)/shard_map/ppermute | solution.py:21
  6.1 0.4 collective-permute-start.7
  6.6 1.8 %collective-permute-done.8.refs_10_.refs_2_ = bf16[1,3,4608]{2,1,0:T(4,128)(2,1)S(1)} collective-permute-done((bf16[1,3,4608]{2,1,0:T(4,128)(2,1)S(1)}, bf16[1,3,4608]{2,1,0:T(4,128)(2,1)S(1)}, u32[]{:S(2)}, u32[]{:S(2)}) %collective-permute-start.8) | collective-permute-done | bytes 27680 | tf_op jit(solution)/shard_map/ppermute | solution.py:21
  8.4 0.8 %collective-permute-start.9 = (bf16[1,3,4608]{2,1,0:T(4,128)(2,1)S(1)}, bf16[1,3,4608]{2,1,0:T(4,128)(2,1)S(1)}, u32[]{:S(2)}, u32[]{:S(2)}) collective-permute-start(bf16[1,3,4608]{2,1,0:T(4,128)(2,1)S(1)} %collective-permute-done.8.refs_10_.refs_2_), channel_id=1, source_target_pairs={{0,4},{2,6},{4,0},{6,2},{8,12},{10,14},{12,8},{14,10},{1,5},{3,7},... | collective-permute-start | bytes 82952 | tf_op jit(solution)/shard_map/ppermute | solution.py:21
  9.2 1.3 %collective-permute-done.7.refs_9_.refs_1_ = bf16[1,3,4608]{2,1,0:T(4,128)(2,1)S(1)} collective-permute-done((bf16[1,3,4608]{2,1,0:T(4,128)(2,1)S(1)}, bf16[1,3,4608]{2,1,0:T(4,128)(2,1)S(1)}, u32[]{:S(2)}, u32[]{:S(2)}) %collective-permute-start.7) | collective-permute-done | bytes 27680 | tf_op jit(solution)/shard_map/ppermute | solution.py:21
  10.5 0.4 collective-permute-start.1
  10.9 1.9 %collective-permute-done.9.refs_11_.refs_3_ = bf16[1,3,4608]{2,1,0:T(4,128)(2,1)S(1)} collective-permute-done((bf16[1,3,4608]{2,1,0:T(4,128)(2,1)S(1)}, bf16[1,3,4608]{2,1,0:T(4,128)(2,1)S(1)}, u32[]{:S(2)}, u32[]{:S(2)}) %collective-permute-start.9) | collective-permute-done | bytes 27680 | tf_op jit(solution)/shard_map/ppermute | solution.py:21
  12.7 0.6 collective-permute-start.2
  13.3 0.0 collective-permute-done.refs_1_
  13.3 2.7 %collective-permute-start.3 = (bf16[512,128]{1,0:T(8,128)(2,1)S(1)}, bf16[512,128]{1,0:T(8,128)(2,1)S(1)}, u32[]{:S(2)}, u32[]{:S(2)}) collective-permute-start(bf16[512,128]{1,0:T(8,128)(2,1)S(1)} %get-tuple-element.30), channel_id=1, source_target_pairs={{0,8},{2,10},{4,12},{6,14},{8,0},{10,2},{12,4},{14,6},{1,9},{3,11}... | collective-permute-start | bytes 393224 | tf_op jit(solution)/shard_map/ppermute | solution.py:21
  16.0 0.8 %collective-permute-done.1.refs_2_ = bf16[512,128]{1,0:T(8,128)(2,1)S(1)} collective-permute-done((bf16[512,128]{1,0:T(8,128)(2,1)S(1)}, bf16[512,128]{1,0:T(8,128)(2,1)S(1)}, u32[]{:S(2)}, u32[]{:S(2)}) %collective-permute-start.1) | collective-permute-done | bytes 131104 | tf_op jit(solution)/shard_map/ppermute | solution.py:21
  16.8 0.5 collective-permute-start.4
  17.4 2.6 %collective-permute-done.2.refs_3_ = bf16[512,128]{1,0:T(8,128)(2,1)S(1)} collective-permute-done((bf16[512,128]{1,0:T(8,128)(2,1)S(1)}, bf16[512,128]{1,0:T(8,128)(2,1)S(1)}, u32[]{:S(2)}, u32[]{:S(2)}) %collective-permute-start.2) | collective-permute-done | bytes 131104 | tf_op jit(solution)/shard_map/ppermute | solution.py:21
  20.0 1.8 %collective-permute-start.5 = (bf16[512,128]{1,0:T(8,128)(2,1)S(1)}, bf16[512,128]{1,0:T(8,128)(2,1)S(1)}, u32[]{:S(2)}, u32[]{:S(2)}) collective-permute-start(bf16[512,128]{1,0:T(8,128)(2,1)S(1)} %get-tuple-element.32), channel_id=1, source_target_pairs={{0,12},{2,14},{4,8},{6,10},{8,4},{10,6},{12,0},{14,2},{1,13},{3,15... | collective-permute-start | bytes 393224 | tf_op jit(solution)/shard_map/ppermute | solution.py:21
  21.9 5.8 %collective-permute-done.3.refs_4_ = bf16[512,128]{1,0:T(8,128)(2,1)S(1)} collective-permute-done((bf16[512,128]{1,0:T(8,128)(2,1)S(1)}, bf16[512,128]{1,0:T(8,128)(2,1)S(1)}, u32[]{:S(2)}, u32[]{:S(2)}) %collective-permute-start.3) | collective-permute-done | bytes 131104 | tf_op jit(solution)/shard_map/ppermute | solution.py:21
  27.6 1.9 %collective-permute-start.6 = (bf16[512,128]{1,0:T(8,128)(2,1)S(1)}, bf16[512,128]{1,0:T(8,128)(2,1)S(1)}, u32[]{:S(2)}, u32[]{:S(2)}) collective-permute-start(bf16[512,128]{1,0:T(8,128)(2,1)S(1)} %get-tuple-element.33), channel_id=1, source_target_pairs={{0,14},{2,12},{4,10},{6,8},{8,6},{10,4},{12,2},{14,0},{1,15},{3,13... | collective-permute-start | bytes 393224 | tf_op jit(solution)/shard_map/ppermute | solution.py:21
  30.9 0.0 copy-start.7
  30.9 0.6 copy-done.7
  31.5 0.6 plan_stage.1.plan
  32.1 2.8 %collective-permute-done.5.refs_6_ = bf16[512,128]{1,0:T(8,128)(2,1)S(1)} collective-permute-done((bf16[512,128]{1,0:T(8,128)(2,1)S(1)}, bf16[512,128]{1,0:T(8,128)(2,1)S(1)}, u32[]{:S(2)}, u32[]{:S(2)}) %collective-permute-start.5) | collective-permute-done | bytes 131104 | tf_op jit(solution)/shard_map/ppermute | solution.py:21
  34.9 3.3 %collective-permute-done.6.refs_7_ = bf16[512,128]{1,0:T(8,128)(2,1)S(1)} collective-permute-done((bf16[512,128]{1,0:T(8,128)(2,1)S(1)}, bf16[512,128]{1,0:T(8,128)(2,1)S(1)}, u32[]{:S(2)}, u32[]{:S(2)}) %collective-permute-start.6) | collective-permute-done | bytes 131104 | tf_op jit(solution)/shard_map/ppermute | solution.py:21
  38.1 0.5 pick_stage.1
  38.6 1.1 %collective-permute-start.18 = (bf16[512,128]{1,0:T(8,128)(2,1)S(1)}, bf16[512,128]{1,0:T(8,128)(2,1)S(1)}, u32[]{:S(2)}, u32[]{:S(2)}) collective-permute-start(bf16[512,128]{1,0:T(8,128)(2,1)S(1)} %get-tuple-element.44), channel_id=1, source_target_pairs={{0,2},{2,0},{4,6},{6,4},{8,10},{10,8},{12,14},{14,12},{1,3},{3,1},... | collective-permute-start | bytes 393224 | tf_op jit(solution)/shard_map/ppermute | solution.py:21
  39.7 0.7 collective-permute-start.19
  40.4 0.0 collective-permute-start.16
  40.4 1.2 %collective-permute-done.16.peer_dt = bf16[64,128]{1,0:T(8,128)(2,1)S(1)} collective-permute-done((bf16[64,128]{1,0:T(8,128)(2,1)S(1)}, bf16[64,128]{1,0:T(8,128)(2,1)S(1)}, u32[]{:S(2)}, u32[]{:S(2)}) %collective-permute-start.16) | collective-permute-done | bytes 16416 | tf_op jit(solution)/shard_map/ppermute | solution.py:21
  41.6 1.0 %collective-permute-start.17 = (bf16[1,3,4608]{2,1,0:T(4,128)(2,1)S(1)}, bf16[1,3,4608]{2,1,0:T(4,128)(2,1)S(1)}, u32[]{:S(2)}, u32[]{:S(2)}) collective-permute-start(bf16[1,3,4608]{2,1,0:T(4,128)(2,1)S(1)} %get-tuple-element.39), channel_id=1, source_target_pairs={{0,2},{2,0},{4,6},{6,4},{8,10},{10,8},{12,14},{14,12},{1,3},{3,1},... | collective-permute-start | bytes 82952 | tf_op jit(solution)/shard_map/ppermute | solution.py:21
  42.5 3.0 %collective-permute-done.17.refs_4_ = bf16[1,3,4608]{2,1,0:T(4,128)(2,1)S(1)} collective-permute-done((bf16[1,3,4608]{2,1,0:T(4,128)(2,1)S(1)}, bf16[1,3,4608]{2,1,0:T(4,128)(2,1)S(1)}, u32[]{:S(2)}, u32[]{:S(2)}) %collective-permute-start.17) | collective-permute-done | bytes 27680 | tf_op jit(solution)/shard_map/ppermute | solution.py:21
  45.5 1.8 %collective-permute-start.20 = (bf16[512,128]{1,0:T(8,128)(2,1)S(1)}, bf16[512,128]{1,0:T(8,128)(2,1)S(1)}, u32[]{:S(2)}, u32[]{:S(2)}) collective-permute-start(bf16[512,128]{1,0:T(8,128)(2,1)S(1)} %get-tuple-element.46), channel_id=1, source_target_pairs={{0,6},{2,4},{4,2},{6,0},{8,14},{10,12},{12,10},{14,8},{1,7},{3,5},... | collective-permute-start | bytes 393224 | tf_op jit(solution)/shard_map/ppermute | solution.py:21
  47.3 0.7 collective-permute-start.10
  48.0 0.0 collective-permute-done.19.refs_2_
  48.0 2.7 %collective-permute-start.11 = (bf16[512,128]{1,0:T(8,128)(2,1)S(1)}, bf16[512,128]{1,0:T(8,128)(2,1)S(1)}, u32[]{:S(2)}, u32[]{:S(2)}) collective-permute-start(bf16[512,128]{1,0:T(8,128)(2,1)S(1)} %get-tuple-element.36), channel_id=1, source_target_pairs={{0,10},{2,8},{4,14},{6,12},{8,2},{10,0},{12,6},{14,4},{1,11},{3,9}... | collective-permute-start | bytes 393224 | tf_op jit(solution)/shard_map/ppermute | solution.py:21
  50.7 0.0 collective-permute-done.15.peer_gate
  50.7 0.0 collective-permute-start.12
  50.7 0.0 collective-permute-done.14.peer_x.peer_bc
  50.7 2.5 %collective-permute-start.13 = (bf16[512,128]{1,0:T(8,128)(2,1)S(1)}, bf16[512,128]{1,0:T(8,128)(2,1)S(1)}, u32[]{:S(2)}, u32[]{:S(2)}) collective-permute-start(bf16[512,128]{1,0:T(8,128)(2,1)S(1)} %get-tuple-element.38), channel_id=1, source_target_pairs={{0,14},{2,12},{4,10},{6,8},{8,6},{10,4},{12,2},{14,0},{1,15},{3,13... | collective-permute-start | bytes 393224 | tf_op jit(solution)/shard_map/ppermute | solution.py:21
  53.2 0.0 copy-start.2
  53.2 8.5 %main_stage.1 = (f32[128,4096]{1,0:T(8,128)S(1)}, f32[128,4096]{1,0:T(8,128)S(1)}, bf16[128,256]{1,0:T(8,128)(2,1)S(1)}) custom-call(s32[12]{0:T(128)S(4)} %plan_stage.1.plan, f32[64]{0:T(128)S(1)} %copy-done.4, bf16[64,9216]{1,0:T(8,128)(2,1)} %own_bc.1, bf16[64,9216]{1,0:T(8,128)(2,1)S(1)} %collective-permute-done.14.peer_x.peer_bc, ...), custom_call_target="tpu_custom_call" | custom-call | flops 400000000 | bytes 8000000 | tf_op jit(solution)/shard_map/main_stage/pallas_call | solution.py:211
  61.7 0.0 collective-permute-done.20.refs_3_
  61.7 1.3 %shard_map.136.refs_8_ = bf16[128,4096]{1,0:T(8,128)(2,1)} custom-call(s32[12]{0:T(128)S(4)} %plan_stage.1.plan, bf16[512,128]{1,0:T(8,128)(2,1)S(1)} %get-tuple-element.43.refs_0_, bf16[512,128]{1,0:T(8,128)(2,1)S(1)} %collective-permute-done.18.refs_1_, bf16[512,128]{1,0:T(8,128)(2,1)S(1)} %collective-permute-done.19.refs_2_, ...), custom_call_target="tpu_custom_call" | custom-call | flops 70000000 | bytes 3000000 | tf_op jit(solution)/shard_map/pallas_call | solution.py:299
  63.0 2.3 %collective-permute-done.11.refs_1_ = bf16[512,128]{1,0:T(8,128)(2,1)S(1)} collective-permute-done((bf16[512,128]{1,0:T(8,128)(2,1)S(1)}, bf16[512,128]{1,0:T(8,128)(2,1)S(1)}, u32[]{:S(2)}, u32[]{:S(2)}) %collective-permute-start.11) | collective-permute-done | bytes 131104 | tf_op jit(solution)/shard_map/ppermute | solution.py:21
  65.3 4.6 %collective-permute-done.12.refs_2_ = bf16[512,128]{1,0:T(8,128)(2,1)S(1)} collective-permute-done((bf16[512,128]{1,0:T(8,128)(2,1)S(1)}, bf16[512,128]{1,0:T(8,128)(2,1)S(1)}, u32[]{:S(2)}, u32[]{:S(2)}) %collective-permute-start.12) | collective-permute-done | bytes 131104 | tf_op jit(solution)/shard_map/ppermute | solution.py:21
  69.9 2.0 %collective-permute-done.13.refs_3_ = bf16[512,128]{1,0:T(8,128)(2,1)S(1)} collective-permute-done((bf16[512,128]{1,0:T(8,128)(2,1)S(1)}, bf16[512,128]{1,0:T(8,128)(2,1)S(1)}, u32[]{:S(2)}, u32[]{:S(2)}) %collective-permute-start.13) | collective-permute-done | bytes 131104 | tf_op jit(solution)/shard_map/ppermute | solution.py:21
  71.9 1.3 %shard_map.137 = bf16[128,4096]{1,0:T(8,128)(2,1)} custom-call(s32[12]{0:T(128)S(4)} %plan_stage.1.plan, bf16[512,128]{1,0:T(8,128)(2,1)S(1)} %collective-permute-done.10.refs_0_, bf16[512,128]{1,0:T(8,128)(2,1)S(1)} %collective-permute-done.11.refs_1_, bf16[512,128]{1,0:T(8,128)(2,1)S(1)} %collective-permute-done.12.refs_2_, ...), custom_call_target="tpu_custom_call", output_to_operand_aliasing={{}: (9, {})} | custom-call | flops 70000000 | bytes 3000000 | tf_op jit(solution)/shard_map/pallas_call | solution.py:299
  (16 shorter events, 0.0 us)
Async XLA Ops:
  0.0 40.4 %copy-start.3 = (bf16[64,128]{1,0:T(8,128)(2,1)S(1)}, bf16[64,128]{1,0:T(8,128)(2,1)}, u32[]{:S(2)}) copy-start(bf16[64,128]{1,0:T(8,128)(2,1)} %own_dt.1) | copy-start | bytes 49156
  0.0 53.2 %copy-start.4 = (f32[64]{0:T(128)S(1)}, f32[64]{0:T(128)}, u32[]{:S(2)}) copy-start(f32[64]{0:T(128)} %skip_ref.1) | copy-start | bytes 772
  0.0 53.2 %copy-start.6 = (f32[64]{0:T(128)S(1)}, f32[64]{0:T(128)}, u32[]{:S(2)}) copy-start(f32[64]{0:T(128)} %param.20) | copy-start | bytes 772
  0.0 53.2 %copy-start.5 = (f32[64]{0:T(128)S(1)}, f32[64]{0:T(128)}, u32[]{:S(2)}) copy-start(f32[64]{0:T(128)} %param.19) | copy-start | bytes 772
  0.0 53.1 %copy-start.1 = (f32[9216]{0:T(1024)S(1)}, f32[9216]{0:T(1024)}, u32[]{:S(2)}) copy-start(f32[9216]{0:T(1024)} %param.18) | copy-start | bytes 110596
  0.0 53.1 %copy-start = (f32[4,9216]{1,0:T(4,128)S(1)}, f32[4,9216]{1,0:T(4,128)}, u32[]{:S(2)}) copy-start(f32[4,9216]{1,0:T(4,128)} %weight_bc.1) | copy-start | bytes 442372
  0.0 50.7 %collective-permute-start.14 = (bf16[64,9216]{1,0:T(8,128)(2,1)}, bf16[64,9216]{1,0:T(8,128)(2,1)S(1)}, u32[]{:S(2)}, u32[]{:S(2)}) collective-permute-start(bf16[64,9216]{1,0:T(8,128)(2,1)} %own_bc.1), channel_id=1, source_target_pairs={{0,1},{1,0},{2,3},{3,2},{4,5},{5,4},{6,7},{7,6},{8,9},{9,8},{10,11... | collective-permute-start | bytes 3538952 | tf_op jit(solution)/shard_map/ppermute | solution.py:21
  0.1 50.6 %collective-permute-start.15 = (bf16[64,8192]{1,0:T(8,128)(2,1)}, bf16[64,8192]{1,0:T(8,128)(2,1)S(1)}, u32[]{:S(2)}, u32[]{:S(2)}) collective-permute-start(bf16[64,8192]{1,0:T(8,128)(2,1)} %own_gate.1), channel_id=1, source_target_pairs={{0,1},{1,0},{2,3},{3,2},{4,5},{5,4},{6,7},{7,6},{8,9},{9,8},{10,11... | collective-permute-start | bytes 3145736 | tf_op jit(solution)/shard_map/ppermute | solution.py:21
  2.0 11.4 %collective-permute-start = (bf16[512,128]{1,0:T(8,128)(2,1)S(1)}, bf16[512,128]{1,0:T(8,128)(2,1)S(1)}, u32[]{:S(2)}, u32[]{:S(2)}) collective-permute-start(bf16[512,128]{1,0:T(8,128)(2,1)S(1)} %get-tuple-element.27), channel_id=1, source_target_pairs={{0,2},{2,0},{4,6},{6,4},{8,10},{10,8},{12,14},{14,12},{1,3},{3,1},... | collective-permute-start | bytes 393224 | tf_op jit(solution)/shard_map/ppermute | solution.py:21
  3.5 4.9 %collective-permute-start.8 = (bf16[1,3,4608]{2,1,0:T(4,128)(2,1)S(1)}, bf16[1,3,4608]{2,1,0:T(4,128)(2,1)S(1)}, u32[]{:S(2)}, u32[]{:S(2)}) collective-permute-start(bf16[1,3,4608]{2,1,0:T(4,128)(2,1)S(1)} %get-tuple-element.34.refs_8_.refs_0_), channel_id=1, source_target_pairs={{0,8},{2,10},{4,12},{6,14},{8,0},{10,2},{12,4},{14,6},{1,9},{3,11}... | collective-permute-start | bytes 82952 | tf_op jit(solution)/shard_map/ppermute | solution.py:21
  6.1 4.3 %collective-permute-start.7 = (bf16[1,3,4608]{2,1,0:T(4,128)(2,1)S(1)}, bf16[1,3,4608]{2,1,0:T(4,128)(2,1)S(1)}, u32[]{:S(2)}, u32[]{:S(2)}) collective-permute-start(bf16[1,3,4608]{2,1,0:T(4,128)(2,1)S(1)} %get-tuple-element.34.refs_8_.refs_0_), channel_id=1, source_target_pairs={{0,4},{2,6},{4,0},{6,2},{8,12},{10,14},{12,8},{14,10},{1,5},{3,7},... | collective-permute-start | bytes 82952 | tf_op jit(solution)/shard_map/ppermute | solution.py:21
  8.4 4.3 %collective-permute-start.9 = (bf16[1,3,4608]{2,1,0:T(4,128)(2,1)S(1)}, bf16[1,3,4608]{2,1,0:T(4,128)(2,1)S(1)}, u32[]{:S(2)}, u32[]{:S(2)}) collective-permute-start(bf16[1,3,4608]{2,1,0:T(4,128)(2,1)S(1)} %collective-permute-done.8.refs_10_.refs_2_), channel_id=1, source_target_pairs={{0,4},{2,6},{4,0},{6,2},{8,12},{10,14},{12,8},{14,10},{1,5},{3,7},... | collective-permute-start | bytes 82952 | tf_op jit(solution)/shard_map/ppermute | solution.py:21
  10.5 6.4 %collective-permute-start.1 = (bf16[512,128]{1,0:T(8,128)(2,1)S(1)}, bf16[512,128]{1,0:T(8,128)(2,1)S(1)}, u32[]{:S(2)}, u32[]{:S(2)}) collective-permute-start(bf16[512,128]{1,0:T(8,128)(2,1)S(1)} %get-tuple-element.28), channel_id=1, source_target_pairs={{0,4},{2,6},{4,0},{6,2},{8,12},{10,14},{12,8},{14,10},{1,5},{3,7},... | collective-permute-start | bytes 393224 | tf_op jit(solution)/shard_map/ppermute | solution.py:21
  12.7 7.3 %collective-permute-start.2 = (bf16[512,128]{1,0:T(8,128)(2,1)S(1)}, bf16[512,128]{1,0:T(8,128)(2,1)S(1)}, u32[]{:S(2)}, u32[]{:S(2)}) collective-permute-start(bf16[512,128]{1,0:T(8,128)(2,1)S(1)} %get-tuple-element.29), channel_id=1, source_target_pairs={{0,6},{2,4},{4,2},{6,0},{8,14},{10,12},{12,10},{14,8},{1,7},{3,5},... | collective-permute-start | bytes 393224 | tf_op jit(solution)/shard_map/ppermute | solution.py:21
  13.3 14.3 %collective-permute-start.3 = (bf16[512,128]{1,0:T(8,128)(2,1)S(1)}, bf16[512,128]{1,0:T(8,128)(2,1)S(1)}, u32[]{:S(2)}, u32[]{:S(2)}) collective-permute-start(bf16[512,128]{1,0:T(8,128)(2,1)S(1)} %get-tuple-element.30), channel_id=1, source_target_pairs={{0,8},{2,10},{4,12},{6,14},{8,0},{10,2},{12,4},{14,6},{1,9},{3,11}... | collective-permute-start | bytes 393224 | tf_op jit(solution)/shard_map/ppermute | solution.py:21
  16.8 15.3 %collective-permute-start.4 = (bf16[512,128]{1,0:T(8,128)(2,1)S(1)}, bf16[512,128]{1,0:T(8,128)(2,1)S(1)}, u32[]{:S(2)}, u32[]{:S(2)}) collective-permute-start(bf16[512,128]{1,0:T(8,128)(2,1)S(1)} %get-tuple-element.31), channel_id=1, source_target_pairs={{0,10},{2,8},{4,14},{6,12},{8,2},{10,0},{12,6},{14,4},{1,11},{3,9}... | collective-permute-start | bytes 393224 | tf_op jit(solution)/shard_map/ppermute | solution.py:21
  20.0 14.8 %collective-permute-start.5 = (bf16[512,128]{1,0:T(8,128)(2,1)S(1)}, bf16[512,128]{1,0:T(8,128)(2,1)S(1)}, u32[]{:S(2)}, u32[]{:S(2)}) collective-permute-start(bf16[512,128]{1,0:T(8,128)(2,1)S(1)} %get-tuple-element.32), channel_id=1, source_target_pairs={{0,12},{2,14},{4,8},{6,10},{8,4},{10,6},{12,0},{14,2},{1,13},{3,15... | collective-permute-start | bytes 393224 | tf_op jit(solution)/shard_map/ppermute | solution.py:21
  27.6 10.5 %collective-permute-start.6 = (bf16[512,128]{1,0:T(8,128)(2,1)S(1)}, bf16[512,128]{1,0:T(8,128)(2,1)S(1)}, u32[]{:S(2)}, u32[]{:S(2)}) collective-permute-start(bf16[512,128]{1,0:T(8,128)(2,1)S(1)} %get-tuple-element.33), channel_id=1, source_target_pairs={{0,14},{2,12},{4,10},{6,8},{8,6},{10,4},{12,2},{14,0},{1,15},{3,13... | collective-permute-start | bytes 393224 | tf_op jit(solution)/shard_map/ppermute | solution.py:21
  30.9 0.7 copy-start.7
  38.6 8.7 %collective-permute-start.18 = (bf16[512,128]{1,0:T(8,128)(2,1)S(1)}, bf16[512,128]{1,0:T(8,128)(2,1)S(1)}, u32[]{:S(2)}, u32[]{:S(2)}) collective-permute-start(bf16[512,128]{1,0:T(8,128)(2,1)S(1)} %get-tuple-element.44), channel_id=1, source_target_pairs={{0,2},{2,0},{4,6},{6,4},{8,10},{10,8},{12,14},{14,12},{1,3},{3,1},... | collective-permute-start | bytes 393224 | tf_op jit(solution)/shard_map/ppermute | solution.py:21
  39.7 8.3 %collective-permute-start.19 = (bf16[512,128]{1,0:T(8,128)(2,1)S(1)}, bf16[512,128]{1,0:T(8,128)(2,1)S(1)}, u32[]{:S(2)}, u32[]{:S(2)}) collective-permute-start(bf16[512,128]{1,0:T(8,128)(2,1)S(1)} %get-tuple-element.45), channel_id=1, source_target_pairs={{0,4},{2,6},{4,0},{6,2},{8,12},{10,14},{12,8},{14,10},{1,5},{3,7},... | collective-permute-start | bytes 393224 | tf_op jit(solution)/shard_map/ppermute | solution.py:21
  40.4 1.2 %collective-permute-start.16 = (bf16[64,128]{1,0:T(8,128)(2,1)S(1)}, bf16[64,128]{1,0:T(8,128)(2,1)S(1)}, u32[]{:S(2)}, u32[]{:S(2)}) collective-permute-start(bf16[64,128]{1,0:T(8,128)(2,1)S(1)} %copy-done.3), channel_id=1, source_target_pairs={{0,1},{1,0},{2,3},{3,2},{4,5},{5,4},{6,7},{7,6},{8,9},{9,8},{10,11... | collective-permute-start | bytes 49160 | tf_op jit(solution)/shard_map/ppermute | solution.py:21
  41.6 4.0 %collective-permute-start.17 = (bf16[1,3,4608]{2,1,0:T(4,128)(2,1)S(1)}, bf16[1,3,4608]{2,1,0:T(4,128)(2,1)S(1)}, u32[]{:S(2)}, u32[]{:S(2)}) collective-permute-start(bf16[1,3,4608]{2,1,0:T(4,128)(2,1)S(1)} %get-tuple-element.39), channel_id=1, source_target_pairs={{0,2},{2,0},{4,6},{6,4},{8,10},{10,8},{12,14},{14,12},{1,3},{3,1},... | collective-permute-start | bytes 82952 | tf_op jit(solution)/shard_map/ppermute | solution.py:21
  45.5 16.2 %collective-permute-start.20 = (bf16[512,128]{1,0:T(8,128)(2,1)S(1)}, bf16[512,128]{1,0:T(8,128)(2,1)S(1)}, u32[]{:S(2)}, u32[]{:S(2)}) collective-permute-start(bf16[512,128]{1,0:T(8,128)(2,1)S(1)} %get-tuple-element.46), channel_id=1, source_target_pairs={{0,6},{2,4},{4,2},{6,0},{8,14},{10,12},{12,10},{14,8},{1,7},{3,5},... | collective-permute-start | bytes 393224 | tf_op jit(solution)/shard_map/ppermute | solution.py:21
  47.3 15.7 %collective-permute-start.10 = (bf16[512,128]{1,0:T(8,128)(2,1)S(1)}, bf16[512,128]{1,0:T(8,128)(2,1)S(1)}, u32[]{:S(2)}, u32[]{:S(2)}) collective-permute-start(bf16[512,128]{1,0:T(8,128)(2,1)S(1)} %get-tuple-element.35), channel_id=1, source_target_pairs={{0,8},{2,10},{4,12},{6,14},{8,0},{10,2},{12,4},{14,6},{1,9},{3,11}... | collective-permute-start | bytes 393224 | tf_op jit(solution)/shard_map/ppermute | solution.py:21
  48.0 17.3 %collective-permute-start.11 = (bf16[512,128]{1,0:T(8,128)(2,1)S(1)}, bf16[512,128]{1,0:T(8,128)(2,1)S(1)}, u32[]{:S(2)}, u32[]{:S(2)}) collective-permute-start(bf16[512,128]{1,0:T(8,128)(2,1)S(1)} %get-tuple-element.36), channel_id=1, source_target_pairs={{0,10},{2,8},{4,14},{6,12},{8,2},{10,0},{12,6},{14,4},{1,11},{3,9}... | collective-permute-start | bytes 393224 | tf_op jit(solution)/shard_map/ppermute | solution.py:21
  50.7 19.2 %collective-permute-start.12 = (bf16[512,128]{1,0:T(8,128)(2,1)S(1)}, bf16[512,128]{1,0:T(8,128)(2,1)S(1)}, u32[]{:S(2)}, u32[]{:S(2)}) collective-permute-start(bf16[512,128]{1,0:T(8,128)(2,1)S(1)} %get-tuple-element.37), channel_id=1, source_target_pairs={{0,12},{2,14},{4,8},{6,10},{8,4},{10,6},{12,0},{14,2},{1,13},{3,15... | collective-permute-start | bytes 393224 | tf_op jit(solution)/shard_map/ppermute | solution.py:21
  50.7 21.2 %collective-permute-start.13 = (bf16[512,128]{1,0:T(8,128)(2,1)S(1)}, bf16[512,128]{1,0:T(8,128)(2,1)S(1)}, u32[]{:S(2)}, u32[]{:S(2)}) collective-permute-start(bf16[512,128]{1,0:T(8,128)(2,1)S(1)} %get-tuple-element.38), channel_id=1, source_target_pairs={{0,14},{2,12},{4,10},{6,8},{8,6},{10,4},{12,2},{14,0},{1,15},{3,13... | collective-permute-start | bytes 393224 | tf_op jit(solution)/shard_map/ppermute | solution.py:21
  53.2 8.5 %copy-start.2 = (f32[4096]{0:T(1024)S(1)}, f32[4096]{0:T(1024)}, u32[]{:S(2)}) copy-start(f32[4096]{0:T(1024)} %param.22) | copy-start | bytes 49156

commit v3 on v2

--- a/solution.py
+++ b/solution.py
@@ -390,13 +390,14 @@
     )(plan, *keep_in(pltpu.VMEM, *held), *keep_in(pltpu.VMEM, *column))
 
 
-def column_rims(conv_store):
+def column_rims(conv_store, own_rims):
     count = lax.axis_size("dp")
     held = {0: conv_store}
     bit = count // 2
     while bit > 1:
         for k in sorted(held):
             held[k ^ bit] = swap(held[k], "dp", bit)
+        held[0] = own_rims
         bit //= 2
     return [held[2 * i] for i in range(count // 2)]
 
@@ -441,9 +442,9 @@
     if direct:
         held = [None] * owners
         every = order + [0]
-        *pieces, own_rims = cut_stage(state, conv_store, every)
-        column = column_rims(own_rims)
-        for k, piece in zip(every, pieces):
+        *pieces, own_rims = cut_stage(state, conv_store, every[1:])
+        column = column_rims(conv_store, own_rims)
+        for k, piece in zip(every, [state[every[0]]] + pieces):
             held[k] = swap(piece, "dp", k) if k else piece
         got = [None] * owners
         *picked, rim = pick_stage(plan, held, column, every)

time: 73.7 us -> 73.9 us (level)
  the two profiles are of different devices: /device:TPU:8 before, /device:TPU:12 now
where the time goes in v3:
time: 73.9 us; the launch traced here: 73.4 us
  starting transfers between devices  29.3 us (40%)
  waiting for transfers between devices  27.7 us (37%)
  Pallas kernels  13.4 us (18%)
  local copies, waits for them, and re-layouts  1.59 us (2%)
  between operations  1.45 us (2%)
    ppermute x21, starting transfers between devices, swap(): return lax.ppermute(value, axis, [(i, i ^ offset) for i in range(count)])  29.3 us
    ppermute x21, waiting for transfers between devices, swap(): return lax.ppermute(value, axis, [(i, i ^ offset) for i in range(count)])  27.7 us
    pallas_call x1, Pallas kernels, main_stage(): pl.pallas_call(functools.partial(main_kernel, len(rims)), grid_spec=grid_...  8.48 us
    pallas_call x2, Pallas kernels, tail_stage(): pl.pallas_call(functools.partial(tail_kernel, base, len(earlier)), grid_s...  2.59 us
  transfers between devices with their start and end apart: 21, of which 12 were waited for; matrix products, arithmetic and copies ran while one was open for 1% of the time, Pallas kernels for 16%

profile of v3, /device:TPU:12, one launch (start us, length us, event | category | flops | bytes accessed | tf_op | source)
XLA Modules:
  0.0 73.4 jit_solution(6354067846901501253)
XLA Ops:
  0.0 0.1 collective-permute-start.14
  0.1 0.5 collective-permute-start.15
  0.6 0.9 %slice.4 = bf16[1,8,64,128]{3,2,1,0:T(8,128)(2,1)S(1)} slice(bf16[1,64,64,128]{3,2,1,0:T(8,128)(2,1)} %param.23), slice={[0:1], [32:40], [0:64], [0:128]} | slice | bytes 262144 | tf_op jit(solution)/shard_map/slice | solution.py:447
  1.5 2.7 %collective-permute-start.3 = (bf16[512,128]{1,0:T(8,128)(2,1)S(1)}, bf16[512,128]{1,0:T(8,128)(2,1)S(1)}, u32[]{:S(2)}, u32[]{:S(2)}) collective-permute-start(bf16[512,128]{1,0:T(8,128)(2,1)S(1)} %bitcast.13), channel_id=1, source_target_pairs={{0,8},{2,10},{4,12},{6,14},{8,0},{10,2},{12,4},{14,6},{1,9},{3,11}... | collective-permute-start | bytes 393224 | tf_op jit(solution)/shard_map/ppermute | solution.py:21
  4.2 0.3 collective-permute-start.8
  4.5 1.3 %cut_stage.1 = (bf16[512,128]{1,0:T(8,128)(2,1)S(1)}, bf16[512,128]{1,0:T(8,128)(2,1)S(1)}, bf16[512,128]{1,0:T(8,128)(2,1)S(1)}, bf16[512,128]{1,0:T(8,128)(2,1...) custom-call(bf16[8,512,128]{2,1,0:T(8,128)(2,1)} %bitcast.12, ...), custom_call_target="tpu_custom_call" | custom-call | tf_op jit(solution)/shard_map/cut_stage/pallas_call | solution.py:344
  5.8 0.5 collective-permute-start.7
  6.4 5.3 %collective-permute-done.8.refs_10_.refs_2_ = bf16[1,3,4608]{2,1,0:T(4,128)(2,1)S(1)} collective-permute-done((bf16[1,3,4608]{2,1,0:T(4,128)(2,1)}, bf16[1,3,4608]{2,1,0:T(4,128)(2,1)S(1)}, u32[]{:S(2)}, u32[]{:S(2)}) %collective-permute-start.8) | collective-permute-done | bytes 27680 | tf_op jit(solution)/shard_map/ppermute | solution.py:21
  11.6 1.2 %collective-permute-start.9 = (bf16[1,3,4608]{2,1,0:T(4,128)(2,1)S(1)}, bf16[1,3,4608]{2,1,0:T(4,128)(2,1)S(1)}, u32[]{:S(2)}, u32[]{:S(2)}) collective-permute-start(bf16[1,3,4608]{2,1,0:T(4,128)(2,1)S(1)} %collective-permute-done.8.refs_10_.refs_2_), channel_id=1, source_target_pairs={{0,4},{2,6},{4,0},{6,2},{8,12},{10,14},{12,8},{14,10},{1,5},{3,7},... | collective-permute-start | bytes 82952 | tf_op jit(solution)/shard_map/ppermute | solution.py:21
  12.8 0.0 collective-permute-done.7.refs_9_.refs_1_
  12.8 1.5 %collective-permute-start = (bf16[512,128]{1,0:T(8,128)(2,1)S(1)}, bf16[512,128]{1,0:T(8,128)(2,1)S(1)}, u32[]{:S(2)}, u32[]{:S(2)}) collective-permute-start(bf16[512,128]{1,0:T(8,128)(2,1)S(1)} %get-tuple-element.26), channel_id=1, source_target_pairs={{0,2},{2,0},{4,6},{6,4},{8,10},{10,8},{12,14},{14,12},{1,3},{3,1},... | collective-permute-start | bytes 393224 | tf_op jit(solution)/shard_map/ppermute | solution.py:21
  14.3 1.3 %collective-permute-done.9.refs_11_.refs_3_ = bf16[1,3,4608]{2,1,0:T(4,128)(2,1)S(1)} collective-permute-done((bf16[1,3,4608]{2,1,0:T(4,128)(2,1)S(1)}, bf16[1,3,4608]{2,1,0:T(4,128)(2,1)S(1)}, u32[]{:S(2)}, u32[]{:S(2)}) %collective-permute-start.9) | collective-permute-done | bytes 27680 | tf_op jit(solution)/shard_map/ppermute | solution.py:21
  15.6 1.2 %collective-permute-start.1 = (bf16[512,128]{1,0:T(8,128)(2,1)S(1)}, bf16[512,128]{1,0:T(8,128)(2,1)S(1)}, u32[]{:S(2)}, u32[]{:S(2)}) collective-permute-start(bf16[512,128]{1,0:T(8,128)(2,1)S(1)} %get-tuple-element.27), channel_id=1, source_target_pairs={{0,4},{2,6},{4,0},{6,2},{8,12},{10,14},{12,8},{14,10},{1,5},{3,7},... | collective-permute-start | bytes 393224 | tf_op jit(solution)/shard_map/ppermute | solution.py:21
  16.8 0.0 collective-permute-done.3.refs_4_
  16.8 1.7 %collective-permute-start.2 = (bf16[512,128]{1,0:T(8,128)(2,1)S(1)}, bf16[512,128]{1,0:T(8,128)(2,1)S(1)}, u32[]{:S(2)}, u32[]{:S(2)}) collective-permute-start(bf16[512,128]{1,0:T(8,128)(2,1)S(1)} %get-tuple-element.28), channel_id=1, source_target_pairs={{0,6},{2,4},{4,2},{6,0},{8,14},{10,12},{12,10},{14,8},{1,7},{3,5},... | collective-permute-start | bytes 393224 | tf_op jit(solution)/shard_map/ppermute | solution.py:21
  18.5 0.0 collective-permute-done.refs_1_
  18.5 3.3 %collective-permute-start.4 = (bf16[512,128]{1,0:T(8,128)(2,1)S(1)}, bf16[512,128]{1,0:T(8,128)(2,1)S(1)}, u32[]{:S(2)}, u32[]{:S(2)}) collective-permute-start(bf16[512,128]{1,0:T(8,128)(2,1)S(1)} %get-tuple-element.29), channel_id=1, source_target_pairs={{0,10},{2,8},{4,14},{6,12},{8,2},{10,0},{12,6},{14,4},{1,11},{3,9}... | collective-permute-start | bytes 393224 | tf_op jit(solution)/shard_map/ppermute | solution.py:21
  21.8 0.0 collective-permute-done.1.refs_2_
  21.8 2.2 %collective-permute-start.5 = (bf16[512,128]{1,0:T(8,128)(2,1)S(1)}, bf16[512,128]{1,0:T(8,128)(2,1)S(1)}, u32[]{:S(2)}, u32[]{:S(2)}) collective-permute-start(bf16[512,128]{1,0:T(8,128)(2,1)S(1)} %get-tuple-element.30), channel_id=1, source_target_pairs={{0,12},{2,14},{4,8},{6,10},{8,4},{10,6},{12,0},{14,2},{1,13},{3,15... | collective-permute-start | bytes 393224 | tf_op jit(solution)/shard_map/ppermute | solution.py:21
  24.1 0.8 %collective-permute-done.2.refs_3_ = bf16[512,128]{1,0:T(8,128)(2,1)S(1)} collective-permute-done((bf16[512,128]{1,0:T(8,128)(2,1)S(1)}, bf16[512,128]{1,0:T(8,128)(2,1)S(1)}, u32[]{:S(2)}, u32[]{:S(2)}) %collective-permute-start.2) | collective-permute-done | bytes 131104 | tf_op jit(solution)/shard_map/ppermute | solution.py:21
  24.8 3.2 %collective-permute-start.6 = (bf16[512,128]{1,0:T(8,128)(2,1)S(1)}, bf16[512,128]{1,0:T(8,128)(2,1)S(1)}, u32[]{:S(2)}, u32[]{:S(2)}) collective-permute-start(bf16[512,128]{1,0:T(8,128)(2,1)S(1)} %get-tuple-element.31), channel_id=1, source_target_pairs={{0,14},{2,12},{4,10},{6,8},{8,6},{10,4},{12,2},{14,0},{1,15},{3,13... | collective-permute-start | bytes 393224 | tf_op jit(solution)/shard_map/ppermute | solution.py:21
  29.3 0.0 copy-start.7
  29.3 0.6 copy-done.7
  30.0 0.6 plan_stage.1.plan
  30.6 1.1 %collective-permute-done.4.refs_5_ = bf16[512,128]{1,0:T(8,128)(2,1)S(1)} collective-permute-done((bf16[512,128]{1,0:T(8,128)(2,1)S(1)}, bf16[512,128]{1,0:T(8,128)(2,1)S(1)}, u32[]{:S(2)}, u32[]{:S(2)}) %collective-permute-start.4) | collective-permute-done | bytes 131104 | tf_op jit(solution)/shard_map/ppermute | solution.py:21
  31.6 4.8 %collective-permute-done.5.refs_6_ = bf16[512,128]{1,0:T(8,128)(2,1)S(1)} collective-permute-done((bf16[512,128]{1,0:T(8,128)(2,1)S(1)}, bf16[512,128]{1,0:T(8,128)(2,1)S(1)}, u32[]{:S(2)}, u32[]{:S(2)}) %collective-permute-start.5) | collective-permute-done | bytes 131104 | tf_op jit(solution)/shard_map/ppermute | solution.py:21
  36.5 2.3 %collective-permute-done.6.refs_7_ = bf16[512,128]{1,0:T(8,128)(2,1)S(1)} collective-permute-done((bf16[512,128]{1,0:T(8,128)(2,1)S(1)}, bf16[512,128]{1,0:T(8,128)(2,1)S(1)}, u32[]{:S(2)}, u32[]{:S(2)}) %collective-permute-start.6) | collective-permute-done | bytes 131104 | tf_op jit(solution)/shard_map/ppermute | solution.py:21
  38.8 0.5 pick_stage.1
  39.2 0.6 collective-permute-start.18
  39.8 0.0 collective-permute-start.19
  39.9 0.0 collective-permute-start.16
  39.9 1.2 %collective-permute-done.16.peer_dt = bf16[64,128]{1,0:T(8,128)(2,1)S(1)} collective-permute-done((bf16[64,128]{1,0:T(8,128)(2,1)S(1)}, bf16[64,128]{1,0:T(8,128)(2,1)S(1)}, u32[]{:S(2)}, u32[]{:S(2)}) %collective-permute-start.16) | collective-permute-done | bytes 16416 | tf_op jit(solution)/shard_map/ppermute | solution.py:21
  41.0 1.5 %collective-permute-start.17 = (bf16[1,3,4608]{2,1,0:T(4,128)(2,1)S(1)}, bf16[1,3,4608]{2,1,0:T(4,128)(2,1)S(1)}, u32[]{:S(2)}, u32[]{:S(2)}) collective-permute-start(bf16[1,3,4608]{2,1,0:T(4,128)(2,1)S(1)} %get-tuple-element.37), channel_id=1, source_target_pairs={{0,2},{2,0},{4,6},{6,4},{8,10},{10,8},{12,14},{14,12},{1,3},{3,1},... | collective-permute-start | bytes 82952 | tf_op jit(solution)/shard_map/ppermute | solution.py:21
  42.5 2.5 %collective-permute-done.17.refs_4_ = bf16[1,3,4608]{2,1,0:T(4,128)(2,1)S(1)} collective-permute-done((bf16[1,3,4608]{2,1,0:T(4,128)(2,1)S(1)}, bf16[1,3,4608]{2,1,0:T(4,128)(2,1)S(1)}, u32[]{:S(2)}, u32[]{:S(2)}) %collective-permute-start.17) | collective-permute-done | bytes 27680 | tf_op jit(solution)/shard_map/ppermute | solution.py:21
  45.1 2.9 %collective-permute-start.20 = (bf16[512,128]{1,0:T(8,128)(2,1)S(1)}, bf16[512,128]{1,0:T(8,128)(2,1)S(1)}, u32[]{:S(2)}, u32[]{:S(2)}) collective-permute-start(bf16[512,128]{1,0:T(8,128)(2,1)S(1)} %get-tuple-element.44), channel_id=1, source_target_pairs={{0,6},{2,4},{4,2},{6,0},{8,14},{10,12},{12,10},{14,8},{1,7},{3,5},... | collective-permute-start | bytes 393224 | tf_op jit(solution)/shard_map/ppermute | solution.py:21
  47.9 0.0 collective-permute-done.18.refs_1_
  47.9 1.1 %collective-permute-start.10 = (bf16[512,128]{1,0:T(8,128)(2,1)S(1)}, bf16[512,128]{1,0:T(8,128)(2,1)S(1)}, u32[]{:S(2)}, u32[]{:S(2)}) collective-permute-start(bf16[512,128]{1,0:T(8,128)(2,1)S(1)} %get-tuple-element.33), channel_id=1, source_target_pairs={{0,8},{2,10},{4,12},{6,14},{8,0},{10,2},{12,4},{14,6},{1,9},{3,11}... | collective-permute-start | bytes 393224 | tf_op jit(solution)/shard_map/ppermute | solution.py:21
  49.1 1.8 %collective-permute-start.11 = (bf16[512,128]{1,0:T(8,128)(2,1)S(1)}, bf16[512,128]{1,0:T(8,128)(2,1)S(1)}, u32[]{:S(2)}, u32[]{:S(2)}) collective-permute-start(bf16[512,128]{1,0:T(8,128)(2,1)S(1)} %get-tuple-element.34), channel_id=1, source_target_pairs={{0,10},{2,8},{4,14},{6,12},{8,2},{10,0},{12,6},{14,4},{1,11},{3,9}... | collective-permute-start | bytes 393224 | tf_op jit(solution)/shard_map/ppermute | solution.py:21
  50.9 1.7 %collective-permute-start.12 = (bf16[512,128]{1,0:T(8,128)(2,1)S(1)}, bf16[512,128]{1,0:T(8,128)(2,1)S(1)}, u32[]{:S(2)}, u32[]{:S(2)}) collective-permute-start(bf16[512,128]{1,0:T(8,128)(2,1)S(1)} %get-tuple-element.35), channel_id=1, source_target_pairs={{0,12},{2,14},{4,8},{6,10},{8,4},{10,6},{12,0},{14,2},{1,13},{3,15... | collective-permute-start | bytes 393224 | tf_op jit(solution)/shard_map/ppermute | solution.py:21
  52.6 1.2 %collective-permute-start.13 = (bf16[512,128]{1,0:T(8,128)(2,1)S(1)}, bf16[512,128]{1,0:T(8,128)(2,1)S(1)}, u32[]{:S(2)}, u32[]{:S(2)}) collective-permute-start(bf16[512,128]{1,0:T(8,128)(2,1)S(1)} %get-tuple-element.36), channel_id=1, source_target_pairs={{0,14},{2,12},{4,10},{6,8},{8,6},{10,4},{12,2},{14,0},{1,15},{3,13... | collective-permute-start | bytes 393224 | tf_op jit(solution)/shard_map/ppermute | solution.py:21
  53.8 0.0 copy-start.2
  53.8 8.5 %main_stage.1 = (f32[128,4096]{1,0:T(8,128)S(1)}, f32[128,4096]{1,0:T(8,128)S(1)}, bf16[128,256]{1,0:T(8,128)(2,1)S(1)}) custom-call(s32[12]{0:T(128)S(4)} %plan_stage.1.plan, f32[64]{0:T(128)S(1)} %copy-done.4, bf16[64,9216]{1,0:T(8,128)(2,1)} %own_bc.1, bf16[64,9216]{1,0:T(8,128)(2,1)S(1)} %collective-permute-done.14.peer_x.peer_bc, ...), custom_call_target="tpu_custom_call" | custom-call | flops 400000000 | bytes 8000000 | tf_op jit(solution)/shard_map/main_stage/pallas_call | solution.py:211
  62.3 1.3 %shard_map.136.refs_8_ = bf16[128,4096]{1,0:T(8,128)(2,1)} custom-call(s32[12]{0:T(128)S(4)} %plan_stage.1.plan, bf16[512,128]{1,0:T(8,128)(2,1)S(1)} %get-tuple-element.41.refs_0_, bf16[512,128]{1,0:T(8,128)(2,1)S(1)} %collective-permute-done.18.refs_1_, bf16[512,128]{1,0:T(8,128)(2,1)S(1)} %collective-permute-done.19.refs_2_, ...), custom_call_target="tpu_custom_call" | custom-call | flops 70000000 | bytes 3000000 | tf_op jit(solution)/shard_map/pallas_call | solution.py:299
  63.6 0.2 collective-permute-done.10.refs_0_
  63.8 2.8 %collective-permute-done.11.refs_1_ = bf16[512,128]{1,0:T(8,128)(2,1)S(1)} collective-permute-done((bf16[512,128]{1,0:T(8,128)(2,1)S(1)}, bf16[512,128]{1,0:T(8,128)(2,1)S(1)}, u32[]{:S(2)}, u32[]{:S(2)}) %collective-permute-start.11) | collective-permute-done | bytes 131104 | tf_op jit(solution)/shard_map/ppermute | solution.py:21
  66.6 3.5 %collective-permute-done.12.refs_2_ = bf16[512,128]{1,0:T(8,128)(2,1)S(1)} collective-permute-done((bf16[512,128]{1,0:T(8,128)(2,1)S(1)}, bf16[512,128]{1,0:T(8,128)(2,1)S(1)}, u32[]{:S(2)}, u32[]{:S(2)}) %collective-permute-start.12) | collective-permute-done | bytes 131104 | tf_op jit(solution)/shard_map/ppermute | solution.py:21
  70.2 1.9 %collective-permute-done.13.refs_3_ = bf16[512,128]{1,0:T(8,128)(2,1)S(1)} collective-permute-done((bf16[512,128]{1,0:T(8,128)(2,1)S(1)}, bf16[512,128]{1,0:T(8,128)(2,1)S(1)}, u32[]{:S(2)}, u32[]{:S(2)}) %collective-permute-start.13) | collective-permute-done | bytes 131104 | tf_op jit(solution)/shard_map/ppermute | solution.py:21
  72.1 1.3 %shard_map.137 = bf16[128,4096]{1,0:T(8,128)(2,1)} custom-call(s32[12]{0:T(128)S(4)} %plan_stage.1.plan, bf16[512,128]{1,0:T(8,128)(2,1)S(1)} %collective-permute-done.10.refs_0_, bf16[512,128]{1,0:T(8,128)(2,1)S(1)} %collective-permute-done.11.refs_1_, bf16[512,128]{1,0:T(8,128)(2,1)S(1)} %collective-permute-done.12.refs_2_, ...), custom_call_target="tpu_custom_call", output_to_operand_aliasing={{}: (9, {})} | custom-call | flops 70000000 | bytes 3000000 | tf_op jit(solution)/shard_map/pallas_call | solution.py:299
  (17 shorter events, 0.0 us)
Async XLA Ops:
  0.0 39.9 %copy-start.3 = (bf16[64,128]{1,0:T(8,128)(2,1)S(1)}, bf16[64,128]{1,0:T(8,128)(2,1)}, u32[]{:S(2)}) copy-start(bf16[64,128]{1,0:T(8,128)(2,1)} %own_dt.1) | copy-start | bytes 49156
  0.0 53.8 %copy-start.4 = (f32[64]{0:T(128)S(1)}, f32[64]{0:T(128)}, u32[]{:S(2)}) copy-start(f32[64]{0:T(128)} %skip_ref.1) | copy-start | bytes 772
  0.0 53.8 %copy-start.6 = (f32[64]{0:T(128)S(1)}, f32[64]{0:T(128)}, u32[]{:S(2)}) copy-start(f32[64]{0:T(128)} %param.20) | copy-start | bytes 772
  0.0 53.8 %copy-start.5 = (f32[64]{0:T(128)S(1)}, f32[64]{0:T(128)}, u32[]{:S(2)}) copy-start(f32[64]{0:T(128)} %param.19) | copy-start | bytes 772
  0.0 53.8 %copy-start.1 = (f32[9216]{0:T(1024)S(1)}, f32[9216]{0:T(1024)}, u32[]{:S(2)}) copy-start(f32[9216]{0:T(1024)} %param.18) | copy-start | bytes 110596
  0.0 53.8 %copy-start = (f32[4,9216]{1,0:T(4,128)S(1)}, f32[4,9216]{1,0:T(4,128)}, u32[]{:S(2)}) copy-start(f32[4,9216]{1,0:T(4,128)} %weight_bc.1) | copy-start | bytes 442372
  0.0 52.6 %collective-permute-start.14 = (bf16[64,9216]{1,0:T(8,128)(2,1)}, bf16[64,9216]{1,0:T(8,128)(2,1)S(1)}, u32[]{:S(2)}, u32[]{:S(2)}) collective-permute-start(bf16[64,9216]{1,0:T(8,128)(2,1)} %own_bc.1), channel_id=1, source_target_pairs={{0,1},{1,0},{2,3},{3,2},{4,5},{5,4},{6,7},{7,6},{8,9},{9,8},{10,11... | collective-permute-start | bytes 3538952 | tf_op jit(solution)/shard_map/ppermute | solution.py:21
  0.1 50.7 %collective-permute-start.15 = (bf16[64,8192]{1,0:T(8,128)(2,1)}, bf16[64,8192]{1,0:T(8,128)(2,1)S(1)}, u32[]{:S(2)}, u32[]{:S(2)}) collective-permute-start(bf16[64,8192]{1,0:T(8,128)(2,1)} %own_gate.1), channel_id=1, source_target_pairs={{0,1},{1,0},{2,3},{3,2},{4,5},{5,4},{6,7},{7,6},{8,9},{9,8},{10,11... | collective-permute-start | bytes 3145736 | tf_op jit(solution)/shard_map/ppermute | solution.py:21
  1.5 15.2 %collective-permute-start.3 = (bf16[512,128]{1,0:T(8,128)(2,1)S(1)}, bf16[512,128]{1,0:T(8,128)(2,1)S(1)}, u32[]{:S(2)}, u32[]{:S(2)}) collective-permute-start(bf16[512,128]{1,0:T(8,128)(2,1)S(1)} %bitcast.13), channel_id=1, source_target_pairs={{0,8},{2,10},{4,12},{6,14},{8,0},{10,2},{12,4},{14,6},{1,9},{3,11}... | collective-permute-start | bytes 393224 | tf_op jit(solution)/shard_map/ppermute | solution.py:21
  4.2 7.4 %collective-permute-start.8 = (bf16[1,3,4608]{2,1,0:T(4,128)(2,1)}, bf16[1,3,4608]{2,1,0:T(4,128)(2,1)S(1)}, u32[]{:S(2)}, u32[]{:S(2)}) collective-permute-start(bf16[1,3,4608]{2,1,0:T(4,128)(2,1)} %rims.1), channel_id=1, source_target_pairs={{0,8},{2,10},{4,12},{6,14},{8,0},{10,2},{12,4},{14,6},{1,9},{3,11}... | collective-permute-start | bytes 82952 | tf_op jit(solution)/shard_map/ppermute | solution.py:21
  5.8 7.0 %collective-permute-start.7 = (bf16[1,3,4608]{2,1,0:T(4,128)(2,1)S(1)}, bf16[1,3,4608]{2,1,0:T(4,128)(2,1)S(1)}, u32[]{:S(2)}, u32[]{:S(2)}) collective-permute-start(bf16[1,3,4608]{2,1,0:T(4,128)(2,1)S(1)} %get-tuple-element.32.refs_8_.refs_0_), channel_id=1, source_target_pairs={{0,4},{2,6},{4,0},{6,2},{8,12},{10,14},{12,8},{14,10},{1,5},{3,7},... | collective-permute-start | bytes 82952 | tf_op jit(solution)/shard_map/ppermute | solution.py:21
  11.6 4.0 %collective-permute-start.9 = (bf16[1,3,4608]{2,1,0:T(4,128)(2,1)S(1)}, bf16[1,3,4608]{2,1,0:T(4,128)(2,1)S(1)}, u32[]{:S(2)}, u32[]{:S(2)}) collective-permute-start(bf16[1,3,4608]{2,1,0:T(4,128)(2,1)S(1)} %collective-permute-done.8.refs_10_.refs_2_), channel_id=1, source_target_pairs={{0,4},{2,6},{4,0},{6,2},{8,12},{10,14},{12,8},{14,10},{1,5},{3,7},... | collective-permute-start | bytes 82952 | tf_op jit(solution)/shard_map/ppermute | solution.py:21
  12.8 5.7 %collective-permute-start = (bf16[512,128]{1,0:T(8,128)(2,1)S(1)}, bf16[512,128]{1,0:T(8,128)(2,1)S(1)}, u32[]{:S(2)}, u32[]{:S(2)}) collective-permute-start(bf16[512,128]{1,0:T(8,128)(2,1)S(1)} %get-tuple-element.26), channel_id=1, source_target_pairs={{0,2},{2,0},{4,6},{6,4},{8,10},{10,8},{12,14},{14,12},{1,3},{3,1},... | collective-permute-start | bytes 393224 | tf_op jit(solution)/shard_map/ppermute | solution.py:21
  15.6 6.3 %collective-permute-start.1 = (bf16[512,128]{1,0:T(8,128)(2,1)S(1)}, bf16[512,128]{1,0:T(8,128)(2,1)S(1)}, u32[]{:S(2)}, u32[]{:S(2)}) collective-permute-start(bf16[512,128]{1,0:T(8,128)(2,1)S(1)} %get-tuple-element.27), channel_id=1, source_target_pairs={{0,4},{2,6},{4,0},{6,2},{8,12},{10,14},{12,8},{14,10},{1,5},{3,7},... | collective-permute-start | bytes 393224 | tf_op jit(solution)/shard_map/ppermute | solution.py:21
  16.8 8.0 %collective-permute-start.2 = (bf16[512,128]{1,0:T(8,128)(2,1)S(1)}, bf16[512,128]{1,0:T(8,128)(2,1)S(1)}, u32[]{:S(2)}, u32[]{:S(2)}) collective-permute-start(bf16[512,128]{1,0:T(8,128)(2,1)S(1)} %get-tuple-element.28), channel_id=1, source_target_pairs={{0,6},{2,4},{4,2},{6,0},{8,14},{10,12},{12,10},{14,8},{1,7},{3,5},... | collective-permute-start | bytes 393224 | tf_op jit(solution)/shard_map/ppermute | solution.py:21
  18.5 13.1 %collective-permute-start.4 = (bf16[512,128]{1,0:T(8,128)(2,1)S(1)}, bf16[512,128]{1,0:T(8,128)(2,1)S(1)}, u32[]{:S(2)}, u32[]{:S(2)}) collective-permute-start(bf16[512,128]{1,0:T(8,128)(2,1)S(1)} %get-tuple-element.29), channel_id=1, source_target_pairs={{0,10},{2,8},{4,14},{6,12},{8,2},{10,0},{12,6},{14,4},{1,11},{3,9}... | collective-permute-start | bytes 393224 | tf_op jit(solution)/shard_map/ppermute | solution.py:21
  21.8 14.6 %collective-permute-start.5 = (bf16[512,128]{1,0:T(8,128)(2,1)S(1)}, bf16[512,128]{1,0:T(8,128)(2,1)S(1)}, u32[]{:S(2)}, u32[]{:S(2)}) collective-permute-start(bf16[512,128]{1,0:T(8,128)(2,1)S(1)} %get-tuple-element.30), channel_id=1, source_target_pairs={{0,12},{2,14},{4,8},{6,10},{8,4},{10,6},{12,0},{14,2},{1,13},{3,15... | collective-permute-start | bytes 393224 | tf_op jit(solution)/shard_map/ppermute | solution.py:21
  24.8 14.0 %collective-permute-start.6 = (bf16[512,128]{1,0:T(8,128)(2,1)S(1)}, bf16[512,128]{1,0:T(8,128)(2,1)S(1)}, u32[]{:S(2)}, u32[]{:S(2)}) collective-permute-start(bf16[512,128]{1,0:T(8,128)(2,1)S(1)} %get-tuple-element.31), channel_id=1, source_target_pairs={{0,14},{2,12},{4,10},{6,8},{8,6},{10,4},{12,2},{14,0},{1,15},{3,13... | collective-permute-start | bytes 393224 | tf_op jit(solution)/shard_map/ppermute | solution.py:21
  29.3 0.7 copy-start.7
  39.2 8.7 %collective-permute-start.18 = (bf16[512,128]{1,0:T(8,128)(2,1)S(1)}, bf16[512,128]{1,0:T(8,128)(2,1)S(1)}, u32[]{:S(2)}, u32[]{:S(2)}) collective-permute-start(bf16[512,128]{1,0:T(8,128)(2,1)S(1)} %get-tuple-element.42), channel_id=1, source_target_pairs={{0,2},{2,0},{4,6},{6,4},{8,10},{10,8},{12,14},{14,12},{1,3},{3,1},... | collective-permute-start | bytes 393224 | tf_op jit(solution)/shard_map/ppermute | solution.py:21
  39.8 9.2 %collective-permute-start.19 = (bf16[512,128]{1,0:T(8,128)(2,1)S(1)}, bf16[512,128]{1,0:T(8,128)(2,1)S(1)}, u32[]{:S(2)}, u32[]{:S(2)}) collective-permute-start(bf16[512,128]{1,0:T(8,128)(2,1)S(1)} %get-tuple-element.43), channel_id=1, source_target_pairs={{0,4},{2,6},{4,0},{6,2},{8,12},{10,14},{12,8},{14,10},{1,5},{3,7},... | collective-permute-start | bytes 393224 | tf_op jit(solution)/shard_map/ppermute | solution.py:21
  39.9 1.2 %collective-permute-start.16 = (bf16[64,128]{1,0:T(8,128)(2,1)S(1)}, bf16[64,128]{1,0:T(8,128)(2,1)S(1)}, u32[]{:S(2)}, u32[]{:S(2)}) collective-permute-start(bf16[64,128]{1,0:T(8,128)(2,1)S(1)} %copy-done.3), channel_id=1, source_target_pairs={{0,1},{1,0},{2,3},{3,2},{4,5},{5,4},{6,7},{7,6},{8,9},{9,8},{10,11... | collective-permute-start | bytes 49160 | tf_op jit(solution)/shard_map/ppermute | solution.py:21
  41.0 4.0 %collective-permute-start.17 = (bf16[1,3,4608]{2,1,0:T(4,128)(2,1)S(1)}, bf16[1,3,4608]{2,1,0:T(4,128)(2,1)S(1)}, u32[]{:S(2)}, u32[]{:S(2)}) collective-permute-start(bf16[1,3,4608]{2,1,0:T(4,128)(2,1)S(1)} %get-tuple-element.37), channel_id=1, source_target_pairs={{0,2},{2,0},{4,6},{6,4},{8,10},{10,8},{12,14},{14,12},{1,3},{3,1},... | collective-permute-start | bytes 82952 | tf_op jit(solution)/shard_map/ppermute | solution.py:21
  45.1 17.3 %collective-permute-start.20 = (bf16[512,128]{1,0:T(8,128)(2,1)S(1)}, bf16[512,128]{1,0:T(8,128)(2,1)S(1)}, u32[]{:S(2)}, u32[]{:S(2)}) collective-permute-start(bf16[512,128]{1,0:T(8,128)(2,1)S(1)} %get-tuple-element.44), channel_id=1, source_target_pairs={{0,6},{2,4},{4,2},{6,0},{8,14},{10,12},{12,10},{14,8},{1,7},{3,5},... | collective-permute-start | bytes 393224 | tf_op jit(solution)/shard_map/ppermute | solution.py:21
  47.9 15.9 %collective-permute-start.10 = (bf16[512,128]{1,0:T(8,128)(2,1)S(1)}, bf16[512,128]{1,0:T(8,128)(2,1)S(1)}, u32[]{:S(2)}, u32[]{:S(2)}) collective-permute-start(bf16[512,128]{1,0:T(8,128)(2,1)S(1)} %get-tuple-element.33), channel_id=1, source_target_pairs={{0,8},{2,10},{4,12},{6,14},{8,0},{10,2},{12,4},{14,6},{1,9},{3,11}... | collective-permute-start | bytes 393224 | tf_op jit(solution)/shard_map/ppermute | solution.py:21
  49.1 17.5 %collective-permute-start.11 = (bf16[512,128]{1,0:T(8,128)(2,1)S(1)}, bf16[512,128]{1,0:T(8,128)(2,1)S(1)}, u32[]{:S(2)}, u32[]{:S(2)}) collective-permute-start(bf16[512,128]{1,0:T(8,128)(2,1)S(1)} %get-tuple-element.34), channel_id=1, source_target_pairs={{0,10},{2,8},{4,14},{6,12},{8,2},{10,0},{12,6},{14,4},{1,11},{3,9}... | collective-permute-start | bytes 393224 | tf_op jit(solution)/shard_map/ppermute | solution.py:21
  50.9 19.3 %collective-permute-start.12 = (bf16[512,128]{1,0:T(8,128)(2,1)S(1)}, bf16[512,128]{1,0:T(8,128)(2,1)S(1)}, u32[]{:S(2)}, u32[]{:S(2)}) collective-permute-start(bf16[512,128]{1,0:T(8,128)(2,1)S(1)} %get-tuple-element.35), channel_id=1, source_target_pairs={{0,12},{2,14},{4,8},{6,10},{8,4},{10,6},{12,0},{14,2},{1,13},{3,15... | collective-permute-start | bytes 393224 | tf_op jit(solution)/shard_map/ppermute | solution.py:21
  52.6 19.5 %collective-permute-start.13 = (bf16[512,128]{1,0:T(8,128)(2,1)S(1)}, bf16[512,128]{1,0:T(8,128)(2,1)S(1)}, u32[]{:S(2)}, u32[]{:S(2)}) collective-permute-start(bf16[512,128]{1,0:T(8,128)(2,1)S(1)} %get-tuple-element.36), channel_id=1, source_target_pairs={{0,14},{2,12},{4,10},{6,8},{8,6},{10,4},{12,2},{14,0},{1,15},{3,13... | collective-permute-start | bytes 393224 | tf_op jit(solution)/shard_map/ppermute | solution.py:21
  53.8 8.5 %copy-start.2 = (f32[4096]{0:T(1024)S(1)}, f32[4096]{0:T(1024)}, u32[]{:S(2)}) copy-start(f32[4096]{0:T(1024)} %param.22) | copy-start | bytes 49156

commit v4 on v3

--- a/solution.py
+++ b/solution.py
@@ -393,12 +393,14 @@
 def column_rims(conv_store, own_rims):
     count = lax.axis_size("dp")
     held = {0: conv_store}
+    step = count - 2
     bit = count // 2
     while bit > 1:
         for k in sorted(held):
-            held[k ^ bit] = swap(held[k], "dp", bit)
+            held[k ^ step] = swap(held[k], "dp", step)
         held[0] = own_rims
         bit //= 2
+        step = bit
     return [held[2 * i] for i in range(count // 2)]
 
 
@@ -441,7 +443,8 @@
     state = ssm_store.reshape(owners, -1, STATE)
     if direct:
         held = [None] * owners
-        every = order + [0]
+        opening = owners - 2
+        every = [opening] + [k for k in order if k != opening] + [0]
         *pieces, own_rims = cut_stage(state, conv_store, every[1:])
         column = column_rims(conv_store, own_rims)
         for k, piece in zip(every, [state[every[0]]] + pieces):

time: 73.9 us -> 71.6 us (0.969)
  the two profiles are of different devices: /device:TPU:12 before, /device:TPU:8 now
where the time goes in v4:
time: 71.6 us; the launch traced here: 71.1 us
  waiting for transfers between devices  28.7 us (40%)
  starting transfers between devices  26 us (36%)
  Pallas kernels  13.4 us (19%)
  local copies, waits for them, and re-layouts  1.59 us (2%)
  between operations  1.46 us (2%)
    ppermute x21, waiting for transfers between devices, swap(): return lax.ppermute(value, axis, [(i, i ^ offset) for i in range(count)])  28.7 us
    ppermute x21, starting transfers between devices, swap(): return lax.ppermute(value, axis, [(i, i ^ offset) for i in range(count)])  26 us
    pallas_call x1, Pallas kernels, main_stage(): pl.pallas_call(functools.partial(main_kernel, len(rims)), grid_spec=grid_...  8.47 us
    pallas_call x2, Pallas kernels, tail_stage(): pl.pallas_call(functools.partial(tail_kernel, base, len(earlier)), grid_s...  2.6 us
  transfers between devices with their start and end apart: 21, of which 11 were waited for; matrix products, arithmetic and copies ran while one was open for 1% of the time, Pallas kernels for 17%

profile of v4, /device:TPU:8, one launch (start us, length us, event | category | flops | bytes accessed | tf_op | source)
XLA Modules:
  0.0 71.1 jit_solution(10199160892680218354)
XLA Ops:
  0.0 0.1 collective-permute-start.14
  0.1 0.5 collective-permute-start.15
  0.6 0.9 %slice.4 = bf16[1,8,64,128]{3,2,1,0:T(8,128)(2,1)S(1)} slice(bf16[1,64,64,128]{3,2,1,0:T(8,128)(2,1)} %param.23), slice={[0:1], [48:56], [0:64], [0:128]} | slice | bytes 262144 | tf_op jit(solution)/shard_map/slice | solution.py:450
  1.5 1.6 %collective-permute-start.5 = (bf16[512,128]{1,0:T(8,128)(2,1)S(1)}, bf16[512,128]{1,0:T(8,128)(2,1)S(1)}, u32[]{:S(2)}, u32[]{:S(2)}) collective-permute-start(bf16[512,128]{1,0:T(8,128)(2,1)S(1)} %bitcast.13), channel_id=1, source_target_pairs={{0,12},{2,14},{4,8},{6,10},{8,4},{10,6},{12,0},{14,2},{1,13},{3,15... | collective-permute-start | bytes 393224 | tf_op jit(solution)/shard_map/ppermute | solution.py:21
  3.2 0.4 collective-permute-start.8
  3.6 1.3 %cut_stage.1 = (bf16[512,128]{1,0:T(8,128)(2,1)S(1)}, bf16[512,128]{1,0:T(8,128)(2,1)S(1)}, bf16[512,128]{1,0:T(8,128)(2,1)S(1)}, bf16[512,128]{1,0:T(8,128)(2,1...) custom-call(bf16[8,512,128]{2,1,0:T(8,128)(2,1)} %bitcast.12, ...), custom_call_target="tpu_custom_call" | custom-call | tf_op jit(solution)/shard_map/cut_stage/pallas_call | solution.py:344
  4.9 2.2 %collective-permute-start.7 = (bf16[1,3,4608]{2,1,0:T(4,128)(2,1)S(1)}, bf16[1,3,4608]{2,1,0:T(4,128)(2,1)S(1)}, u32[]{:S(2)}, u32[]{:S(2)}) collective-permute-start(bf16[1,3,4608]{2,1,0:T(4,128)(2,1)S(1)} %get-tuple-element.32.refs_8_.refs_0_), channel_id=1, source_target_pairs={{0,4},{2,6},{4,0},{6,2},{8,12},{10,14},{12,8},{14,10},{1,5},{3,7},... | collective-permute-start | bytes 82952 | tf_op jit(solution)/shard_map/ppermute | solution.py:21
  7.1 4.4 %collective-permute-done.8.refs_11_.refs_3_ = bf16[1,3,4608]{2,1,0:T(4,128)(2,1)S(1)} collective-permute-done((bf16[1,3,4608]{2,1,0:T(4,128)(2,1)}, bf16[1,3,4608]{2,1,0:T(4,128)(2,1)S(1)}, u32[]{:S(2)}, u32[]{:S(2)}) %collective-permute-start.8) | collective-permute-done | bytes 27680 | tf_op jit(solution)/shard_map/ppermute | solution.py:21
  11.5 0.5 collective-permute-start.9
  12.0 0.0 collective-permute-done.7.refs_9_.refs_1_
  12.0 1.5 %collective-permute-start = (bf16[512,128]{1,0:T(8,128)(2,1)S(1)}, bf16[512,128]{1,0:T(8,128)(2,1)S(1)}, u32[]{:S(2)}, u32[]{:S(2)}) collective-permute-start(bf16[512,128]{1,0:T(8,128)(2,1)S(1)} %get-tuple-element.26), channel_id=1, source_target_pairs={{0,2},{2,0},{4,6},{6,4},{8,10},{10,8},{12,14},{14,12},{1,3},{3,1},... | collective-permute-start | bytes 393224 | tf_op jit(solution)/shard_map/ppermute | solution.py:21
  13.5 1.9 %collective-permute-done.9.refs_10_.refs_2_ = bf16[1,3,4608]{2,1,0:T(4,128)(2,1)S(1)} collective-permute-done((bf16[1,3,4608]{2,1,0:T(4,128)(2,1)S(1)}, bf16[1,3,4608]{2,1,0:T(4,128)(2,1)S(1)}, u32[]{:S(2)}, u32[]{:S(2)}) %collective-permute-start.9) | collective-permute-done | bytes 27680 | tf_op jit(solution)/shard_map/ppermute | solution.py:21
  15.4 0.5 collective-permute-start.1
  16.0 0.0 collective-permute-done.5.refs_6_
  16.0 2.4 %collective-permute-start.2 = (bf16[512,128]{1,0:T(8,128)(2,1)S(1)}, bf16[512,128]{1,0:T(8,128)(2,1)S(1)}, u32[]{:S(2)}, u32[]{:S(2)}) collective-permute-start(bf16[512,128]{1,0:T(8,128)(2,1)S(1)} %get-tuple-element.28), channel_id=1, source_target_pairs={{0,6},{2,4},{4,2},{6,0},{8,14},{10,12},{12,10},{14,8},{1,7},{3,5},... | collective-permute-start | bytes 393224 | tf_op jit(solution)/shard_map/ppermute | solution.py:21
  18.4 0.0 collective-permute-done.refs_1_
  18.4 1.2 %collective-permute-start.3 = (bf16[512,128]{1,0:T(8,128)(2,1)S(1)}, bf16[512,128]{1,0:T(8,128)(2,1)S(1)}, u32[]{:S(2)}, u32[]{:S(2)}) collective-permute-start(bf16[512,128]{1,0:T(8,128)(2,1)S(1)} %get-tuple-element.29), channel_id=1, source_target_pairs={{0,8},{2,10},{4,12},{6,14},{8,0},{10,2},{12,4},{14,6},{1,9},{3,11}... | collective-permute-start | bytes 393224 | tf_op jit(solution)/shard_map/ppermute | solution.py:21
  19.6 1.7 %collective-permute-done.1.refs_2_ = bf16[512,128]{1,0:T(8,128)(2,1)S(1)} collective-permute-done((bf16[512,128]{1,0:T(8,128)(2,1)S(1)}, bf16[512,128]{1,0:T(8,128)(2,1)S(1)}, u32[]{:S(2)}, u32[]{:S(2)}) %collective-permute-start.1) | collective-permute-done | bytes 131104 | tf_op jit(solution)/shard_map/ppermute | solution.py:21
  21.3 2.6 %collective-permute-start.4 = (bf16[512,128]{1,0:T(8,128)(2,1)S(1)}, bf16[512,128]{1,0:T(8,128)(2,1)S(1)}, u32[]{:S(2)}, u32[]{:S(2)}) collective-permute-start(bf16[512,128]{1,0:T(8,128)(2,1)S(1)} %get-tuple-element.30), channel_id=1, source_target_pairs={{0,10},{2,8},{4,14},{6,12},{8,2},{10,0},{12,6},{14,4},{1,11},{3,9}... | collective-permute-start | bytes 393224 | tf_op jit(solution)/shard_map/ppermute | solution.py:21
  23.9 1.7 %collective-permute-done.2.refs_3_ = bf16[512,128]{1,0:T(8,128)(2,1)S(1)} collective-permute-done((bf16[512,128]{1,0:T(8,128)(2,1)S(1)}, bf16[512,128]{1,0:T(8,128)(2,1)S(1)}, u32[]{:S(2)}, u32[]{:S(2)}) %collective-permute-start.2) | collective-permute-done | bytes 131104 | tf_op jit(solution)/shard_map/ppermute | solution.py:21
  25.5 1.5 %collective-permute-start.6 = (bf16[512,128]{1,0:T(8,128)(2,1)S(1)}, bf16[512,128]{1,0:T(8,128)(2,1)S(1)}, u32[]{:S(2)}, u32[]{:S(2)}) collective-permute-start(bf16[512,128]{1,0:T(8,128)(2,1)S(1)} %get-tuple-element.31), channel_id=1, source_target_pairs={{0,14},{2,12},{4,10},{6,8},{8,6},{10,4},{12,2},{14,0},{1,15},{3,13... | collective-permute-start | bytes 393224 | tf_op jit(solution)/shard_map/ppermute | solution.py:21
  28.4 0.0 copy-start.7
  28.4 0.6 copy-done.7
  29.0 0.6 plan_stage.1.plan
  29.6 3.7 %collective-permute-done.4.refs_5_ = bf16[512,128]{1,0:T(8,128)(2,1)S(1)} collective-permute-done((bf16[512,128]{1,0:T(8,128)(2,1)S(1)}, bf16[512,128]{1,0:T(8,128)(2,1)S(1)}, u32[]{:S(2)}, u32[]{:S(2)}) %collective-permute-start.4) | collective-permute-done | bytes 131104 | tf_op jit(solution)/shard_map/ppermute | solution.py:21
  33.3 3.4 %collective-permute-done.6.refs_7_ = bf16[512,128]{1,0:T(8,128)(2,1)S(1)} collective-permute-done((bf16[512,128]{1,0:T(8,128)(2,1)S(1)}, bf16[512,128]{1,0:T(8,128)(2,1)S(1)}, u32[]{:S(2)}, u32[]{:S(2)}) %collective-permute-start.6) | collective-permute-done | bytes 131104 | tf_op jit(solution)/shard_map/ppermute | solution.py:21
  36.6 0.5 pick_stage.1
  37.1 0.7 collective-permute-start.18
  37.8 0.0 collective-permute-start.19
  37.8 0.0 collective-permute-start.16
  37.8 1.2 %collective-permute-done.16.peer_dt = bf16[64,128]{1,0:T(8,128)(2,1)S(1)} collective-permute-done((bf16[64,128]{1,0:T(8,128)(2,1)S(1)}, bf16[64,128]{1,0:T(8,128)(2,1)S(1)}, u32[]{:S(2)}, u32[]{:S(2)}) %collective-permute-start.16) | collective-permute-done | bytes 16416 | tf_op jit(solution)/shard_map/ppermute | solution.py:21
  39.0 1.4 %collective-permute-start.17 = (bf16[1,3,4608]{2,1,0:T(4,128)(2,1)S(1)}, bf16[1,3,4608]{2,1,0:T(4,128)(2,1)S(1)}, u32[]{:S(2)}, u32[]{:S(2)}) collective-permute-start(bf16[1,3,4608]{2,1,0:T(4,128)(2,1)S(1)} %get-tuple-element.37), channel_id=1, source_target_pairs={{0,2},{2,0},{4,6},{6,4},{8,10},{10,8},{12,14},{14,12},{1,3},{3,1},... | collective-permute-start | bytes 82952 | tf_op jit(solution)/shard_map/ppermute | solution.py:21
  40.4 2.6 %collective-permute-done.17.refs_4_ = bf16[1,3,4608]{2,1,0:T(4,128)(2,1)S(1)} collective-permute-done((bf16[1,3,4608]{2,1,0:T(4,128)(2,1)S(1)}, bf16[1,3,4608]{2,1,0:T(4,128)(2,1)S(1)}, u32[]{:S(2)}, u32[]{:S(2)}) %collective-permute-start.17) | collective-permute-done | bytes 27680 | tf_op jit(solution)/shard_map/ppermute | solution.py:21
  43.0 2.8 %collective-permute-start.20 = (bf16[512,128]{1,0:T(8,128)(2,1)S(1)}, bf16[512,128]{1,0:T(8,128)(2,1)S(1)}, u32[]{:S(2)}, u32[]{:S(2)}) collective-permute-start(bf16[512,128]{1,0:T(8,128)(2,1)S(1)} %get-tuple-element.44), channel_id=1, source_target_pairs={{0,6},{2,4},{4,2},{6,0},{8,14},{10,12},{12,10},{14,8},{1,7},{3,5},... | collective-permute-start | bytes 393224 | tf_op jit(solution)/shard_map/ppermute | solution.py:21
  45.8 0.0 collective-permute-done.18.refs_1_
  45.8 0.6 collective-permute-start.10
  46.4 2.4 %collective-permute-start.11 = (bf16[512,128]{1,0:T(8,128)(2,1)S(1)}, bf16[512,128]{1,0:T(8,128)(2,1)S(1)}, u32[]{:S(2)}, u32[]{:S(2)}) collective-permute-start(bf16[512,128]{1,0:T(8,128)(2,1)S(1)} %get-tuple-element.34), channel_id=1, source_target_pairs={{0,10},{2,8},{4,14},{6,12},{8,2},{10,0},{12,6},{14,4},{1,11},{3,9}... | collective-permute-start | bytes 393224 | tf_op jit(solution)/shard_map/ppermute | solution.py:21
  48.8 1.4 %collective-permute-start.12 = (bf16[512,128]{1,0:T(8,128)(2,1)S(1)}, bf16[512,128]{1,0:T(8,128)(2,1)S(1)}, u32[]{:S(2)}, u32[]{:S(2)}) collective-permute-start(bf16[512,128]{1,0:T(8,128)(2,1)S(1)} %get-tuple-element.35), channel_id=1, source_target_pairs={{0,12},{2,14},{4,8},{6,10},{8,4},{10,6},{12,0},{14,2},{1,13},{3,15... | collective-permute-start | bytes 393224 | tf_op jit(solution)/shard_map/ppermute | solution.py:21
  50.2 0.0 collective-permute-done.14.peer_x.peer_bc
  50.2 1.5 %collective-permute-start.13 = (bf16[512,128]{1,0:T(8,128)(2,1)S(1)}, bf16[512,128]{1,0:T(8,128)(2,1)S(1)}, u32[]{:S(2)}, u32[]{:S(2)}) collective-permute-start(bf16[512,128]{1,0:T(8,128)(2,1)S(1)} %get-tuple-element.36), channel_id=1, source_target_pairs={{0,14},{2,12},{4,10},{6,8},{8,6},{10,4},{12,2},{14,0},{1,15},{3,13... | collective-permute-start | bytes 393224 | tf_op jit(solution)/shard_map/ppermute | solution.py:21
  51.7 0.0 copy-start.2
  51.7 8.5 %main_stage.1 = (f32[128,4096]{1,0:T(8,128)S(1)}, f32[128,4096]{1,0:T(8,128)S(1)}, bf16[128,256]{1,0:T(8,128)(2,1)S(1)}) custom-call(s32[12]{0:T(128)S(4)} %plan_stage.1.plan, f32[64]{0:T(128)S(1)} %copy-done.4, bf16[64,9216]{1,0:T(8,128)(2,1)} %own_bc.1, bf16[64,9216]{1,0:T(8,128)(2,1)S(1)} %collective-permute-done.14.peer_x.peer_bc, ...), custom_call_target="tpu_custom_call" | custom-call | flops 400000000 | bytes 8000000 | tf_op jit(solution)/shard_map/main_stage/pallas_call | solution.py:211
  60.2 1.3 %shard_map.136.refs_8_ = bf16[128,4096]{1,0:T(8,128)(2,1)} custom-call(s32[12]{0:T(128)S(4)} %plan_stage.1.plan, bf16[512,128]{1,0:T(8,128)(2,1)S(1)} %get-tuple-element.41.refs_0_, bf16[512,128]{1,0:T(8,128)(2,1)S(1)} %collective-permute-done.18.refs_1_, bf16[512,128]{1,0:T(8,128)(2,1)S(1)} %collective-permute-done.19.refs_2_, ...), custom_call_target="tpu_custom_call" | custom-call | flops 70000000 | bytes 3000000 | tf_op jit(solution)/shard_map/pallas_call | solution.py:299
  61.5 0.0 collective-permute-done.10.refs_0_
  61.5 2.4 %collective-permute-done.11.refs_1_ = bf16[512,128]{1,0:T(8,128)(2,1)S(1)} collective-permute-done((bf16[512,128]{1,0:T(8,128)(2,1)S(1)}, bf16[512,128]{1,0:T(8,128)(2,1)S(1)}, u32[]{:S(2)}, u32[]{:S(2)}) %collective-permute-start.11) | collective-permute-done | bytes 131104 | tf_op jit(solution)/shard_map/ppermute | solution.py:21
  63.9 4.0 %collective-permute-done.12.refs_2_ = bf16[512,128]{1,0:T(8,128)(2,1)S(1)} collective-permute-done((bf16[512,128]{1,0:T(8,128)(2,1)S(1)}, bf16[512,128]{1,0:T(8,128)(2,1)S(1)}, u32[]{:S(2)}, u32[]{:S(2)}) %collective-permute-start.12) | collective-permute-done | bytes 131104 | tf_op jit(solution)/shard_map/ppermute | solution.py:21
  67.9 1.9 %collective-permute-done.13.refs_3_ = bf16[512,128]{1,0:T(8,128)(2,1)S(1)} collective-permute-done((bf16[512,128]{1,0:T(8,128)(2,1)S(1)}, bf16[512,128]{1,0:T(8,128)(2,1)S(1)}, u32[]{:S(2)}, u32[]{:S(2)}) %collective-permute-start.13) | collective-permute-done | bytes 131104 | tf_op jit(solution)/shard_map/ppermute | solution.py:21
  69.8 1.3 %shard_map.137 = bf16[128,4096]{1,0:T(8,128)(2,1)} custom-call(s32[12]{0:T(128)S(4)} %plan_stage.1.plan, bf16[512,128]{1,0:T(8,128)(2,1)S(1)} %collective-permute-done.10.refs_0_, bf16[512,128]{1,0:T(8,128)(2,1)S(1)} %collective-permute-done.11.refs_1_, bf16[512,128]{1,0:T(8,128)(2,1)S(1)} %collective-permute-done.12.refs_2_, ...), custom_call_target="tpu_custom_call", output_to_operand_aliasing={{}: (9, {})} | custom-call | flops 70000000 | bytes 3000000 | tf_op jit(solution)/shard_map/pallas_call | solution.py:299
  (17 shorter events, 0.0 us)
Async XLA Ops:
  0.0 37.8 %copy-start.3 = (bf16[64,128]{1,0:T(8,128)(2,1)S(1)}, bf16[64,128]{1,0:T(8,128)(2,1)}, u32[]{:S(2)}) copy-start(bf16[64,128]{1,0:T(8,128)(2,1)} %own_dt.1) | copy-start | bytes 49156
  0.0 51.7 %copy-start.4 = (f32[64]{0:T(128)S(1)}, f32[64]{0:T(128)}, u32[]{:S(2)}) copy-start(f32[64]{0:T(128)} %skip_ref.1) | copy-start | bytes 772
  0.0 51.7 %copy-start.6 = (f32[64]{0:T(128)S(1)}, f32[64]{0:T(128)}, u32[]{:S(2)}) copy-start(f32[64]{0:T(128)} %param.20) | copy-start | bytes 772
  0.0 51.7 %copy-start.5 = (f32[64]{0:T(128)S(1)}, f32[64]{0:T(128)}, u32[]{:S(2)}) copy-start(f32[64]{0:T(128)} %param.19) | copy-start | bytes 772
  0.0 51.7 %copy-start.1 = (f32[9216]{0:T(1024)S(1)}, f32[9216]{0:T(1024)}, u32[]{:S(2)}) copy-start(f32[9216]{0:T(1024)} %param.18) | copy-start | bytes 110596
  0.0 51.6 %copy-start = (f32[4,9216]{1,0:T(4,128)S(1)}, f32[4,9216]{1,0:T(4,128)}, u32[]{:S(2)}) copy-start(f32[4,9216]{1,0:T(4,128)} %weight_bc.1) | copy-start | bytes 442372
  0.0 50.1 %collective-permute-start.14 = (bf16[64,9216]{1,0:T(8,128)(2,1)}, bf16[64,9216]{1,0:T(8,128)(2,1)S(1)}, u32[]{:S(2)}, u32[]{:S(2)}) collective-permute-start(bf16[64,9216]{1,0:T(8,128)(2,1)} %own_bc.1), channel_id=1, source_target_pairs={{0,1},{1,0},{2,3},{3,2},{4,5},{5,4},{6,7},{7,6},{8,9},{9,8},{10,11... | collective-permute-start | bytes 3538952 | tf_op jit(solution)/shard_map/ppermute | solution.py:21
  0.1 48.7 %collective-permute-start.15 = (bf16[64,8192]{1,0:T(8,128)(2,1)}, bf16[64,8192]{1,0:T(8,128)(2,1)S(1)}, u32[]{:S(2)}, u32[]{:S(2)}) collective-permute-start(bf16[64,8192]{1,0:T(8,128)(2,1)} %own_gate.1), channel_id=1, source_target_pairs={{0,1},{1,0},{2,3},{3,2},{4,5},{5,4},{6,7},{7,6},{8,9},{9,8},{10,11... | collective-permute-start | bytes 3145736 | tf_op jit(solution)/shard_map/ppermute | solution.py:21
  1.5 14.4 %collective-permute-start.5 = (bf16[512,128]{1,0:T(8,128)(2,1)S(1)}, bf16[512,128]{1,0:T(8,128)(2,1)S(1)}, u32[]{:S(2)}, u32[]{:S(2)}) collective-permute-start(bf16[512,128]{1,0:T(8,128)(2,1)S(1)} %bitcast.13), channel_id=1, source_target_pairs={{0,12},{2,14},{4,8},{6,10},{8,4},{10,6},{12,0},{14,2},{1,13},{3,15... | collective-permute-start | bytes 393224 | tf_op jit(solution)/shard_map/ppermute | solution.py:21
  3.2 8.3 %collective-permute-start.8 = (bf16[1,3,4608]{2,1,0:T(4,128)(2,1)}, bf16[1,3,4608]{2,1,0:T(4,128)(2,1)S(1)}, u32[]{:S(2)}, u32[]{:S(2)}) collective-permute-start(bf16[1,3,4608]{2,1,0:T(4,128)(2,1)} %rims.1), channel_id=1, source_target_pairs={{0,12},{2,14},{4,8},{6,10},{8,4},{10,6},{12,0},{14,2},{1,13},{3,15... | collective-permute-start | bytes 82952 | tf_op jit(solution)/shard_map/ppermute | solution.py:21
  4.9 7.1 %collective-permute-start.7 = (bf16[1,3,4608]{2,1,0:T(4,128)(2,1)S(1)}, bf16[1,3,4608]{2,1,0:T(4,128)(2,1)S(1)}, u32[]{:S(2)}, u32[]{:S(2)}) collective-permute-start(bf16[1,3,4608]{2,1,0:T(4,128)(2,1)S(1)} %get-tuple-element.32.refs_8_.refs_0_), channel_id=1, source_target_pairs={{0,4},{2,6},{4,0},{6,2},{8,12},{10,14},{12,8},{14,10},{1,5},{3,7},... | collective-permute-start | bytes 82952 | tf_op jit(solution)/shard_map/ppermute | solution.py:21
  11.5 4.0 %collective-permute-start.9 = (bf16[1,3,4608]{2,1,0:T(4,128)(2,1)S(1)}, bf16[1,3,4608]{2,1,0:T(4,128)(2,1)S(1)}, u32[]{:S(2)}, u32[]{:S(2)}) collective-permute-start(bf16[1,3,4608]{2,1,0:T(4,128)(2,1)S(1)} %collective-permute-done.8.refs_11_.refs_3_), channel_id=1, source_target_pairs={{0,4},{2,6},{4,0},{6,2},{8,12},{10,14},{12,8},{14,10},{1,5},{3,7},... | collective-permute-start | bytes 82952 | tf_op jit(solution)/shard_map/ppermute | solution.py:21
  12.0 6.4 %collective-permute-start = (bf16[512,128]{1,0:T(8,128)(2,1)S(1)}, bf16[512,128]{1,0:T(8,128)(2,1)S(1)}, u32[]{:S(2)}, u32[]{:S(2)}) collective-permute-start(bf16[512,128]{1,0:T(8,128)(2,1)S(1)} %get-tuple-element.26), channel_id=1, source_target_pairs={{0,2},{2,0},{4,6},{6,4},{8,10},{10,8},{12,14},{14,12},{1,3},{3,1},... | collective-permute-start | bytes 393224 | tf_op jit(solution)/shard_map/ppermute | solution.py:21
  15.4 5.9 %collective-permute-start.1 = (bf16[512,128]{1,0:T(8,128)(2,1)S(1)}, bf16[512,128]{1,0:T(8,128)(2,1)S(1)}, u32[]{:S(2)}, u32[]{:S(2)}) collective-permute-start(bf16[512,128]{1,0:T(8,128)(2,1)S(1)} %get-tuple-element.27), channel_id=1, source_target_pairs={{0,4},{2,6},{4,0},{6,2},{8,12},{10,14},{12,8},{14,10},{1,5},{3,7},... | collective-permute-start | bytes 393224 | tf_op jit(solution)/shard_map/ppermute | solution.py:21
  16.0 9.6 %collective-permute-start.2 = (bf16[512,128]{1,0:T(8,128)(2,1)S(1)}, bf16[512,128]{1,0:T(8,128)(2,1)S(1)}, u32[]{:S(2)}, u32[]{:S(2)}) collective-permute-start(bf16[512,128]{1,0:T(8,128)(2,1)S(1)} %get-tuple-element.28), channel_id=1, source_target_pairs={{0,6},{2,4},{4,2},{6,0},{8,14},{10,12},{12,10},{14,8},{1,7},{3,5},... | collective-permute-start | bytes 393224 | tf_op jit(solution)/shard_map/ppermute | solution.py:21
  18.4 11.2 %collective-permute-start.3 = (bf16[512,128]{1,0:T(8,128)(2,1)S(1)}, bf16[512,128]{1,0:T(8,128)(2,1)S(1)}, u32[]{:S(2)}, u32[]{:S(2)}) collective-permute-start(bf16[512,128]{1,0:T(8,128)(2,1)S(1)} %get-tuple-element.29), channel_id=1, source_target_pairs={{0,8},{2,10},{4,12},{6,14},{8,0},{10,2},{12,4},{14,6},{1,9},{3,11}... | collective-permute-start | bytes 393224 | tf_op jit(solution)/shard_map/ppermute | solution.py:21
  21.3 12.0 %collective-permute-start.4 = (bf16[512,128]{1,0:T(8,128)(2,1)S(1)}, bf16[512,128]{1,0:T(8,128)(2,1)S(1)}, u32[]{:S(2)}, u32[]{:S(2)}) collective-permute-start(bf16[512,128]{1,0:T(8,128)(2,1)S(1)} %get-tuple-element.30), channel_id=1, source_target_pairs={{0,10},{2,8},{4,14},{6,12},{8,2},{10,0},{12,6},{14,4},{1,11},{3,9}... | collective-permute-start | bytes 393224 | tf_op jit(solution)/shard_map/ppermute | solution.py:21
  25.5 11.1 %collective-permute-start.6 = (bf16[512,128]{1,0:T(8,128)(2,1)S(1)}, bf16[512,128]{1,0:T(8,128)(2,1)S(1)}, u32[]{:S(2)}, u32[]{:S(2)}) collective-permute-start(bf16[512,128]{1,0:T(8,128)(2,1)S(1)} %get-tuple-element.31), channel_id=1, source_target_pairs={{0,14},{2,12},{4,10},{6,8},{8,6},{10,4},{12,2},{14,0},{1,15},{3,13... | collective-permute-start | bytes 393224 | tf_op jit(solution)/shard_map/ppermute | solution.py:21
  28.4 0.7 copy-start.7
  37.1 8.7 %collective-permute-start.18 = (bf16[512,128]{1,0:T(8,128)(2,1)S(1)}, bf16[512,128]{1,0:T(8,128)(2,1)S(1)}, u32[]{:S(2)}, u32[]{:S(2)}) collective-permute-start(bf16[512,128]{1,0:T(8,128)(2,1)S(1)} %get-tuple-element.42), channel_id=1, source_target_pairs={{0,2},{2,0},{4,6},{6,4},{8,10},{10,8},{12,14},{14,12},{1,3},{3,1},... | collective-permute-start | bytes 393224 | tf_op jit(solution)/shard_map/ppermute | solution.py:21
  37.8 8.6 %collective-permute-start.19 = (bf16[512,128]{1,0:T(8,128)(2,1)S(1)}, bf16[512,128]{1,0:T(8,128)(2,1)S(1)}, u32[]{:S(2)}, u32[]{:S(2)}) collective-permute-start(bf16[512,128]{1,0:T(8,128)(2,1)S(1)} %get-tuple-element.43), channel_id=1, source_target_pairs={{0,4},{2,6},{4,0},{6,2},{8,12},{10,14},{12,8},{14,10},{1,5},{3,7},... | collective-permute-start | bytes 393224 | tf_op jit(solution)/shard_map/ppermute | solution.py:21
  37.8 1.2 %collective-permute-start.16 = (bf16[64,128]{1,0:T(8,128)(2,1)S(1)}, bf16[64,128]{1,0:T(8,128)(2,1)S(1)}, u32[]{:S(2)}, u32[]{:S(2)}) collective-permute-start(bf16[64,128]{1,0:T(8,128)(2,1)S(1)} %copy-done.3), channel_id=1, source_target_pairs={{0,1},{1,0},{2,3},{3,2},{4,5},{5,4},{6,7},{7,6},{8,9},{9,8},{10,11... | collective-permute-start | bytes 49160 | tf_op jit(solution)/shard_map/ppermute | solution.py:21
  39.0 4.0 %collective-permute-start.17 = (bf16[1,3,4608]{2,1,0:T(4,128)(2,1)S(1)}, bf16[1,3,4608]{2,1,0:T(4,128)(2,1)S(1)}, u32[]{:S(2)}, u32[]{:S(2)}) collective-permute-start(bf16[1,3,4608]{2,1,0:T(4,128)(2,1)S(1)} %get-tuple-element.37), channel_id=1, source_target_pairs={{0,2},{2,0},{4,6},{6,4},{8,10},{10,8},{12,14},{14,12},{1,3},{3,1},... | collective-permute-start | bytes 82952 | tf_op jit(solution)/shard_map/ppermute | solution.py:21
  43.0 17.2 %collective-permute-start.20 = (bf16[512,128]{1,0:T(8,128)(2,1)S(1)}, bf16[512,128]{1,0:T(8,128)(2,1)S(1)}, u32[]{:S(2)}, u32[]{:S(2)}) collective-permute-start(bf16[512,128]{1,0:T(8,128)(2,1)S(1)} %get-tuple-element.44), channel_id=1, source_target_pairs={{0,6},{2,4},{4,2},{6,0},{8,14},{10,12},{12,10},{14,8},{1,7},{3,5},... | collective-permute-start | bytes 393224 | tf_op jit(solution)/shard_map/ppermute | solution.py:21
  45.8 15.7 %collective-permute-start.10 = (bf16[512,128]{1,0:T(8,128)(2,1)S(1)}, bf16[512,128]{1,0:T(8,128)(2,1)S(1)}, u32[]{:S(2)}, u32[]{:S(2)}) collective-permute-start(bf16[512,128]{1,0:T(8,128)(2,1)S(1)} %get-tuple-element.33), channel_id=1, source_target_pairs={{0,8},{2,10},{4,12},{6,14},{8,0},{10,2},{12,4},{14,6},{1,9},{3,11}... | collective-permute-start | bytes 393224 | tf_op jit(solution)/shard_map/ppermute | solution.py:21
  46.4 17.5 %collective-permute-start.11 = (bf16[512,128]{1,0:T(8,128)(2,1)S(1)}, bf16[512,128]{1,0:T(8,128)(2,1)S(1)}, u32[]{:S(2)}, u32[]{:S(2)}) collective-permute-start(bf16[512,128]{1,0:T(8,128)(2,1)S(1)} %get-tuple-element.34), channel_id=1, source_target_pairs={{0,10},{2,8},{4,14},{6,12},{8,2},{10,0},{12,6},{14,4},{1,11},{3,9}... | collective-permute-start | bytes 393224 | tf_op jit(solution)/shard_map/ppermute | solution.py:21
  48.8 19.1 %collective-permute-start.12 = (bf16[512,128]{1,0:T(8,128)(2,1)S(1)}, bf16[512,128]{1,0:T(8,128)(2,1)S(1)}, u32[]{:S(2)}, u32[]{:S(2)}) collective-permute-start(bf16[512,128]{1,0:T(8,128)(2,1)S(1)} %get-tuple-element.35), channel_id=1, source_target_pairs={{0,12},{2,14},{4,8},{6,10},{8,4},{10,6},{12,0},{14,2},{1,13},{3,15... | collective-permute-start | bytes 393224 | tf_op jit(solution)/shard_map/ppermute | solution.py:21
  50.2 19.6 %collective-permute-start.13 = (bf16[512,128]{1,0:T(8,128)(2,1)S(1)}, bf16[512,128]{1,0:T(8,128)(2,1)S(1)}, u32[]{:S(2)}, u32[]{:S(2)}) collective-permute-start(bf16[512,128]{1,0:T(8,128)(2,1)S(1)} %get-tuple-element.36), channel_id=1, source_target_pairs={{0,14},{2,12},{4,10},{6,8},{8,6},{10,4},{12,2},{14,0},{1,15},{3,13... | collective-permute-start | bytes 393224 | tf_op jit(solution)/shard_map/ppermute | solution.py:21
  51.7 8.5 %copy-start.2 = (f32[4096]{0:T(1024)S(1)}, f32[4096]{0:T(1024)}, u32[]{:S(2)}) copy-start(f32[4096]{0:T(1024)} %param.22) | copy-start | bytes 49156

commit v5 on v4

--- a/solution.py
+++ b/solution.py
@@ -240,16 +240,23 @@
     )
 
 
-def tail_kernel(base, has_before, plan, *refs):
-    out, wide, narrow, sems = refs[-4:]
-    intra, carry, c_proj, gain = refs[-8 - has_before : -4 - has_before]
-    pieces = refs[: -8 - has_before]
+def tail_kernel(base, piece_count, last, plan, *refs):
+    pieces, refs = refs[:piece_count], refs[piece_count:]
+    intra, carry, c_proj, gain = refs[:4]
+    before, refs = (refs[4 : 4 + base], refs[4 + base :]) if last else ((), refs[4:])
+    out, wide = refs[:2]
     tokens = wide.shape[0]
     count, rows = len(pieces), pieces[0].shape[0]
     turn = plan[TURNED + plan[ME]] if count > 1 else 0
     group = base ^ (turn // count)
     within = turn % count
     keep = lax.broadcasted_iota(jnp.int32, (tokens, 1), 0) < plan[SPAN]
+    narrow, sems = (refs[2], refs[3]) if last else (out, None)
+    copies = []
+    for earlier, part_out in enumerate(before):
+        column = pl.multiple_of((earlier ^ (turn // count)) * NORM_WIDTH, NORM_WIDTH)
+        copies.append(pltpu.make_async_copy(part_out, out.at[:, pl.ds(column, NORM_WIDTH)], sems.at[earlier]))
+        copies[-1].start()
     c = c_proj[:, pl.ds(pl.multiple_of(group * STATE, STATE), STATE)]
     part = min(rows, 512)
     total = jnp.zeros((tokens, 1), jnp.float32)
@@ -267,40 +274,43 @@
             wide[:, index * part : (index + 1) * part] = value
             places.append(column)
     scale = lax.rsqrt(total * (1.0 / NORM_WIDTH) + EPSILON)
-    copies = []
     for index, column in enumerate(places):
         lanes = slice(index * part, (index + 1) * part)
         normed = wide[:, lanes] * scale * gain[:, pl.ds(column, part)]
-        narrow[:, lanes] = jnp.where(keep, normed, 0.0).astype(jnp.bfloat16)
-        copy = pltpu.make_async_copy(narrow.at[:, lanes], out.at[:, pl.ds(column, part)], sems.at[index])
-        copy.start()
-        copies.append(copy)
+        value = jnp.where(keep, normed, 0.0).astype(jnp.bfloat16)
+        if last:
+            narrow[:, lanes] = value
+            target = out.at[:, pl.ds(column, part)]
+            copies.append(pltpu.make_async_copy(narrow.at[:, lanes], target, sems.at[base + index]))
+            copies[-1].start()
+        else:
+            narrow[:, pl.ds(pl.multiple_of(column - group * NORM_WIDTH, part), part)] = value
     for copy in copies:
         copy.wait()
 
 
-def tail_stage(base, plan, pieces, intra, carry, c_proj, gain, before=None):
+def tail_stage(base, last, plan, pieces, intra, carry, c_proj, gain, before):
     tokens, _ = intra.shape
     vmem = pl.BlockSpec(memory_space=pltpu.VMEM)
-    whole = pl.BlockSpec(memory_space=pltpu.HBM)
-    earlier = [] if before is None else [before]
     parts = NORM_WIDTH // min(pieces[0].shape[0], 512)
+    earlier = before if last else []
+    scratch = [pltpu.VMEM((tokens, NORM_WIDTH), jnp.float32)]
+    if last:
+        scratch += [pltpu.VMEM((tokens, NORM_WIDTH), jnp.bfloat16), pltpu.SemaphoreType.DMA((base + parts,))]
+        out_shape = jax.ShapeDtypeStruct(intra.shape, jnp.bfloat16)
+    else:
+        out_shape = pltpu.VMEM((tokens, NORM_WIDTH), jnp.bfloat16)
     grid_spec = pltpu.PrefetchScalarGridSpec(
         num_scalar_prefetch=1,
         grid=(),
-        in_specs=[vmem] * (len(pieces) + 4) + [whole] * len(earlier),
-        out_specs=whole,
-        scratch_shapes=[
-            pltpu.VMEM((tokens, NORM_WIDTH), jnp.float32),
-            pltpu.VMEM((tokens, NORM_WIDTH), jnp.bfloat16),
-            pltpu.SemaphoreType.DMA((parts,)),
-        ],
+        in_specs=[vmem] * (len(pieces) + 4 + len(earlier)),
+        out_specs=pl.BlockSpec(memory_space=pltpu.HBM) if last else vmem,
+        scratch_shapes=scratch,
     )
     return pl.pallas_call(
-        functools.partial(tail_kernel, base, len(earlier)),
+        functools.partial(tail_kernel, base, len(pieces), last),
         grid_spec=grid_spec,
-        out_shape=jax.ShapeDtypeStruct(intra.shape, jnp.bfloat16),
-        input_output_aliases={1 + len(pieces) + 4: 0} if earlier else {},
+        out_shape=out_shape,
         compiler_params=pltpu.CompilerParams(vmem_limit_bytes=16 << 20),
         cost_estimate=pl.CostEstimate(flops=70_000_000, bytes_accessed=3_000_000, transcendentals=0),
     )(plan, *pieces, intra, carry, c_proj, gain, *earlier)
@@ -480,13 +490,13 @@
         rims,
     )
     gain = norm_gain.reshape(1, -1)
-    mixed = None
     norms = norm_gain.shape[0] // NORM_WIDTH
     share = len(got) // norms
+    done = []
     for base in range(norms):
         mine = got[base * share : (base + 1) * share]
-        mixed = tail_stage(base, plan, mine, intra, carry, c_proj, gain, mixed)
-    return mixed
+        done.append(tail_stage(base, base == norms - 1, plan, mine, intra, carry, c_proj, gain, done))
+    return done[-1]
 
 
 def solution(mesh):

time: 71.6 us -> 71.6 us (level)
  Pallas kernels: 13.4 us -> 12.6 us
  waiting for transfers between devices: 28.7 us -> 29.5 us
    ppermute x21, waiting for transfers between devices: 28.7 us -> 29.5 us  [swap(): return lax.ppermute(value, axis, [(i, i ^ offset) for i in range(count)])]
    pallas_call x2, Pallas kernels: 2.6 us -> 1.83 us  [tail_stage(): pl.pallas_call(functools.partial(tail_kernel, base, len(pieces), last), g...]
  transfers between devices with their start and end apart: 21 -> 21, of which waited for: 11 -> 12; matrix products, arithmetic and copies ran while one was open for 1% -> 1% of each run, Pallas kernels for 17% -> 16%
where the time goes in v5:
time: 71.6 us; the launch traced here: 71.1 us
  waiting for transfers between devices  29.5 us (41%)
  starting transfers between devices  26 us (36%)
  Pallas kernels  12.6 us (18%)
  local copies, waits for them, and re-layouts  1.59 us (2%)
  between operations  1.45 us (2%)
    ppermute x21, waiting for transfers between devices, swap(): return lax.ppermute(value, axis, [(i, i ^ offset) for i in range(count)])  29.5 us
    ppermute x21, starting transfers between devices, swap(): return lax.ppermute(value, axis, [(i, i ^ offset) for i in range(count)])  26 us
    pallas_call x1, Pallas kernels, main_stage(): pl.pallas_call(functools.partial(main_kernel, len(rims)), grid_spec=grid_...  8.47 us
    pallas_call x2, Pallas kernels, tail_stage(): pl.pallas_call(functools.partial(tail_kernel, base, len(pieces), last), g...  1.83 us
  transfers between devices with their start and end apart: 21, of which 12 were waited for; matrix products, arithmetic and copies ran while one was open for 1% of the time, Pallas kernels for 16%

profile of v5, /device:TPU:8, one launch (start us, length us, event | category | flops | bytes accessed | tf_op | source)
XLA Modules:
  0.0 71.1 jit_solution(13740417914537894514)
XLA Ops:
  0.0 0.1 collective-permute-start.14
  0.1 0.5 collective-permute-start.15
  0.6 0.9 %slice.4 = bf16[1,8,64,128]{3,2,1,0:T(8,128)(2,1)S(1)} slice(bf16[1,64,64,128]{3,2,1,0:T(8,128)(2,1)} %param.23), slice={[0:1], [48:56], [0:64], [0:128]} | slice | bytes 262144 | tf_op jit(solution)/shard_map/slice | solution.py:460
  1.5 1.6 %collective-permute-start.5 = (bf16[512,128]{1,0:T(8,128)(2,1)S(1)}, bf16[512,128]{1,0:T(8,128)(2,1)S(1)}, u32[]{:S(2)}, u32[]{:S(2)}) collective-permute-start(bf16[512,128]{1,0:T(8,128)(2,1)S(1)} %bitcast.13), channel_id=1, source_target_pairs={{0,12},{2,14},{4,8},{6,10},{8,4},{10,6},{12,0},{14,2},{1,13},{3,15... | collective-permute-start | bytes 393224 | tf_op jit(solution)/shard_map/ppermute | solution.py:21
  3.2 0.4 collective-permute-start.8
  3.6 1.3 %cut_stage.1 = (bf16[512,128]{1,0:T(8,128)(2,1)S(1)}, bf16[512,128]{1,0:T(8,128)(2,1)S(1)}, bf16[512,128]{1,0:T(8,128)(2,1)S(1)}, bf16[512,128]{1,0:T(8,128)(2,1...) custom-call(bf16[8,512,128]{2,1,0:T(8,128)(2,1)} %bitcast.12, ...), custom_call_target="tpu_custom_call" | custom-call | tf_op jit(solution)/shard_map/cut_stage/pallas_call | solution.py:354
  4.9 2.2 %collective-permute-start.7 = (bf16[1,3,4608]{2,1,0:T(4,128)(2,1)S(1)}, bf16[1,3,4608]{2,1,0:T(4,128)(2,1)S(1)}, u32[]{:S(2)}, u32[]{:S(2)}) collective-permute-start(bf16[1,3,4608]{2,1,0:T(4,128)(2,1)S(1)} %get-tuple-element.32.refs_8_.refs_0_), channel_id=1, source_target_pairs={{0,4},{2,6},{4,0},{6,2},{8,12},{10,14},{12,8},{14,10},{1,5},{3,7},... | collective-permute-start | bytes 82952 | tf_op jit(solution)/shard_map/ppermute | solution.py:21
  7.1 4.4 %collective-permute-done.8.refs_11_.refs_3_ = bf16[1,3,4608]{2,1,0:T(4,128)(2,1)S(1)} collective-permute-done((bf16[1,3,4608]{2,1,0:T(4,128)(2,1)}, bf16[1,3,4608]{2,1,0:T(4,128)(2,1)S(1)}, u32[]{:S(2)}, u32[]{:S(2)}) %collective-permute-start.8) | collective-permute-done | bytes 27680 | tf_op jit(solution)/shard_map/ppermute | solution.py:21
  11.5 0.5 collective-permute-start.9
  12.0 0.0 collective-permute-done.7.refs_9_.refs_1_
  12.0 1.5 %collective-permute-start = (bf16[512,128]{1,0:T(8,128)(2,1)S(1)}, bf16[512,128]{1,0:T(8,128)(2,1)S(1)}, u32[]{:S(2)}, u32[]{:S(2)}) collective-permute-start(bf16[512,128]{1,0:T(8,128)(2,1)S(1)} %get-tuple-element.26), channel_id=1, source_target_pairs={{0,2},{2,0},{4,6},{6,4},{8,10},{10,8},{12,14},{14,12},{1,3},{3,1},... | collective-permute-start | bytes 393224 | tf_op jit(solution)/shard_map/ppermute | solution.py:21
  13.5 1.9 %collective-permute-done.9.refs_10_.refs_2_ = bf16[1,3,4608]{2,1,0:T(4,128)(2,1)S(1)} collective-permute-done((bf16[1,3,4608]{2,1,0:T(4,128)(2,1)S(1)}, bf16[1,3,4608]{2,1,0:T(4,128)(2,1)S(1)}, u32[]{:S(2)}, u32[]{:S(2)}) %collective-permute-start.9) | collective-permute-done | bytes 27680 | tf_op jit(solution)/shard_map/ppermute | solution.py:21
  15.4 0.5 collective-permute-start.1
  16.0 0.0 collective-permute-done.5.refs_6_
  16.0 2.4 %collective-permute-start.2 = (bf16[512,128]{1,0:T(8,128)(2,1)S(1)}, bf16[512,128]{1,0:T(8,128)(2,1)S(1)}, u32[]{:S(2)}, u32[]{:S(2)}) collective-permute-start(bf16[512,128]{1,0:T(8,128)(2,1)S(1)} %get-tuple-element.28), channel_id=1, source_target_pairs={{0,6},{2,4},{4,2},{6,0},{8,14},{10,12},{12,10},{14,8},{1,7},{3,5},... | collective-permute-start | bytes 393224 | tf_op jit(solution)/shard_map/ppermute | solution.py:21
  18.4 0.0 collective-permute-done.refs_1_
  18.4 1.2 %collective-permute-start.3 = (bf16[512,128]{1,0:T(8,128)(2,1)S(1)}, bf16[512,128]{1,0:T(8,128)(2,1)S(1)}, u32[]{:S(2)}, u32[]{:S(2)}) collective-permute-start(bf16[512,128]{1,0:T(8,128)(2,1)S(1)} %get-tuple-element.29), channel_id=1, source_target_pairs={{0,8},{2,10},{4,12},{6,14},{8,0},{10,2},{12,4},{14,6},{1,9},{3,11}... | collective-permute-start | bytes 393224 | tf_op jit(solution)/shard_map/ppermute | solution.py:21
  19.6 1.7 %collective-permute-done.1.refs_2_ = bf16[512,128]{1,0:T(8,128)(2,1)S(1)} collective-permute-done((bf16[512,128]{1,0:T(8,128)(2,1)S(1)}, bf16[512,128]{1,0:T(8,128)(2,1)S(1)}, u32[]{:S(2)}, u32[]{:S(2)}) %collective-permute-start.1) | collective-permute-done | bytes 131104 | tf_op jit(solution)/shard_map/ppermute | solution.py:21
  21.3 2.6 %collective-permute-start.4 = (bf16[512,128]{1,0:T(8,128)(2,1)S(1)}, bf16[512,128]{1,0:T(8,128)(2,1)S(1)}, u32[]{:S(2)}, u32[]{:S(2)}) collective-permute-start(bf16[512,128]{1,0:T(8,128)(2,1)S(1)} %get-tuple-element.30), channel_id=1, source_target_pairs={{0,10},{2,8},{4,14},{6,12},{8,2},{10,0},{12,6},{14,4},{1,11},{3,9}... | collective-permute-start | bytes 393224 | tf_op jit(solution)/shard_map/ppermute | solution.py:21
  23.9 1.7 %collective-permute-done.2.refs_3_ = bf16[512,128]{1,0:T(8,128)(2,1)S(1)} collective-permute-done((bf16[512,128]{1,0:T(8,128)(2,1)S(1)}, bf16[512,128]{1,0:T(8,128)(2,1)S(1)}, u32[]{:S(2)}, u32[]{:S(2)}) %collective-permute-start.2) | collective-permute-done | bytes 131104 | tf_op jit(solution)/shard_map/ppermute | solution.py:21
  25.5 1.5 %collective-permute-start.6 = (bf16[512,128]{1,0:T(8,128)(2,1)S(1)}, bf16[512,128]{1,0:T(8,128)(2,1)S(1)}, u32[]{:S(2)}, u32[]{:S(2)}) collective-permute-start(bf16[512,128]{1,0:T(8,128)(2,1)S(1)} %get-tuple-element.31), channel_id=1, source_target_pairs={{0,14},{2,12},{4,10},{6,8},{8,6},{10,4},{12,2},{14,0},{1,15},{3,13... | collective-permute-start | bytes 393224 | tf_op jit(solution)/shard_map/ppermute | solution.py:21
  28.4 0.0 copy-start.7
  28.4 0.6 copy-done.7
  29.0 0.6 plan_stage.1.plan
  29.6 3.7 %collective-permute-done.4.refs_5_ = bf16[512,128]{1,0:T(8,128)(2,1)S(1)} collective-permute-done((bf16[512,128]{1,0:T(8,128)(2,1)S(1)}, bf16[512,128]{1,0:T(8,128)(2,1)S(1)}, u32[]{:S(2)}, u32[]{:S(2)}) %collective-permute-start.4) | collective-permute-done | bytes 131104 | tf_op jit(solution)/shard_map/ppermute | solution.py:21
  33.3 3.4 %collective-permute-done.6.refs_7_ = bf16[512,128]{1,0:T(8,128)(2,1)S(1)} collective-permute-done((bf16[512,128]{1,0:T(8,128)(2,1)S(1)}, bf16[512,128]{1,0:T(8,128)(2,1)S(1)}, u32[]{:S(2)}, u32[]{:S(2)}) %collective-permute-start.6) | collective-permute-done | bytes 131104 | tf_op jit(solution)/shard_map/ppermute | solution.py:21
  36.6 0.5 pick_stage.1
  37.1 0.7 collective-permute-start.18
  37.8 0.0 collective-permute-start.19
  37.8 0.0 collective-permute-start.16
  37.8 1.2 %collective-permute-done.16.peer_dt = bf16[64,128]{1,0:T(8,128)(2,1)S(1)} collective-permute-done((bf16[64,128]{1,0:T(8,128)(2,1)S(1)}, bf16[64,128]{1,0:T(8,128)(2,1)S(1)}, u32[]{:S(2)}, u32[]{:S(2)}) %collective-permute-start.16) | collective-permute-done | bytes 16416 | tf_op jit(solution)/shard_map/ppermute | solution.py:21
  39.0 1.4 %collective-permute-start.17 = (bf16[1,3,4608]{2,1,0:T(4,128)(2,1)S(1)}, bf16[1,3,4608]{2,1,0:T(4,128)(2,1)S(1)}, u32[]{:S(2)}, u32[]{:S(2)}) collective-permute-start(bf16[1,3,4608]{2,1,0:T(4,128)(2,1)S(1)} %get-tuple-element.37), channel_id=1, source_target_pairs={{0,2},{2,0},{4,6},{6,4},{8,10},{10,8},{12,14},{14,12},{1,3},{3,1},... | collective-permute-start | bytes 82952 | tf_op jit(solution)/shard_map/ppermute | solution.py:21
  40.4 2.6 %collective-permute-done.17.refs_4_ = bf16[1,3,4608]{2,1,0:T(4,128)(2,1)S(1)} collective-permute-done((bf16[1,3,4608]{2,1,0:T(4,128)(2,1)S(1)}, bf16[1,3,4608]{2,1,0:T(4,128)(2,1)S(1)}, u32[]{:S(2)}, u32[]{:S(2)}) %collective-permute-start.17) | collective-permute-done | bytes 27680 | tf_op jit(solution)/shard_map/ppermute | solution.py:21
  43.0 2.8 %collective-permute-start.20 = (bf16[512,128]{1,0:T(8,128)(2,1)S(1)}, bf16[512,128]{1,0:T(8,128)(2,1)S(1)}, u32[]{:S(2)}, u32[]{:S(2)}) collective-permute-start(bf16[512,128]{1,0:T(8,128)(2,1)S(1)} %get-tuple-element.44), channel_id=1, source_target_pairs={{0,6},{2,4},{4,2},{6,0},{8,14},{10,12},{12,10},{14,8},{1,7},{3,5},... | collective-permute-start | bytes 393224 | tf_op jit(solution)/shard_map/ppermute | solution.py:21
  45.8 0.0 collective-permute-done.18.refs_1_
  45.8 0.6 collective-permute-start.10
  46.4 2.4 %collective-permute-start.11 = (bf16[512,128]{1,0:T(8,128)(2,1)S(1)}, bf16[512,128]{1,0:T(8,128)(2,1)S(1)}, u32[]{:S(2)}, u32[]{:S(2)}) collective-permute-start(bf16[512,128]{1,0:T(8,128)(2,1)S(1)} %get-tuple-element.34), channel_id=1, source_target_pairs={{0,10},{2,8},{4,14},{6,12},{8,2},{10,0},{12,6},{14,4},{1,11},{3,9}... | collective-permute-start | bytes 393224 | tf_op jit(solution)/shard_map/ppermute | solution.py:21
  48.8 1.4 %collective-permute-start.12 = (bf16[512,128]{1,0:T(8,128)(2,1)S(1)}, bf16[512,128]{1,0:T(8,128)(2,1)S(1)}, u32[]{:S(2)}, u32[]{:S(2)}) collective-permute-start(bf16[512,128]{1,0:T(8,128)(2,1)S(1)} %get-tuple-element.35), channel_id=1, source_target_pairs={{0,12},{2,14},{4,8},{6,10},{8,4},{10,6},{12,0},{14,2},{1,13},{3,15... | collective-permute-start | bytes 393224 | tf_op jit(solution)/shard_map/ppermute | solution.py:21
  50.2 0.0 collective-permute-done.14.peer_x.peer_bc
  50.2 1.5 %collective-permute-start.13 = (bf16[512,128]{1,0:T(8,128)(2,1)S(1)}, bf16[512,128]{1,0:T(8,128)(2,1)S(1)}, u32[]{:S(2)}, u32[]{:S(2)}) collective-permute-start(bf16[512,128]{1,0:T(8,128)(2,1)S(1)} %get-tuple-element.36), channel_id=1, source_target_pairs={{0,14},{2,12},{4,10},{6,8},{8,6},{10,4},{12,2},{14,0},{1,15},{3,13... | collective-permute-start | bytes 393224 | tf_op jit(solution)/shard_map/ppermute | solution.py:21
  51.7 0.0 copy-start.2
  51.7 8.5 %main_stage.1 = (f32[128,4096]{1,0:T(8,128)S(1)}, f32[128,4096]{1,0:T(8,128)S(1)}, bf16[128,256]{1,0:T(8,128)(2,1)S(1)}) custom-call(s32[12]{0:T(128)S(4)} %plan_stage.1.plan, f32[64]{0:T(128)S(1)} %copy-done.4, bf16[64,9216]{1,0:T(8,128)(2,1)} %own_bc.1, bf16[64,9216]{1,0:T(8,128)(2,1)S(1)} %collective-permute-done.14.peer_x.peer_bc, ...), custom_call_target="tpu_custom_call" | custom-call | flops 400000000 | bytes 8000000 | tf_op jit(solution)/shard_map/main_stage/pallas_call | solution.py:211
  60.2 0.5 shard_map.136.refs_8_
  60.7 0.4 collective-permute-done.10.refs_0_
  61.1 2.8 %collective-permute-done.11.refs_1_ = bf16[512,128]{1,0:T(8,128)(2,1)S(1)} collective-permute-done((bf16[512,128]{1,0:T(8,128)(2,1)S(1)}, bf16[512,128]{1,0:T(8,128)(2,1)S(1)}, u32[]{:S(2)}, u32[]{:S(2)}) %collective-permute-start.11) | collective-permute-done | bytes 131104 | tf_op jit(solution)/shard_map/ppermute | solution.py:21
  63.9 4.0 %collective-permute-done.12.refs_2_ = bf16[512,128]{1,0:T(8,128)(2,1)S(1)} collective-permute-done((bf16[512,128]{1,0:T(8,128)(2,1)S(1)}, bf16[512,128]{1,0:T(8,128)(2,1)S(1)}, u32[]{:S(2)}, u32[]{:S(2)}) %collective-permute-start.12) | collective-permute-done | bytes 131104 | tf_op jit(solution)/shard_map/ppermute | solution.py:21
  67.9 1.9 %collective-permute-done.13.refs_3_ = bf16[512,128]{1,0:T(8,128)(2,1)S(1)} collective-permute-done((bf16[512,128]{1,0:T(8,128)(2,1)S(1)}, bf16[512,128]{1,0:T(8,128)(2,1)S(1)}, u32[]{:S(2)}, u32[]{:S(2)}) %collective-permute-start.13) | collective-permute-done | bytes 131104 | tf_op jit(solution)/shard_map/ppermute | solution.py:21
  69.8 1.3 %shard_map.137 = bf16[128,4096]{1,0:T(8,128)(2,1)} custom-call(s32[12]{0:T(128)S(4)} %plan_stage.1.plan, bf16[512,128]{1,0:T(8,128)(2,1)S(1)} %collective-permute-done.10.refs_0_, bf16[512,128]{1,0:T(8,128)(2,1)S(1)} %collective-permute-done.11.refs_1_, bf16[512,128]{1,0:T(8,128)(2,1)S(1)} %collective-permute-done.12.refs_2_, ...), custom_call_target="tpu_custom_call" | custom-call | flops 70000000 | bytes 3000000 | tf_op jit(solution)/shard_map/pallas_call | solution.py:310
  (17 shorter events, 0.0 us)
Async XLA Ops:
  0.0 37.8 %copy-start.3 = (bf16[64,128]{1,0:T(8,128)(2,1)S(1)}, bf16[64,128]{1,0:T(8,128)(2,1)}, u32[]{:S(2)}) copy-start(bf16[64,128]{1,0:T(8,128)(2,1)} %own_dt.1) | copy-start | bytes 49156
  0.0 51.7 %copy-start.4 = (f32[64]{0:T(128)S(1)}, f32[64]{0:T(128)}, u32[]{:S(2)}) copy-start(f32[64]{0:T(128)} %skip_ref.1) | copy-start | bytes 772
  0.0 51.7 %copy-start.6 = (f32[64]{0:T(128)S(1)}, f32[64]{0:T(128)}, u32[]{:S(2)}) copy-start(f32[64]{0:T(128)} %param.20) | copy-start | bytes 772
  0.0 51.7 %copy-start.5 = (f32[64]{0:T(128)S(1)}, f32[64]{0:T(128)}, u32[]{:S(2)}) copy-start(f32[64]{0:T(128)} %param.19) | copy-start | bytes 772
  0.0 51.7 %copy-start.1 = (f32[9216]{0:T(1024)S(1)}, f32[9216]{0:T(1024)}, u32[]{:S(2)}) copy-start(f32[9216]{0:T(1024)} %param.18) | copy-start | bytes 110596
  0.0 51.6 %copy-start = (f32[4,9216]{1,0:T(4,128)S(1)}, f32[4,9216]{1,0:T(4,128)}, u32[]{:S(2)}) copy-start(f32[4,9216]{1,0:T(4,128)} %weight_bc.1) | copy-start | bytes 442372
  0.0 50.1 %collective-permute-start.14 = (bf16[64,9216]{1,0:T(8,128)(2,1)}, bf16[64,9216]{1,0:T(8,128)(2,1)S(1)}, u32[]{:S(2)}, u32[]{:S(2)}) collective-permute-start(bf16[64,9216]{1,0:T(8,128)(2,1)} %own_bc.1), channel_id=1, source_target_pairs={{0,1},{1,0},{2,3},{3,2},{4,5},{5,4},{6,7},{7,6},{8,9},{9,8},{10,11... | collective-permute-start | bytes 3538952 | tf_op jit(solution)/shard_map/ppermute | solution.py:21
  0.1 48.7 %collective-permute-start.15 = (bf16[64,8192]{1,0:T(8,128)(2,1)}, bf16[64,8192]{1,0:T(8,128)(2,1)S(1)}, u32[]{:S(2)}, u32[]{:S(2)}) collective-permute-start(bf16[64,8192]{1,0:T(8,128)(2,1)} %own_gate.1), channel_id=1, source_target_pairs={{0,1},{1,0},{2,3},{3,2},{4,5},{5,4},{6,7},{7,6},{8,9},{9,8},{10,11... | collective-permute-start | bytes 3145736 | tf_op jit(solution)/shard_map/ppermute | solution.py:21
  1.5 14.4 %collective-permute-start.5 = (bf16[512,128]{1,0:T(8,128)(2,1)S(1)}, bf16[512,128]{1,0:T(8,128)(2,1)S(1)}, u32[]{:S(2)}, u32[]{:S(2)}) collective-permute-start(bf16[512,128]{1,0:T(8,128)(2,1)S(1)} %bitcast.13), channel_id=1, source_target_pairs={{0,12},{2,14},{4,8},{6,10},{8,4},{10,6},{12,0},{14,2},{1,13},{3,15... | collective-permute-start | bytes 393224 | tf_op jit(solution)/shard_map/ppermute | solution.py:21
  3.2 8.3 %collective-permute-start.8 = (bf16[1,3,4608]{2,1,0:T(4,128)(2,1)}, bf16[1,3,4608]{2,1,0:T(4,128)(2,1)S(1)}, u32[]{:S(2)}, u32[]{:S(2)}) collective-permute-start(bf16[1,3,4608]{2,1,0:T(4,128)(2,1)} %rims.1), channel_id=1, source_target_pairs={{0,12},{2,14},{4,8},{6,10},{8,4},{10,6},{12,0},{14,2},{1,13},{3,15... | collective-permute-start | bytes 82952 | tf_op jit(solution)/shard_map/ppermute | solution.py:21
  4.9 7.1 %collective-permute-start.7 = (bf16[1,3,4608]{2,1,0:T(4,128)(2,1)S(1)}, bf16[1,3,4608]{2,1,0:T(4,128)(2,1)S(1)}, u32[]{:S(2)}, u32[]{:S(2)}) collective-permute-start(bf16[1,3,4608]{2,1,0:T(4,128)(2,1)S(1)} %get-tuple-element.32.refs_8_.refs_0_), channel_id=1, source_target_pairs={{0,4},{2,6},{4,0},{6,2},{8,12},{10,14},{12,8},{14,10},{1,5},{3,7},... | collective-permute-start | bytes 82952 | tf_op jit(solution)/shard_map/ppermute | solution.py:21
  11.5 4.0 %collective-permute-start.9 = (bf16[1,3,4608]{2,1,0:T(4,128)(2,1)S(1)}, bf16[1,3,4608]{2,1,0:T(4,128)(2,1)S(1)}, u32[]{:S(2)}, u32[]{:S(2)}) collective-permute-start(bf16[1,3,4608]{2,1,0:T(4,128)(2,1)S(1)} %collective-permute-done.8.refs_11_.refs_3_), channel_id=1, source_target_pairs={{0,4},{2,6},{4,0},{6,2},{8,12},{10,14},{12,8},{14,10},{1,5},{3,7},... | collective-permute-start | bytes 82952 | tf_op jit(solution)/shard_map/ppermute | solution.py:21
  12.0 6.4 %collective-permute-start = (bf16[512,128]{1,0:T(8,128)(2,1)S(1)}, bf16[512,128]{1,0:T(8,128)(2,1)S(1)}, u32[]{:S(2)}, u32[]{:S(2)}) collective-permute-start(bf16[512,128]{1,0:T(8,128)(2,1)S(1)} %get-tuple-element.26), channel_id=1, source_target_pairs={{0,2},{2,0},{4,6},{6,4},{8,10},{10,8},{12,14},{14,12},{1,3},{3,1},... | collective-permute-start | bytes 393224 | tf_op jit(solution)/shard_map/ppermute | solution.py:21
  15.4 5.9 %collective-permute-start.1 = (bf16[512,128]{1,0:T(8,128)(2,1)S(1)}, bf16[512,128]{1,0:T(8,128)(2,1)S(1)}, u32[]{:S(2)}, u32[]{:S(2)}) collective-permute-start(bf16[512,128]{1,0:T(8,128)(2,1)S(1)} %get-tuple-element.27), channel_id=1, source_target_pairs={{0,4},{2,6},{4,0},{6,2},{8,12},{10,14},{12,8},{14,10},{1,5},{3,7},... | collective-permute-start | bytes 393224 | tf_op jit(solution)/shard_map/ppermute | solution.py:21
  16.0 9.6 %collective-permute-start.2 = (bf16[512,128]{1,0:T(8,128)(2,1)S(1)}, bf16[512,128]{1,0:T(8,128)(2,1)S(1)}, u32[]{:S(2)}, u32[]{:S(2)}) collective-permute-start(bf16[512,128]{1,0:T(8,128)(2,1)S(1)} %get-tuple-element.28), channel_id=1, source_target_pairs={{0,6},{2,4},{4,2},{6,0},{8,14},{10,12},{12,10},{14,8},{1,7},{3,5},... | collective-permute-start | bytes 393224 | tf_op jit(solution)/shard_map/ppermute | solution.py:21
  18.4 11.2 %collective-permute-start.3 = (bf16[512,128]{1,0:T(8,128)(2,1)S(1)}, bf16[512,128]{1,0:T(8,128)(2,1)S(1)}, u32[]{:S(2)}, u32[]{:S(2)}) collective-permute-start(bf16[512,128]{1,0:T(8,128)(2,1)S(1)} %get-tuple-element.29), channel_id=1, source_target_pairs={{0,8},{2,10},{4,12},{6,14},{8,0},{10,2},{12,4},{14,6},{1,9},{3,11}... | collective-permute-start | bytes 393224 | tf_op jit(solution)/shard_map/ppermute | solution.py:21
  21.3 12.0 %collective-permute-start.4 = (bf16[512,128]{1,0:T(8,128)(2,1)S(1)}, bf16[512,128]{1,0:T(8,128)(2,1)S(1)}, u32[]{:S(2)}, u32[]{:S(2)}) collective-permute-start(bf16[512,128]{1,0:T(8,128)(2,1)S(1)} %get-tuple-element.30), channel_id=1, source_target_pairs={{0,10},{2,8},{4,14},{6,12},{8,2},{10,0},{12,6},{14,4},{1,11},{3,9}... | collective-permute-start | bytes 393224 | tf_op jit(solution)/shard_map/ppermute | solution.py:21
  25.5 11.1 %collective-permute-start.6 = (bf16[512,128]{1,0:T(8,128)(2,1)S(1)}, bf16[512,128]{1,0:T(8,128)(2,1)S(1)}, u32[]{:S(2)}, u32[]{:S(2)}) collective-permute-start(bf16[512,128]{1,0:T(8,128)(2,1)S(1)} %get-tuple-element.31), channel_id=1, source_target_pairs={{0,14},{2,12},{4,10},{6,8},{8,6},{10,4},{12,2},{14,0},{1,15},{3,13... | collective-permute-start | bytes 393224 | tf_op jit(solution)/shard_map/ppermute | solution.py:21
  28.4 0.7 copy-start.7
  37.1 8.7 %collective-permute-start.18 = (bf16[512,128]{1,0:T(8,128)(2,1)S(1)}, bf16[512,128]{1,0:T(8,128)(2,1)S(1)}, u32[]{:S(2)}, u32[]{:S(2)}) collective-permute-start(bf16[512,128]{1,0:T(8,128)(2,1)S(1)} %get-tuple-element.42), channel_id=1, source_target_pairs={{0,2},{2,0},{4,6},{6,4},{8,10},{10,8},{12,14},{14,12},{1,3},{3,1},... | collective-permute-start | bytes 393224 | tf_op jit(solution)/shard_map/ppermute | solution.py:21
  37.8 8.6 %collective-permute-start.19 = (bf16[512,128]{1,0:T(8,128)(2,1)S(1)}, bf16[512,128]{1,0:T(8,128)(2,1)S(1)}, u32[]{:S(2)}, u32[]{:S(2)}) collective-permute-start(bf16[512,128]{1,0:T(8,128)(2,1)S(1)} %get-tuple-element.43), channel_id=1, source_target_pairs={{0,4},{2,6},{4,0},{6,2},{8,12},{10,14},{12,8},{14,10},{1,5},{3,7},... | collective-permute-start | bytes 393224 | tf_op jit(solution)/shard_map/ppermute | solution.py:21
  37.8 1.2 %collective-permute-start.16 = (bf16[64,128]{1,0:T(8,128)(2,1)S(1)}, bf16[64,128]{1,0:T(8,128)(2,1)S(1)}, u32[]{:S(2)}, u32[]{:S(2)}) collective-permute-start(bf16[64,128]{1,0:T(8,128)(2,1)S(1)} %copy-done.3), channel_id=1, source_target_pairs={{0,1},{1,0},{2,3},{3,2},{4,5},{5,4},{6,7},{7,6},{8,9},{9,8},{10,11... | collective-permute-start | bytes 49160 | tf_op jit(solution)/shard_map/ppermute | solution.py:21
  39.0 4.0 %collective-permute-start.17 = (bf16[1,3,4608]{2,1,0:T(4,128)(2,1)S(1)}, bf16[1,3,4608]{2,1,0:T(4,128)(2,1)S(1)}, u32[]{:S(2)}, u32[]{:S(2)}) collective-permute-start(bf16[1,3,4608]{2,1,0:T(4,128)(2,1)S(1)} %get-tuple-element.37), channel_id=1, source_target_pairs={{0,2},{2,0},{4,6},{6,4},{8,10},{10,8},{12,14},{14,12},{1,3},{3,1},... | collective-permute-start | bytes 82952 | tf_op jit(solution)/shard_map/ppermute | solution.py:21
  43.0 17.2 %collective-permute-start.20 = (bf16[512,128]{1,0:T(8,128)(2,1)S(1)}, bf16[512,128]{1,0:T(8,128)(2,1)S(1)}, u32[]{:S(2)}, u32[]{:S(2)}) collective-permute-start(bf16[512,128]{1,0:T(8,128)(2,1)S(1)} %get-tuple-element.44), channel_id=1, source_target_pairs={{0,6},{2,4},{4,2},{6,0},{8,14},{10,12},{12,10},{14,8},{1,7},{3,5},... | collective-permute-start | bytes 393224 | tf_op jit(solution)/shard_map/ppermute | solution.py:21
  45.8 15.3 %collective-permute-start.10 = (bf16[512,128]{1,0:T(8,128)(2,1)S(1)}, bf16[512,128]{1,0:T(8,128)(2,1)S(1)}, u32[]{:S(2)}, u32[]{:S(2)}) collective-permute-start(bf16[512,128]{1,0:T(8,128)(2,1)S(1)} %get-tuple-element.33), channel_id=1, source_target_pairs={{0,8},{2,10},{4,12},{6,14},{8,0},{10,2},{12,4},{14,6},{1,9},{3,11}... | collective-permute-start | bytes 393224 | tf_op jit(solution)/shard_map/ppermute | solution.py:21
  46.4 17.5 %collective-permute-start.11 = (bf16[512,128]{1,0:T(8,128)(2,1)S(1)}, bf16[512,128]{1,0:T(8,128)(2,1)S(1)}, u32[]{:S(2)}, u32[]{:S(2)}) collective-permute-start(bf16[512,128]{1,0:T(8,128)(2,1)S(1)} %get-tuple-element.34), channel_id=1, source_target_pairs={{0,10},{2,8},{4,14},{6,12},{8,2},{10,0},{12,6},{14,4},{1,11},{3,9}... | collective-permute-start | bytes 393224 | tf_op jit(solution)/shard_map/ppermute | solution.py:21
  48.8 19.1 %collective-permute-start.12 = (bf16[512,128]{1,0:T(8,128)(2,1)S(1)}, bf16[512,128]{1,0:T(8,128)(2,1)S(1)}, u32[]{:S(2)}, u32[]{:S(2)}) collective-permute-start(bf16[512,128]{1,0:T(8,128)(2,1)S(1)} %get-tuple-element.35), channel_id=1, source_target_pairs={{0,12},{2,14},{4,8},{6,10},{8,4},{10,6},{12,0},{14,2},{1,13},{3,15... | collective-permute-start | bytes 393224 | tf_op jit(solution)/shard_map/ppermute | solution.py:21
  50.2 19.6 %collective-permute-start.13 = (bf16[512,128]{1,0:T(8,128)(2,1)S(1)}, bf16[512,128]{1,0:T(8,128)(2,1)S(1)}, u32[]{:S(2)}, u32[]{:S(2)}) collective-permute-start(bf16[512,128]{1,0:T(8,128)(2,1)S(1)} %get-tuple-element.36), channel_id=1, source_target_pairs={{0,14},{2,12},{4,10},{6,8},{8,6},{10,4},{12,2},{14,0},{1,15},{3,13... | collective-permute-start | bytes 393224 | tf_op jit(solution)/shard_map/ppermute | solution.py:21
  51.7 8.5 %copy-start.2 = (f32[4096]{0:T(1024)S(1)}, f32[4096]{0:T(1024)}, u32[]{:S(2)}) copy-start(f32[4096]{0:T(1024)} %param.22) | copy-start | bytes 49156

commit v6 on v5

--- a/solution.py
+++ b/solution.py
@@ -240,13 +240,50 @@
     )
 
 
+def early_kernel(base, count, plan, *refs):
+    intra, carry, c_proj, values, squares = refs[-5:]
+    pieces = refs[:-5]
+    rows = pieces[0].shape[0]
+    turn = plan[TURNED + plan[ME]]
+    group = base ^ (turn // count)
+    c = c_proj[:, pl.ds(pl.multiple_of(group * STATE, STATE), STATE)]
+    total = jnp.zeros((c.shape[0], 1), jnp.float32)
+    for k, piece in enumerate(pieces):
+        column = pl.multiple_of(group * NORM_WIDTH + (k ^ (turn % count)) * rows, rows)
+        carried = lax.dot_general(
+            c, piece[...], (((1,), (1,)), ((), ())), preferred_element_type=jnp.float32
+        )
+        value = intra[:, pl.ds(column, rows)] + carry[:, pl.ds(column, rows)] * carried
+        total = total + jnp.sum(value * value, axis=1, keepdims=True)
+        values[:, k * rows : (k + 1) * rows] = value
+    squares[...] = jnp.broadcast_to(total, squares.shape)
+
+
+def early_stage(base, count, plan, pieces, intra, carry, c_proj):
+    tokens = intra.shape[0]
+    vmem = pl.BlockSpec(memory_space=pltpu.VMEM)
+    return pl.pallas_call(
+        functools.partial(early_kernel, base, count),
+        grid_spec=pltpu.PrefetchScalarGridSpec(
+            num_scalar_prefetch=1, grid=(), in_specs=[vmem] * (len(pieces) + 3), out_specs=[vmem] * 2
+        ),
+        out_shape=[
+            pltpu.VMEM((tokens, len(pieces) * pieces[0].shape[0]), jnp.float32),
+            pltpu.VMEM((tokens, LANES), jnp.float32),
+        ],
+        compiler_params=pltpu.CompilerParams(vmem_limit_bytes=16 << 20),
+        name="early_stage",
+    )(plan, *pieces, intra, carry, c_proj)
+
+
 def tail_kernel(base, piece_count, last, plan, *refs):
     pieces, refs = refs[:piece_count], refs[piece_count:]
     intra, carry, c_proj, gain = refs[:4]
     before, refs = (refs[4 : 4 + base], refs[4 + base :]) if last else ((), refs[4:])
     out, wide = refs[:2]
     tokens = wide.shape[0]
-    count, rows = len(pieces), pieces[0].shape[0]
+    rows = pieces[-1].shape[0]
+    count = NORM_WIDTH // rows
     turn = plan[TURNED + plan[ME]] if count > 1 else 0
     group = base ^ (turn // count)
     within = turn % count
@@ -261,10 +298,17 @@
     part = min(rows, 512)
     total = jnp.zeros((tokens, 1), jnp.float32)
     places = []
-    for k, piece in enumerate(pieces):
+    known = last and count > 1
+    if known:
+        total = total + pieces[1][:, :1]
+    for k in range(count):
         for at in range(0, rows, part):
             local_at = pl.multiple_of((k ^ within) * rows + at, part)
             column = pl.multiple_of(group * NORM_WIDTH + local_at, part)
+            if known and k < count - 1:
+                places.append(column)
+                continue
+            piece = pieces[2] if known else pieces[k]
             carried = lax.dot_general(
                 c, piece[at : at + part, :], (((1,), (1,)), ((), ())), preferred_element_type=jnp.float32
             )
@@ -276,7 +320,8 @@
     scale = lax.rsqrt(total * (1.0 / NORM_WIDTH) + EPSILON)
     for index, column in enumerate(places):
         lanes = slice(index * part, (index + 1) * part)
-        normed = wide[:, lanes] * scale * gain[:, pl.ds(column, part)]
+        gated = pieces[0] if known and index < len(places) - 1 else wide
+        normed = gated[:, lanes] * scale * gain[:, pl.ds(column, part)]
         value = jnp.where(keep, normed, 0.0).astype(jnp.bfloat16)
         if last:
             narrow[:, lanes] = value
@@ -292,7 +337,7 @@
 def tail_stage(base, last, plan, pieces, intra, carry, c_proj, gain, before):
     tokens, _ = intra.shape
     vmem = pl.BlockSpec(memory_space=pltpu.VMEM)
-    parts = NORM_WIDTH // min(pieces[0].shape[0], 512)
+    parts = NORM_WIDTH // min(pieces[-1].shape[0], 512)
     earlier = before if last else []
     scratch = [pltpu.VMEM((tokens, NORM_WIDTH), jnp.float32)]
     if last:
@@ -495,6 +540,8 @@
     done = []
     for base in range(norms):
         mine = got[base * share : (base + 1) * share]
+        if direct and base == norms - 1:
+            mine = [*early_stage(base, share, plan, mine[:-1], intra, carry, c_proj), mine[-1]]
         done.append(tail_stage(base, base == norms - 1, plan, mine, intra, carry, c_proj, gain, done))
     return done[-1]
 

time: 71.6 us -> 71.5 us (level)
  the two profiles are of different devices: /device:TPU:8 before, /device:TPU:0 now
where the time goes in v6:
time: 71.5 us; the launch traced here: 70.9 us
  starting transfers between devices  32.5 us (45%)
  waiting for transfers between devices  22.1 us (31%)
  Pallas kernels  13 us (18%)
  local copies, waits for them, and re-layouts  1.92 us (3%)
  between operations  1.46 us (2%)
    ppermute x21, starting transfers between devices, swap(): return lax.ppermute(value, axis, [(i, i ^ offset) for i in range(count)])  32.5 us
    ppermute x21, waiting for transfers between devices, swap(): return lax.ppermute(value, axis, [(i, i ^ offset) for i in range(count)])  22.1 us
    pallas_call x1, Pallas kernels, main_stage(): pl.pallas_call(functools.partial(main_kernel, len(rims)), grid_spec=grid_...  8.47 us
    pallas_call x2, Pallas kernels, tail_stage(): pl.pallas_call(functools.partial(tail_kernel, base, len(pieces), last), g...  1.81 us
  transfers between devices with their start and end apart: 21, of which 10 were waited for; matrix products, arithmetic and copies ran while one was open for 1% of the time, Pallas kernels for 16%

profile of v6, /device:TPU:0, one launch (start us, length us, event | category | flops | bytes accessed | tf_op | source)
XLA Modules:
  0.0 70.9 jit_solution(16881024502172932007)
XLA Ops:
  0.0 0.6 collective-permute-start.13
  0.6 0.1 collective-permute-start.14
  0.7 0.9 %slice.4 = bf16[1,8,64,128]{3,2,1,0:T(8,128)(2,1)S(1)} slice(bf16[1,64,64,128]{3,2,1,0:T(8,128)(2,1)} %param.23), slice={[0:1], [48:56], [0:64], [0:128]} | slice | bytes 262144 | tf_op jit(solution)/shard_map/slice | solution.py:505
  1.6 5.1 %collective-permute-start.5 = (bf16[512,128]{1,0:T(8,128)(2,1)S(1)}, bf16[512,128]{1,0:T(8,128)(2,1)S(1)}, u32[]{:S(2)}, u32[]{:S(2)}) collective-permute-start(bf16[512,128]{1,0:T(8,128)(2,1)S(1)} %bitcast.13), channel_id=1, source_target_pairs={{0,12},{2,14},{4,8},{6,10},{8,4},{10,6},{12,0},{14,2},{1,13},{3,15... | collective-permute-start | bytes 393224 | tf_op jit(solution)/shard_map/ppermute | solution.py:21
  6.7 0.1 collective-permute-start.8
  6.8 1.3 %cut_stage.1 = (bf16[512,128]{1,0:T(8,128)(2,1)S(1)}, bf16[512,128]{1,0:T(8,128)(2,1)S(1)}, bf16[512,128]{1,0:T(8,128)(2,1)S(1)}, bf16[512,128]{1,0:T(8,128)(2,1...) custom-call(bf16[8,512,128]{2,1,0:T(8,128)(2,1)} %bitcast.12, ...), custom_call_target="tpu_custom_call" | custom-call | tf_op jit(solution)/shard_map/cut_stage/pallas_call | solution.py:399
  8.1 0.1 collective-permute-start.7
  8.2 4.9 %collective-permute-done.8.refs_11_.refs_3_ = bf16[1,3,4608]{2,1,0:T(4,128)(2,1)S(1)} collective-permute-done((bf16[1,3,4608]{2,1,0:T(4,128)(2,1)}, bf16[1,3,4608]{2,1,0:T(4,128)(2,1)S(1)}, u32[]{:S(2)}, u32[]{:S(2)}) %collective-permute-start.8) | collective-permute-done | bytes 27680 | tf_op jit(solution)/shard_map/ppermute | solution.py:21
  13.0 1.5 %collective-permute-start.9 = (bf16[1,3,4608]{2,1,0:T(4,128)(2,1)S(1)}, bf16[1,3,4608]{2,1,0:T(4,128)(2,1)S(1)}, u32[]{:S(2)}, u32[]{:S(2)}) collective-permute-start(bf16[1,3,4608]{2,1,0:T(4,128)(2,1)S(1)} %collective-permute-done.8.refs_11_.refs_3_), channel_id=1, source_target_pairs={{0,4},{2,6},{4,0},{6,2},{8,12},{10,14},{12,8},{14,10},{1,5},{3,7},... | collective-permute-start | bytes 82952 | tf_op jit(solution)/shard_map/ppermute | solution.py:21
  14.5 0.0 collective-permute-done.7.refs_9_.refs_1_
  14.5 1.5 %collective-permute-start = (bf16[512,128]{1,0:T(8,128)(2,1)S(1)}, bf16[512,128]{1,0:T(8,128)(2,1)S(1)}, u32[]{:S(2)}, u32[]{:S(2)}) collective-permute-start(bf16[512,128]{1,0:T(8,128)(2,1)S(1)} %get-tuple-element.28), channel_id=1, source_target_pairs={{0,2},{2,0},{4,6},{6,4},{8,10},{10,8},{12,14},{14,12},{1,3},{3,1},... | collective-permute-start | bytes 393224 | tf_op jit(solution)/shard_map/ppermute | solution.py:21
  16.0 1.0 %collective-permute-done.9.refs_10_.refs_2_ = bf16[1,3,4608]{2,1,0:T(4,128)(2,1)S(1)} collective-permute-done((bf16[1,3,4608]{2,1,0:T(4,128)(2,1)S(1)}, bf16[1,3,4608]{2,1,0:T(4,128)(2,1)S(1)}, u32[]{:S(2)}, u32[]{:S(2)}) %collective-permute-start.9) | collective-permute-done | bytes 27680 | tf_op jit(solution)/shard_map/ppermute | solution.py:21
  17.0 1.5 %collective-permute-start.1 = (bf16[512,128]{1,0:T(8,128)(2,1)S(1)}, bf16[512,128]{1,0:T(8,128)(2,1)S(1)}, u32[]{:S(2)}, u32[]{:S(2)}) collective-permute-start(bf16[512,128]{1,0:T(8,128)(2,1)S(1)} %get-tuple-element.29), channel_id=1, source_target_pairs={{0,4},{2,6},{4,0},{6,2},{8,12},{10,14},{12,8},{14,10},{1,5},{3,7},... | collective-permute-start | bytes 393224 | tf_op jit(solution)/shard_map/ppermute | solution.py:21
  18.5 0.0 collective-permute-done.5.refs_6_
  18.5 1.5 %collective-permute-start.2 = (bf16[512,128]{1,0:T(8,128)(2,1)S(1)}, bf16[512,128]{1,0:T(8,128)(2,1)S(1)}, u32[]{:S(2)}, u32[]{:S(2)}) collective-permute-start(bf16[512,128]{1,0:T(8,128)(2,1)S(1)} %get-tuple-element.30), channel_id=1, source_target_pairs={{0,6},{2,4},{4,2},{6,0},{8,14},{10,12},{12,10},{14,8},{1,7},{3,5},... | collective-permute-start | bytes 393224 | tf_op jit(solution)/shard_map/ppermute | solution.py:21
  19.9 0.0 collective-permute-done.refs_1_
  20.0 2.5 %collective-permute-start.3 = (bf16[512,128]{1,0:T(8,128)(2,1)S(1)}, bf16[512,128]{1,0:T(8,128)(2,1)S(1)}, u32[]{:S(2)}, u32[]{:S(2)}) collective-permute-start(bf16[512,128]{1,0:T(8,128)(2,1)S(1)} %get-tuple-element.31), channel_id=1, source_target_pairs={{0,8},{2,10},{4,12},{6,14},{8,0},{10,2},{12,4},{14,6},{1,9},{3,11}... | collective-permute-start | bytes 393224 | tf_op jit(solution)/shard_map/ppermute | solution.py:21
  22.5 2.2 %collective-permute-done.1.refs_2_ = bf16[512,128]{1,0:T(8,128)(2,1)S(1)} collective-permute-done((bf16[512,128]{1,0:T(8,128)(2,1)S(1)}, bf16[512,128]{1,0:T(8,128)(2,1)S(1)}, u32[]{:S(2)}, u32[]{:S(2)}) %collective-permute-start.1) | collective-permute-done | bytes 131104 | tf_op jit(solution)/shard_map/ppermute | solution.py:21
  24.7 2.1 %collective-permute-start.4 = (bf16[512,128]{1,0:T(8,128)(2,1)S(1)}, bf16[512,128]{1,0:T(8,128)(2,1)S(1)}, u32[]{:S(2)}, u32[]{:S(2)}) collective-permute-start(bf16[512,128]{1,0:T(8,128)(2,1)S(1)} %get-tuple-element.32), channel_id=1, source_target_pairs={{0,10},{2,8},{4,14},{6,12},{8,2},{10,0},{12,6},{14,4},{1,11},{3,9}... | collective-permute-start | bytes 393224 | tf_op jit(solution)/shard_map/ppermute | solution.py:21
  26.8 0.5 collective-permute-done.2.refs_3_
  27.3 3.1 %collective-permute-start.6 = (bf16[512,128]{1,0:T(8,128)(2,1)S(1)}, bf16[512,128]{1,0:T(8,128)(2,1)S(1)}, u32[]{:S(2)}, u32[]{:S(2)}) collective-permute-start(bf16[512,128]{1,0:T(8,128)(2,1)S(1)} %get-tuple-element.33), channel_id=1, source_target_pairs={{0,14},{2,12},{4,10},{6,8},{8,6},{10,4},{12,2},{14,0},{1,15},{3,13... | collective-permute-start | bytes 393224 | tf_op jit(solution)/shard_map/ppermute | solution.py:21
  31.7 0.0 copy-start.7
  31.8 0.6 copy-done.7
  32.4 0.6 plan_stage.1.plan
  33.0 0.2 collective-permute-done.3.refs_4_
  33.2 4.5 %collective-permute-done.4.refs_5_ = bf16[512,128]{1,0:T(8,128)(2,1)S(1)} collective-permute-done((bf16[512,128]{1,0:T(8,128)(2,1)S(1)}, bf16[512,128]{1,0:T(8,128)(2,1)S(1)}, u32[]{:S(2)}, u32[]{:S(2)}) %collective-permute-start.4) | collective-permute-done | bytes 131104 | tf_op jit(solution)/shard_map/ppermute | solution.py:21
  37.7 0.5 pick_stage.1
  38.2 2.5 %collective-permute-start.10 = (bf16[512,128]{1,0:T(8,128)(2,1)S(1)}, bf16[512,128]{1,0:T(8,128)(2,1)S(1)}, u32[]{:S(2)}, u32[]{:S(2)}) collective-permute-start(bf16[512,128]{1,0:T(8,128)(2,1)S(1)} %get-tuple-element.35), channel_id=1, source_target_pairs={{0,8},{2,10},{4,12},{6,14},{8,0},{10,2},{12,4},{14,6},{1,9},{3,11}... | collective-permute-start | bytes 393224 | tf_op jit(solution)/shard_map/ppermute | solution.py:21
  40.7 0.6 collective-permute-start.11
  41.2 0.0 collective-permute-start.15
  41.2 1.2 %collective-permute-done.15.peer_dt = bf16[64,128]{1,0:T(8,128)(2,1)S(1)} collective-permute-done((bf16[64,128]{1,0:T(8,128)(2,1)S(1)}, bf16[64,128]{1,0:T(8,128)(2,1)S(1)}, u32[]{:S(2)}, u32[]{:S(2)}) %collective-permute-start.15) | collective-permute-done | bytes 16416 | tf_op jit(solution)/shard_map/ppermute | solution.py:21
  42.4 1.4 %collective-permute-start.16 = (bf16[1,3,4608]{2,1,0:T(4,128)(2,1)S(1)}, bf16[1,3,4608]{2,1,0:T(4,128)(2,1)S(1)}, u32[]{:S(2)}, u32[]{:S(2)}) collective-permute-start(bf16[1,3,4608]{2,1,0:T(4,128)(2,1)S(1)} %get-tuple-element.38), channel_id=1, source_target_pairs={{0,2},{2,0},{4,6},{6,4},{8,10},{10,8},{12,14},{14,12},{1,3},{3,1},... | collective-permute-start | bytes 82952 | tf_op jit(solution)/shard_map/ppermute | solution.py:21
  43.8 2.6 %collective-permute-done.16.refs_4_ = bf16[1,3,4608]{2,1,0:T(4,128)(2,1)S(1)} collective-permute-done((bf16[1,3,4608]{2,1,0:T(4,128)(2,1)S(1)}, bf16[1,3,4608]{2,1,0:T(4,128)(2,1)S(1)}, u32[]{:S(2)}, u32[]{:S(2)}) %collective-permute-start.16) | collective-permute-done | bytes 27680 | tf_op jit(solution)/shard_map/ppermute | solution.py:21
  46.4 2.3 %collective-permute-start.12 = (bf16[512,128]{1,0:T(8,128)(2,1)S(1)}, bf16[512,128]{1,0:T(8,128)(2,1)S(1)}, u32[]{:S(2)}, u32[]{:S(2)}) collective-permute-start(bf16[512,128]{1,0:T(8,128)(2,1)S(1)} %get-tuple-element.37), channel_id=1, source_target_pairs={{0,12},{2,14},{4,8},{6,10},{8,4},{10,6},{12,0},{14,2},{1,13},{3,15... | collective-permute-start | bytes 393224 | tf_op jit(solution)/shard_map/ppermute | solution.py:21
  48.6 0.9 %collective-permute-done.10.refs_0_ = bf16[512,128]{1,0:T(8,128)(2,1)S(1)} collective-permute-done((bf16[512,128]{1,0:T(8,128)(2,1)S(1)}, bf16[512,128]{1,0:T(8,128)(2,1)S(1)}, u32[]{:S(2)}, u32[]{:S(2)}) %collective-permute-start.10) | collective-permute-done | bytes 131104 | tf_op jit(solution)/shard_map/ppermute | solution.py:21
  49.6 0.6 collective-permute-start.18
  50.2 4.1 %collective-permute-done.11.refs_1_ = bf16[512,128]{1,0:T(8,128)(2,1)S(1)} collective-permute-done((bf16[512,128]{1,0:T(8,128)(2,1)S(1)}, bf16[512,128]{1,0:T(8,128)(2,1)S(1)}, u32[]{:S(2)}, u32[]{:S(2)}) %collective-permute-start.11) | collective-permute-done | bytes 131104 | tf_op jit(solution)/shard_map/ppermute | solution.py:21
  54.2 3.6 %collective-permute-start.20 = (bf16[512,128]{1,0:T(8,128)(2,1)S(1)}, bf16[512,128]{1,0:T(8,128)(2,1)S(1)}, u32[]{:S(2)}, u32[]{:S(2)}) collective-permute-start(bf16[512,128]{1,0:T(8,128)(2,1)S(1)} %get-tuple-element.48), channel_id=1, source_target_pairs={{0,6},{2,4},{4,2},{6,0},{8,14},{10,12},{12,10},{14,8},{1,7},{3,5},... | collective-permute-start | bytes 393224 | tf_op jit(solution)/shard_map/ppermute | solution.py:21
  57.9 0.0 collective-permute-done.13.peer_x.peer_bc
  57.9 2.0 %collective-permute-start.17 = (bf16[512,128]{1,0:T(8,128)(2,1)S(1)}, bf16[512,128]{1,0:T(8,128)(2,1)S(1)}, u32[]{:S(2)}, u32[]{:S(2)}) collective-permute-start(bf16[512,128]{1,0:T(8,128)(2,1)S(1)} %get-tuple-element.44), channel_id=1, source_target_pairs={{0,14},{2,12},{4,10},{6,8},{8,6},{10,4},{12,2},{14,0},{1,15},{3,13... | collective-permute-start | bytes 393224 | tf_op jit(solution)/shard_map/ppermute | solution.py:21
  59.9 8.5 %main_stage.1 = (f32[128,4096]{1,0:T(8,128)S(1)}, f32[128,4096]{1,0:T(8,128)S(1)}, bf16[128,256]{1,0:T(8,128)(2,1)S(1)}) custom-call(s32[12]{0:T(128)S(4)} %plan_stage.1.plan, f32[64]{0:T(128)S(1)} %copy-done.4, bf16[64,9216]{1,0:T(8,128)(2,1)} %own_bc.1, bf16[64,9216]{1,0:T(8,128)(2,1)S(1)} %collective-permute-done.13.peer_x.peer_bc, ...), custom_call_target="tpu_custom_call" | custom-call | flops 400000000 | bytes 8000000 | tf_op jit(solution)/shard_map/main_stage/pallas_call | solution.py:211
  68.4 0.0 copy-start.2
  68.4 0.3 early_stage.1
  68.8 0.0 collective-permute-done.18.refs_1_
  68.8 0.3 copy-done.2
  69.1 0.5 shard_map.136.refs_7_
  69.6 0.0 collective-permute-done.17.refs_2_
  69.7 1.3 %shard_map.137 = bf16[128,4096]{1,0:T(8,128)(2,1)} custom-call(s32[12]{0:T(128)S(4)} %plan_stage.1.plan, f32[128,1536]{1,0:T(8,128)S(1)} %get-tuple-element.42.refs_0_, f32[128,128]{1,0:T(8,128)S(1)} %get-tuple-element.43.refs_1_, bf16[512,128]{1,0:T(8,128)(2,1)S(1)} %collective-permute-done.17.refs_2_, f32[128,4096]{1,0:T(8,128)S(1)} %get-tuple-element.39.refs_3_.refs_4_, ...), custom_call_target="tpu_custom_call" | custom-call | flops 70000000 | bytes 3000000 | tf_op jit(solution)/shard_map/pallas_call | solution.py:355
  (18 shorter events, 0.0 us)
Async XLA Ops:
  0.0 41.2 %copy-start.3 = (bf16[64,128]{1,0:T(8,128)(2,1)S(1)}, bf16[64,128]{1,0:T(8,128)(2,1)}, u32[]{:S(2)}) copy-start(bf16[64,128]{1,0:T(8,128)(2,1)} %own_dt.1) | copy-start | bytes 49156
  0.0 59.9 %copy-start.4 = (f32[64]{0:T(128)S(1)}, f32[64]{0:T(128)}, u32[]{:S(2)}) copy-start(f32[64]{0:T(128)} %skip_ref.1) | copy-start | bytes 772
  0.0 59.9 %copy-start.6 = (f32[64]{0:T(128)S(1)}, f32[64]{0:T(128)}, u32[]{:S(2)}) copy-start(f32[64]{0:T(128)} %param.20) | copy-start | bytes 772
  0.0 59.9 %copy-start.5 = (f32[64]{0:T(128)S(1)}, f32[64]{0:T(128)}, u32[]{:S(2)}) copy-start(f32[64]{0:T(128)} %param.19) | copy-start | bytes 772
  0.0 59.9 %copy-start.1 = (f32[9216]{0:T(1024)S(1)}, f32[9216]{0:T(1024)}, u32[]{:S(2)}) copy-start(f32[9216]{0:T(1024)} %param.18) | copy-start | bytes 110596
  0.0 59.9 %copy-start = (f32[4,9216]{1,0:T(4,128)S(1)}, f32[4,9216]{1,0:T(4,128)}, u32[]{:S(2)}) copy-start(f32[4,9216]{1,0:T(4,128)} %weight_bc.1) | copy-start | bytes 442372
  0.0 57.9 %collective-permute-start.13 = (bf16[64,9216]{1,0:T(8,128)(2,1)}, bf16[64,9216]{1,0:T(8,128)(2,1)S(1)}, u32[]{:S(2)}, u32[]{:S(2)}) collective-permute-start(bf16[64,9216]{1,0:T(8,128)(2,1)} %own_bc.1), channel_id=1, source_target_pairs={{0,1},{1,0},{2,3},{3,2},{4,5},{5,4},{6,7},{7,6},{8,9},{9,8},{10,11... | collective-permute-start | bytes 3538952 | tf_op jit(solution)/shard_map/ppermute | solution.py:21
  0.6 53.6 %collective-permute-start.14 = (bf16[64,8192]{1,0:T(8,128)(2,1)}, bf16[64,8192]{1,0:T(8,128)(2,1)S(1)}, u32[]{:S(2)}, u32[]{:S(2)}) collective-permute-start(bf16[64,8192]{1,0:T(8,128)(2,1)} %own_gate.1), channel_id=1, source_target_pairs={{0,1},{1,0},{2,3},{3,2},{4,5},{5,4},{6,7},{7,6},{8,9},{9,8},{10,11... | collective-permute-start | bytes 3145736 | tf_op jit(solution)/shard_map/ppermute | solution.py:21
  1.6 16.9 %collective-permute-start.5 = (bf16[512,128]{1,0:T(8,128)(2,1)S(1)}, bf16[512,128]{1,0:T(8,128)(2,1)S(1)}, u32[]{:S(2)}, u32[]{:S(2)}) collective-permute-start(bf16[512,128]{1,0:T(8,128)(2,1)S(1)} %bitcast.13), channel_id=1, source_target_pairs={{0,12},{2,14},{4,8},{6,10},{8,4},{10,6},{12,0},{14,2},{1,13},{3,15... | collective-permute-start | bytes 393224 | tf_op jit(solution)/shard_map/ppermute | solution.py:21
  6.7 6.4 %collective-permute-start.8 = (bf16[1,3,4608]{2,1,0:T(4,128)(2,1)}, bf16[1,3,4608]{2,1,0:T(4,128)(2,1)S(1)}, u32[]{:S(2)}, u32[]{:S(2)}) collective-permute-start(bf16[1,3,4608]{2,1,0:T(4,128)(2,1)} %rims.1), channel_id=1, source_target_pairs={{0,12},{2,14},{4,8},{6,10},{8,4},{10,6},{12,0},{14,2},{1,13},{3,15... | collective-permute-start | bytes 82952 | tf_op jit(solution)/shard_map/ppermute | solution.py:21
  8.1 6.5 %collective-permute-start.7 = (bf16[1,3,4608]{2,1,0:T(4,128)(2,1)S(1)}, bf16[1,3,4608]{2,1,0:T(4,128)(2,1)S(1)}, u32[]{:S(2)}, u32[]{:S(2)}) collective-permute-start(bf16[1,3,4608]{2,1,0:T(4,128)(2,1)S(1)} %get-tuple-element.34.refs_8_.refs_0_), channel_id=1, source_target_pairs={{0,4},{2,6},{4,0},{6,2},{8,12},{10,14},{12,8},{14,10},{1,5},{3,7},... | collective-permute-start | bytes 82952 | tf_op jit(solution)/shard_map/ppermute | solution.py:21
  13.0 4.0 %collective-permute-start.9 = (bf16[1,3,4608]{2,1,0:T(4,128)(2,1)S(1)}, bf16[1,3,4608]{2,1,0:T(4,128)(2,1)S(1)}, u32[]{:S(2)}, u32[]{:S(2)}) collective-permute-start(bf16[1,3,4608]{2,1,0:T(4,128)(2,1)S(1)} %collective-permute-done.8.refs_11_.refs_3_), channel_id=1, source_target_pairs={{0,4},{2,6},{4,0},{6,2},{8,12},{10,14},{12,8},{14,10},{1,5},{3,7},... | collective-permute-start | bytes 82952 | tf_op jit(solution)/shard_map/ppermute | solution.py:21
  14.5 5.4 %collective-permute-start = (bf16[512,128]{1,0:T(8,128)(2,1)S(1)}, bf16[512,128]{1,0:T(8,128)(2,1)S(1)}, u32[]{:S(2)}, u32[]{:S(2)}) collective-permute-start(bf16[512,128]{1,0:T(8,128)(2,1)S(1)} %get-tuple-element.28), channel_id=1, source_target_pairs={{0,2},{2,0},{4,6},{6,4},{8,10},{10,8},{12,14},{14,12},{1,3},{3,1},... | collective-permute-start | bytes 393224 | tf_op jit(solution)/shard_map/ppermute | solution.py:21
  17.0 7.7 %collective-permute-start.1 = (bf16[512,128]{1,0:T(8,128)(2,1)S(1)}, bf16[512,128]{1,0:T(8,128)(2,1)S(1)}, u32[]{:S(2)}, u32[]{:S(2)}) collective-permute-start(bf16[512,128]{1,0:T(8,128)(2,1)S(1)} %get-tuple-element.29), channel_id=1, source_target_pairs={{0,4},{2,6},{4,0},{6,2},{8,12},{10,14},{12,8},{14,10},{1,5},{3,7},... | collective-permute-start | bytes 393224 | tf_op jit(solution)/shard_map/ppermute | solution.py:21
  18.5 8.8 %collective-permute-start.2 = (bf16[512,128]{1,0:T(8,128)(2,1)S(1)}, bf16[512,128]{1,0:T(8,128)(2,1)S(1)}, u32[]{:S(2)}, u32[]{:S(2)}) collective-permute-start(bf16[512,128]{1,0:T(8,128)(2,1)S(1)} %get-tuple-element.30), channel_id=1, source_target_pairs={{0,6},{2,4},{4,2},{6,0},{8,14},{10,12},{12,10},{14,8},{1,7},{3,5},... | collective-permute-start | bytes 393224 | tf_op jit(solution)/shard_map/ppermute | solution.py:21
  20.0 13.2 %collective-permute-start.3 = (bf16[512,128]{1,0:T(8,128)(2,1)S(1)}, bf16[512,128]{1,0:T(8,128)(2,1)S(1)}, u32[]{:S(2)}, u32[]{:S(2)}) collective-permute-start(bf16[512,128]{1,0:T(8,128)(2,1)S(1)} %get-tuple-element.31), channel_id=1, source_target_pairs={{0,8},{2,10},{4,12},{6,14},{8,0},{10,2},{12,4},{14,6},{1,9},{3,11}... | collective-permute-start | bytes 393224 | tf_op jit(solution)/shard_map/ppermute | solution.py:21
  24.7 13.0 %collective-permute-start.4 = (bf16[512,128]{1,0:T(8,128)(2,1)S(1)}, bf16[512,128]{1,0:T(8,128)(2,1)S(1)}, u32[]{:S(2)}, u32[]{:S(2)}) collective-permute-start(bf16[512,128]{1,0:T(8,128)(2,1)S(1)} %get-tuple-element.32), channel_id=1, source_target_pairs={{0,10},{2,8},{4,14},{6,12},{8,2},{10,0},{12,6},{14,4},{1,11},{3,9}... | collective-permute-start | bytes 393224 | tf_op jit(solution)/shard_map/ppermute | solution.py:21
  27.3 10.4 %collective-permute-start.6 = (bf16[512,128]{1,0:T(8,128)(2,1)S(1)}, bf16[512,128]{1,0:T(8,128)(2,1)S(1)}, u32[]{:S(2)}, u32[]{:S(2)}) collective-permute-start(bf16[512,128]{1,0:T(8,128)(2,1)S(1)} %get-tuple-element.33), channel_id=1, source_target_pairs={{0,14},{2,12},{4,10},{6,8},{8,6},{10,4},{12,2},{14,0},{1,15},{3,13... | collective-permute-start | bytes 393224 | tf_op jit(solution)/shard_map/ppermute | solution.py:21
  31.7 0.7 copy-start.7
  38.2 11.4 %collective-permute-start.10 = (bf16[512,128]{1,0:T(8,128)(2,1)S(1)}, bf16[512,128]{1,0:T(8,128)(2,1)S(1)}, u32[]{:S(2)}, u32[]{:S(2)}) collective-permute-start(bf16[512,128]{1,0:T(8,128)(2,1)S(1)} %get-tuple-element.35), channel_id=1, source_target_pairs={{0,8},{2,10},{4,12},{6,14},{8,0},{10,2},{12,4},{14,6},{1,9},{3,11}... | collective-permute-start | bytes 393224 | tf_op jit(solution)/shard_map/ppermute | solution.py:21
  40.7 13.6 %collective-permute-start.11 = (bf16[512,128]{1,0:T(8,128)(2,1)S(1)}, bf16[512,128]{1,0:T(8,128)(2,1)S(1)}, u32[]{:S(2)}, u32[]{:S(2)}) collective-permute-start(bf16[512,128]{1,0:T(8,128)(2,1)S(1)} %get-tuple-element.36), channel_id=1, source_target_pairs={{0,10},{2,8},{4,14},{6,12},{8,2},{10,0},{12,6},{14,4},{1,11},{3,9}... | collective-permute-start | bytes 393224 | tf_op jit(solution)/shard_map/ppermute | solution.py:21
  41.2 1.2 %collective-permute-start.15 = (bf16[64,128]{1,0:T(8,128)(2,1)S(1)}, bf16[64,128]{1,0:T(8,128)(2,1)S(1)}, u32[]{:S(2)}, u32[]{:S(2)}) collective-permute-start(bf16[64,128]{1,0:T(8,128)(2,1)S(1)} %copy-done.3), channel_id=1, source_target_pairs={{0,1},{1,0},{2,3},{3,2},{4,5},{5,4},{6,7},{7,6},{8,9},{9,8},{10,11... | collective-permute-start | bytes 49160 | tf_op jit(solution)/shard_map/ppermute | solution.py:21
  42.4 4.0 %collective-permute-start.16 = (bf16[1,3,4608]{2,1,0:T(4,128)(2,1)S(1)}, bf16[1,3,4608]{2,1,0:T(4,128)(2,1)S(1)}, u32[]{:S(2)}, u32[]{:S(2)}) collective-permute-start(bf16[1,3,4608]{2,1,0:T(4,128)(2,1)S(1)} %get-tuple-element.38), channel_id=1, source_target_pairs={{0,2},{2,0},{4,6},{6,4},{8,10},{10,8},{12,14},{14,12},{1,3},{3,1},... | collective-permute-start | bytes 82952 | tf_op jit(solution)/shard_map/ppermute | solution.py:21
  46.4 22.0 %collective-permute-start.12 = (bf16[512,128]{1,0:T(8,128)(2,1)S(1)}, bf16[512,128]{1,0:T(8,128)(2,1)S(1)}, u32[]{:S(2)}, u32[]{:S(2)}) collective-permute-start(bf16[512,128]{1,0:T(8,128)(2,1)S(1)} %get-tuple-element.37), channel_id=1, source_target_pairs={{0,12},{2,14},{4,8},{6,10},{8,4},{10,6},{12,0},{14,2},{1,13},{3,15... | collective-permute-start | bytes 393224 | tf_op jit(solution)/shard_map/ppermute | solution.py:21
  49.6 19.2 %collective-permute-start.18 = (bf16[512,128]{1,0:T(8,128)(2,1)S(1)}, bf16[512,128]{1,0:T(8,128)(2,1)S(1)}, u32[]{:S(2)}, u32[]{:S(2)}) collective-permute-start(bf16[512,128]{1,0:T(8,128)(2,1)S(1)} %get-tuple-element.46), channel_id=1, source_target_pairs={{0,2},{2,0},{4,6},{6,4},{8,10},{10,8},{12,14},{14,12},{1,3},{3,1},... | collective-permute-start | bytes 393224 | tf_op jit(solution)/shard_map/ppermute | solution.py:21
  54.2 14.5 %collective-permute-start.19 = (bf16[512,128]{1,0:T(8,128)(2,1)S(1)}, bf16[512,128]{1,0:T(8,128)(2,1)S(1)}, u32[]{:S(2)}, u32[]{:S(2)}) collective-permute-start(bf16[512,128]{1,0:T(8,128)(2,1)S(1)} %get-tuple-element.47), channel_id=1, source_target_pairs={{0,4},{2,6},{4,0},{6,2},{8,12},{10,14},{12,8},{14,10},{1,5},{3,7},... | collective-permute-start | bytes 393224 | tf_op jit(solution)/shard_map/ppermute | solution.py:21
  54.2 14.5 %collective-permute-start.20 = (bf16[512,128]{1,0:T(8,128)(2,1)S(1)}, bf16[512,128]{1,0:T(8,128)(2,1)S(1)}, u32[]{:S(2)}, u32[]{:S(2)}) collective-permute-start(bf16[512,128]{1,0:T(8,128)(2,1)S(1)} %get-tuple-element.48), channel_id=1, source_target_pairs={{0,6},{2,4},{4,2},{6,0},{8,14},{10,12},{12,10},{14,8},{1,7},{3,5},... | collective-permute-start | bytes 393224 | tf_op jit(solution)/shard_map/ppermute | solution.py:21
  57.9 11.7 %collective-permute-start.17 = (bf16[512,128]{1,0:T(8,128)(2,1)S(1)}, bf16[512,128]{1,0:T(8,128)(2,1)S(1)}, u32[]{:S(2)}, u32[]{:S(2)}) collective-permute-start(bf16[512,128]{1,0:T(8,128)(2,1)S(1)} %get-tuple-element.44), channel_id=1, source_target_pairs={{0,14},{2,12},{4,10},{6,8},{8,6},{10,4},{12,2},{14,0},{1,15},{3,13... | collective-permute-start | bytes 393224 | tf_op jit(solution)/shard_map/ppermute | solution.py:21
  68.4 0.7 %copy-start.2 = (f32[4096]{0:T(1024)S(1)}, f32[4096]{0:T(1024)}, u32[]{:S(2)}) copy-start(f32[4096]{0:T(1024)} %param.22) | copy-start | bytes 49156
